TPU v7x, 32 devices: a whole 2x2x4 slice. The times are simulated.
32 devices in a mesh: dp: 8 (over y, x, core), tensor: 4 (over z).
Axes of the slice: x: 2, y: 2, z: 4, core: 2. Of those that a mesh axis runs over, the one named last changes fastest.
Arguments:
- tokens: bfloat16 [8192, 2048], P(('dp', 'tensor')), may hold values from -6 to 6
- positions: int32 [8192], P('dp'), may hold values from 0 to 1023, as said below
- norm_gain: float32 [2, 2, 2048], replicated, may hold values from 0.25 to 1.75
- norm_bias: float32 [2, 2, 2048], replicated, may hold values from -3 to 3
- w_qkv: bfloat16 [2, 2048, 3, 2048], P(None, 'dp', None, 'tensor'), may hold values from -0.125 to 0.125
- b_qkv: float32 [2, 3, 2048], replicated, may hold values from -3 to 3
- w_out: bfloat16 [2, 2048, 2048], P(None, 'tensor', 'dp'), may hold values from -0.5 to 0.5
- w_gate_up: bfloat16 [2, 2048, 2, 5632], P(None, 'dp', None, 'tensor'), may hold values from -0.125 to 0.125
- w_down: bfloat16 [2, 5632, 2048], P(None, 'tensor', 'dp'), may hold values from -0.078125 to 0.078125
- cotangent: bfloat16 [8192, 2048], P(('dp', 'tensor')), may hold values from -6 to 6
Outputs:
- activations: bfloat16 [8192, 2048], P(('dp', 'tensor'))
- input_grad: float32 [8192, 2048], P(('dp', 'tensor'))
- gain_grad: float32 [2, 2, 2048], replicated
- norm_bias_grad: float32 [2, 2, 2048], replicated
- qkv_grad: float32 [2, 2048, 3, 2048], P(None, 'dp', None, 'tensor')
- qkv_bias_grad: float32 [2, 3, 2048], replicated
- out_grad: float32 [2, 2048, 2048], P(None, 'tensor', 'dp')
- gate_up_grad: float32 [2, 2048, 2, 5632], P(None, 'dp', None, 'tensor')
- down_grad: float32 [2, 5632, 2048], P(None, 'tensor', 'dp')
Inputs may be any that keep to these rules, and one draw needn't show every extreme that they name: positions[i] counts the tokens before i in its document; documents lie end to end in the sequences of 1024 tokens, so the first token of a sequence has 0 and every other token has 0 or one more than the token before it.
All inputs are finite; a program needn't handle non-finite values.
Results may differ from a plain program's by a relative error of at most 0.023.
Values may be sent and summed in bfloat16 or wider, within the bound.
A program may use at most 320 MiB of HBM per device.

v0:
```python
import math

import jax
import jax.numpy as jnp
from jax import lax
from jax.sharding import PartitionSpec as P

HD = 64
ROT = 16
LAYERS = 2


norm_eps = 1e-05
theta_log = math.log(10000.0)
masked_score = -1e30
contract_rows = (((0,), (0,)), ((), ()))
contract_cols = (((1,), (1,)), ((), ()))


def norm_parts(hidden):
    average = jnp.mean(hidden, axis=-1, keepdims=True)
    centred = hidden - average
    variance = jnp.mean(centred * centred, axis=-1, keepdims=True)
    inverse = lax.rsqrt(variance + norm_eps)
    return (centred * inverse, inverse)


def norm_back(grad_normed, scaled, inverse, norm_weight):
    weighted = grad_normed * norm_weight
    first_mean = jnp.mean(weighted, axis=-1, keepdims=True)
    second_mean = jnp.mean(weighted * scaled, axis=-1, keepdims=True)
    grad_input = inverse * (weighted - first_mean - scaled * second_mean)
    return (grad_input, jnp.sum(grad_normed * scaled, axis=0), jnp.sum(grad_normed, axis=0))


def rotary_tables(positions):
    half_rot = ROT // 2
    frequency = jnp.exp(-(jnp.arange(half_rot, dtype=jnp.float32) * 2.0 / ROT) * theta_log)
    angles = positions.astype(jnp.float32)[:, None] * frequency[None, :]
    return (jnp.cos(angles)[:, None, :], jnp.sin(angles)[:, None, :])


def rotate(values, cos_table, sin_table):
    half_rot = ROT // 2
    first_half = values[..., :half_rot]
    second_half = values[..., half_rot:ROT]
    return jnp.concatenate(
        [
            first_half * cos_table - second_half * sin_table,
            second_half * cos_table + first_half * sin_table,
            values[..., ROT:],
        ],
        axis=-1,
    )


def inner_rows(left, right):
    return lax.dot_general(left, right, contract_rows, preferred_element_type=jnp.float32)


def inner_cols(left, right):
    return lax.dot_general(left, right, contract_cols, preferred_element_type=jnp.float32)


def block_scores(queries, key_rows, positions, number, block_rows, score_scale):
    seq_len = key_rows.shape[0]
    row_start = number * block_rows
    query_block = lax.dynamic_slice_in_dim(queries, row_start, block_rows, 0)
    scores = (
        jnp.einsum("qhd,khd->hqk", query_block, key_rows, preferred_element_type=jnp.float32)
        * score_scale
    )
    row_index = row_start + jnp.arange(block_rows, dtype=jnp.int32)
    first_key = row_index - lax.dynamic_slice_in_dim(positions, row_start, block_rows, 0)
    columns = jnp.arange(seq_len, dtype=jnp.int32)
    allowed = (columns[None, :] <= row_index[:, None]) & (columns[None, :] >= first_key[:, None])
    return (query_block, allowed, jnp.where(allowed[None], scores, masked_score))


def attend_forward(queries, key_rows, values, positions, score_scale):
    seq_len = queries.shape[0]
    block_rows = min(512, seq_len)

    def one_block(number):
        query_block, allowed, scores = block_scores(
            queries, key_rows, positions, number, block_rows, score_scale
        )
        row_max = jnp.max(scores, axis=-1, keepdims=True)
        shifted = jnp.exp(scores - row_max)
        row_sum = jnp.sum(shifted, axis=-1, keepdims=True)
        weights_low = (shifted / row_sum).astype(jnp.bfloat16)
        block_out = jnp.einsum(
            "hqk,khd->qhd", weights_low, values, preferred_element_type=jnp.float32
        )
        return (block_out, row_max + jnp.log(row_sum))

    block_outs, logsums = lax.map(one_block, jnp.arange(seq_len // block_rows, dtype=jnp.int32))
    return (block_outs.reshape(seq_len, -1), logsums)


def attend_back(queries, key_rows, values, positions, logsums, grad_attended, score_scale):
    seq_len = queries.shape[0]
    block_rows = min(512, seq_len)

    def one_block(totals, inputs):
        grad_keys, grad_values = totals
        number, logsum = inputs
        query_block, allowed, scores = block_scores(
            queries, key_rows, positions, number, block_rows, score_scale
        )
        softmax_rows = jnp.exp(scores - logsum)
        grad_block = lax.dynamic_slice_in_dim(grad_attended, number * block_rows, block_rows, 0)
        grad_probs = jnp.einsum(
            "qhd,khd->hqk", grad_block, values, preferred_element_type=jnp.float32
        )
        grad_values = grad_values + jnp.einsum(
            "hqk,qhd->khd",
            softmax_rows.astype(jnp.bfloat16),
            grad_block,
            preferred_element_type=jnp.float32,
        )
        row_inner = jnp.sum(softmax_rows * grad_probs, axis=-1, keepdims=True)
        grad_scores = jnp.where(allowed[None], softmax_rows * (grad_probs - row_inner), 0.0).astype(
            jnp.bfloat16
        )
        grad_query = (
            jnp.einsum("hqk,khd->qhd", grad_scores, key_rows, preferred_element_type=jnp.float32)
            * score_scale
        )
        grad_keys = (
            grad_keys
            + jnp.einsum(
                "hqk,qhd->khd", grad_scores, query_block, preferred_element_type=jnp.float32
            )
            * score_scale
        )
        return ((grad_keys, grad_values), grad_query)

    empty_grad = jnp.zeros(key_rows.shape, jnp.float32)
    numbers = jnp.arange(seq_len // block_rows, dtype=jnp.int32)
    (grad_keys, grad_values), grad_queries = lax.scan(
        one_block, (empty_grad, empty_grad), (numbers, logsums)
    )
    return (grad_queries.reshape(queries.shape), grad_keys, grad_values)


def per_device(
    tokens, positions, norm_gain, norm_bias, w_qkv, b_qkv, w_out, w_gate_up, w_down, cotangent
):
    tensor_rank = lax.axis_index("tensor")
    width_local = w_qkv.shape[3]
    heads_local = width_local // HD
    ff_local = w_gate_up.shape[3]
    local_rows = tokens.shape[0]
    seq_len = positions.shape[0]
    score_scale = 1.0 / math.sqrt(HD)
    cos_table, sin_table = rotary_tables(positions)
    hidden = tokens.astype(jnp.float32)
    kept_state = []
    for layer_index in range(LAYERS):
        gathered = (
            lax.all_gather(w_qkv[layer_index], "dp", axis=0, tiled=True),
            lax.all_gather(w_out[layer_index], "dp", axis=1, tiled=True),
            lax.all_gather(w_gate_up[layer_index], "dp", axis=0, tiled=True),
            lax.all_gather(w_down[layer_index], "dp", axis=1, tiled=True),
        )
        full_qkv, full_out, full_gu, full_down = gathered
        scaled_a, inverse_a = norm_parts(hidden)
        normed_a = (scaled_a * norm_gain[layer_index, 0] + norm_bias[layer_index, 0]).astype(
            jnp.bfloat16
        )
        rows_a = lax.all_gather(normed_a, "tensor", axis=0, tiled=True)
        bias_local = lax.dynamic_slice_in_dim(
            b_qkv[layer_index], tensor_rank * width_local, width_local, 1
        )
        mixed = jnp.dot(
            rows_a,
            full_qkv.reshape(full_qkv.shape[0], 3 * width_local),
            preferred_element_type=jnp.float32,
        ) + bias_local.reshape(3 * width_local)
        mixed = mixed.reshape(seq_len, 3, heads_local, HD)
        queries = rotate(mixed[:, 0], cos_table, sin_table).astype(jnp.bfloat16)
        key_rows = rotate(mixed[:, 1], cos_table, sin_table).astype(jnp.bfloat16)
        values = mixed[:, 2].astype(jnp.bfloat16)
        attended, logsums = attend_forward(queries, key_rows, values, positions, score_scale)
        attended = attended.astype(jnp.bfloat16)

        def project_attn(row_start, row_count, source=attended, weight=full_out):
            return jnp.dot(source, weight, preferred_element_type=jnp.float32)

        branch_a = lax.psum_scatter(
            project_attn(jnp.int32(0), local_rows * lax.axis_size("tensor")).astype(jnp.bfloat16),
            "tensor",
            scatter_dimension=0,
            tiled=True,
        ).astype(jnp.float32)
        hidden_mid = hidden + branch_a
        scaled_b, inverse_b = norm_parts(hidden_mid)
        normed_b = (scaled_b * norm_gain[layer_index, 1] + norm_bias[layer_index, 1]).astype(
            jnp.bfloat16
        )
        rows_b = lax.all_gather(normed_b, "tensor", axis=0, tiled=True)
        gate_up = jnp.dot(
            rows_b,
            full_gu.reshape(full_gu.shape[0], 2 * ff_local),
            preferred_element_type=jnp.float32,
        ).reshape(seq_len, 2, ff_local)
        activated = (jax.nn.silu(gate_up[:, 0]) * gate_up[:, 1]).astype(jnp.bfloat16)

        def project_mlp(row_start, row_count, source=activated, weight=full_down):
            return jnp.dot(source, weight, preferred_element_type=jnp.float32)

        hidden = hidden_mid + lax.psum_scatter(
            project_mlp(jnp.int32(0), local_rows * lax.axis_size("tensor")).astype(jnp.bfloat16),
            "tensor",
            scatter_dimension=0,
            tiled=True,
        ).astype(jnp.float32)
        kept_state.append(
            (
                gathered,
                scaled_a,
                inverse_a,
                rows_a,
                queries,
                key_rows,
                values,
                logsums,
                attended,
                scaled_b,
                inverse_b,
                rows_b,
                gate_up,
                activated,
            )
        )
    activations = hidden.astype(jnp.bfloat16)
    grad = cotangent.astype(jnp.float32)
    weight_parts = [None] * LAYERS
    gain_rows = [None] * LAYERS
    shift_rows = [None] * LAYERS
    qkv_shift_rows = [None] * LAYERS
    for layer_index in reversed(range(LAYERS)):
        (
            gathered,
            scaled_a,
            inverse_a,
            rows_a,
            queries,
            key_rows,
            values,
            logsums,
            attended,
            scaled_b,
            inverse_b,
            rows_b,
            gate_up,
            activated,
        ) = kept_state[layer_index]
        full_qkv, full_out, full_gu, full_down = (
            lax.all_gather(w_qkv[layer_index], "dp", axis=0, tiled=True),
            lax.all_gather(w_out[layer_index], "dp", axis=1, tiled=True),
            lax.all_gather(w_gate_up[layer_index], "dp", axis=0, tiled=True),
            lax.all_gather(w_down[layer_index], "dp", axis=1, tiled=True),
        )
        grad_rows_b = lax.all_gather(grad.astype(jnp.bfloat16), "tensor", axis=0, tiled=True)
        grad_down_weight = inner_rows(activated, grad_rows_b)
        grad_act = inner_cols(grad_rows_b, full_down)
        gate_part = gate_up[:, 0]
        up_part = gate_up[:, 1]
        sigmoid_gate = jax.nn.sigmoid(gate_part)
        grad_gate = grad_act * up_part * sigmoid_gate * (1.0 + gate_part * (1.0 - sigmoid_gate))
        grad_up = grad_act * jax.nn.silu(gate_part)
        grad_gate_up = (
            jnp.stack([grad_gate, grad_up], axis=1)
            .astype(jnp.bfloat16)
            .reshape(seq_len, 2 * ff_local)
        )
        grad_gu_weight = inner_rows(rows_b, grad_gate_up).reshape(full_gu.shape)
        flat_gu = full_gu.reshape(full_gu.shape[0], 2 * ff_local)

        def back_mlp(row_start, row_count, source=grad_gate_up, weight=flat_gu):
            return inner_cols(source, weight)

        grad_normed_b = lax.psum_scatter(
            back_mlp(jnp.int32(0), local_rows * lax.axis_size("tensor")).astype(jnp.bfloat16),
            "tensor",
            scatter_dimension=0,
            tiled=True,
        ).astype(jnp.float32)
        grad_in_b, gain_b, shift_b = norm_back(
            grad_normed_b, scaled_b, inverse_b, norm_gain[layer_index, 1]
        )
        grad = grad + grad_in_b
        grad_rows_a = lax.all_gather(grad.astype(jnp.bfloat16), "tensor", axis=0, tiled=True)
        grad_out_weight = inner_rows(attended, grad_rows_a)
        grad_attended = inner_cols(grad_rows_a, full_out).astype(jnp.bfloat16)
        grad_attended = grad_attended.reshape(seq_len, heads_local, HD)
        grad_queries, grad_keys, grad_values = attend_back(
            queries, key_rows, values, positions, logsums, grad_attended, score_scale
        )
        grad_queries = rotate(grad_queries, cos_table, -sin_table)
        grad_keys = rotate(grad_keys, cos_table, -sin_table)
        grad_mixed = jnp.stack([grad_queries, grad_keys, grad_values], axis=1)
        grad_mixed = grad_mixed.reshape(seq_len, 3 * width_local).astype(jnp.bfloat16)
        qkv_shift_local = jnp.sum(grad_mixed, axis=0, dtype=jnp.float32).reshape(3, width_local)
        qkv_shift_rows[layer_index] = lax.dynamic_update_slice(
            jnp.zeros((3, b_qkv.shape[2]), jnp.float32),
            qkv_shift_local,
            (jnp.int32(0), tensor_rank * width_local),
        )
        grad_qkv_weight = inner_rows(rows_a, grad_mixed).reshape(full_qkv.shape)
        flat_qkv = full_qkv.reshape(full_qkv.shape[0], 3 * width_local)

        def back_attn(row_start, row_count, source=grad_mixed, weight=flat_qkv):
            return inner_cols(source, weight)

        grad_normed_a = lax.psum_scatter(
            back_attn(jnp.int32(0), local_rows * lax.axis_size("tensor")).astype(jnp.bfloat16),
            "tensor",
            scatter_dimension=0,
            tiled=True,
        ).astype(jnp.float32)
        grad_in_a, gain_a, shift_a = norm_back(
            grad_normed_a, scaled_a, inverse_a, norm_gain[layer_index, 0]
        )
        grad = grad + grad_in_a
        gain_rows[layer_index] = jnp.stack([gain_a, gain_b])
        shift_rows[layer_index] = jnp.stack([shift_a, shift_b])
        weight_parts[layer_index] = (
            lax.psum_scatter(
                grad_qkv_weight.astype(jnp.bfloat16), "dp", scatter_dimension=0, tiled=True
            ).astype(jnp.float32),
            lax.psum_scatter(
                grad_out_weight.astype(jnp.bfloat16), "dp", scatter_dimension=1, tiled=True
            ).astype(jnp.float32),
            lax.psum_scatter(
                grad_gu_weight.astype(jnp.bfloat16), "dp", scatter_dimension=0, tiled=True
            ).astype(jnp.float32),
            lax.psum_scatter(
                grad_down_weight.astype(jnp.bfloat16), "dp", scatter_dimension=1, tiled=True
            ).astype(jnp.float32),
        )
    stack_qkv = jnp.stack([weight_parts[number][0] for number in range(LAYERS)])
    stack_out = jnp.stack([weight_parts[number][1] for number in range(LAYERS)])
    stack_gu = jnp.stack([weight_parts[number][2] for number in range(LAYERS)])
    stack_down = jnp.stack([weight_parts[number][3] for number in range(LAYERS)])
    gain_grad, norm_bias_grad, qkv_bias_grad = lax.psum(
        (jnp.stack(gain_rows), jnp.stack(shift_rows), jnp.stack(qkv_shift_rows)), ("dp", "tensor")
    )
    return (
        activations,
        grad,
        gain_grad,
        norm_bias_grad,
        stack_qkv,
        qkv_bias_grad,
        stack_out,
        stack_gu,
        stack_down,
    )


def solution(mesh):
    in_specs = (
        P(("dp", "tensor"), None),
        P("dp"),
        P(),
        P(),
        P(None, "dp", None, "tensor"),
        P(),
        P(None, "tensor", "dp"),
        P(None, "dp", None, "tensor"),
        P(None, "tensor", "dp"),
        P(("dp", "tensor"), None),
    )
    out_specs = (
        P(("dp", "tensor"), None),
        P(("dp", "tensor"), None),
        P(),
        P(),
        P(None, "dp", None, "tensor"),
        P(),
        P(None, "tensor", "dp"),
        P(None, "dp", None, "tensor"),
        P(None, "tensor", "dp"),
    )
    return jax.shard_map(
        per_device, mesh=mesh, in_specs=in_specs, out_specs=out_specs, check_vma=False
    )
```

profile of v0, /device:TPU:0, one launch (start us, length us, event | category | flops | bytes accessed | tf_op | source)
XLA Modules:
  0.0 2721.8 jit_solution(6625782385930977792)
XLA Ops:
  20.9 78.7 %all-gather.25.cloned.1.call-done = bf16[1024,2048]{1,0:T(8,128)(2,1)} async-done(((bf16[256,2048]{1,0:T(8,128)(2,1)}), bf16[1024,2048]{1,0:T(8,128)(2,1)}) %all-gather.25.cloned.1.call-update) | async-done | bytes 4194320 | tf_op jit(solution)/shard_map/all_gather | solution.py:172
  99.6 47.7 %all-gather.41.cloned.1.call-done = bf16[1,2048,3,512]{1,3,2,0:T(8,128)(2,1)} async-done(((bf16[1,256,3,512]{1,3,2,0:T(8,128)(2,1)}), bf16[1,2048,3,512]{1,3,2,0:T(8,128)(2,1)}) %all-gather.41.cloned.1.call-update) | async-done | bytes 6291472 | tf_op jit(solution)/shard_map/all_gather | solution.py:162
  172.1 31.3 %while.54 = (s32[]{:T(128)}, bf16[2,512,8,64]{1,3,2,0:T(8,128)(2,1)}, f32[2,8,512,1]{2,1,3,0:T(8,128)S(1)}, s32[2]{0:T(128)S(1)}, s32[1024]{0:T(1024)S(1)}, /*in...) while((s32[]{:T(128)}, ...), condition=%wide.region_5.6_spmd, body=%wide.region_2.5_spmd.sunk | while | flops 1125643264 | bytes 64628996 | solution.py:97
  220.1 70.9 %reduce-scatter.17.cloned.1.call-done = bf16[256,2048]{1,0:T(8,128)(2,1)} async-done(((bf16[1024,2048]{1,0:T(8,128)(2,1)}), bf16[256,2048]{1,0:T(8,128)(2,1)}) %reduce-scatter.17.cloned.1.call-update) | async-done | bytes 1048592 | tf_op jit(solution)/shard_map/reduce_scatter | solution.py:191
  298.7 63.0 %all-gather.45.cloned.1.call-done = bf16[1,2048,2,1408]{3,1,2,0:T(8,128)(2,1)} async-done(((bf16[1,256,2,1408]{3,1,2,0:T(8,128)(2,1)}), bf16[1,2048,2,1408]{3,1,2,0:T(8,128)(2,1)}) %all-gather.45.cloned.1.call-update) | async-done | bytes 11534352 | tf_op jit(solution)/shard_map/all_gather | solution.py:164
  377.5 67.2 %all-gather.27.cloned.1.call-done = bf16[1024,2048]{1,0:T(8,128)(2,1)} async-done(((bf16[256,2048]{1,0:T(8,128)(2,1)}), bf16[1024,2048]{1,0:T(8,128)(2,1)}) %all-gather.27.cloned.1.call-update) | async-done | bytes 4194320 | tf_op jit(solution)/shard_map/all_gather | solution.py:202
  444.6 17.3 fusion.96
  468.8 21.3 all-gather.47.cloned.1.call-done
  503.5 74.5 %reduce-scatter.19.cloned.1.call-done = bf16[256,2048]{1,0:T(8,128)(2,1)} async-done(((bf16[1024,2048]{1,0:T(8,128)(2,1)}), bf16[256,2048]{1,0:T(8,128)(2,1)}) %reduce-scatter.19.cloned.1.call-update) | async-done | bytes 1048592 | tf_op jit(solution)/shard_map/reduce_scatter | solution.py:213
  584.0 43.1 %all-gather.49.cloned.1.call-done = bf16[1,2048,3,512]{1,3,2,0:T(8,128)(2,1)} async-done(((bf16[1,256,3,512]{1,3,2,0:T(8,128)(2,1)}), bf16[1,2048,3,512]{1,3,2,0:T(8,128)(2,1)}) %all-gather.49.cloned.1.call-update) | async-done | bytes 6291472 | tf_op jit(solution)/shard_map/all_gather | solution.py:162
  627.0 82.8 %all-gather.29.cloned.1.call-done = bf16[1024,2048]{1,0:T(8,128)(2,1)} async-done(((bf16[256,2048]{1,0:T(8,128)(2,1)}), bf16[1024,2048]{1,0:T(8,128)(2,1)}) %all-gather.29.cloned.1.call-update) | async-done | bytes 4194320 | tf_op jit(solution)/shard_map/all_gather | solution.py:172
  735.4 33.6 %while.55 = (s32[]{:T(128)}, bf16[2,512,8,64]{1,3,2,0:T(8,128)(2,1)S(1)}, f32[2,8,512,1]{2,1,3,0:T(8,128)S(1)}, s32[2]{0:T(128)S(1)}, s32[1024]{0:T(1024)S(1)}, ...) while((s32[]{:T(128)}, ...), condition=%wide.region_15.16_spmd, body=%wide.region_12.15_spmd.sunk | while | flops 1125643264 | bytes 56240328 | solution.py:97
  779.5 72.7 %reduce-scatter.21.cloned.1.call-done = bf16[256,2048]{1,0:T(8,128)(2,1)} async-done(((bf16[1024,2048]{1,0:T(8,128)(2,1)}), bf16[256,2048]{1,0:T(8,128)(2,1)}) %reduce-scatter.21.cloned.1.call-update) | async-done | bytes 1048592 | tf_op jit(solution)/shard_map/reduce_scatter | solution.py:191
  857.8 64.8 %all-gather.53.cloned.1.call-done = bf16[1,2048,2,1408]{3,1,2,0:T(8,128)(2,1)} async-done(((bf16[1,256,2,1408]{3,1,2,0:T(8,128)(2,1)}), bf16[1,2048,2,1408]{3,1,2,0:T(8,128)(2,1)}) %all-gather.53.cloned.1.call-update) | async-done | bytes 11534352 | tf_op jit(solution)/shard_map/all_gather | solution.py:164
  938.1 67.3 %all-gather.31.cloned.1.call-done = bf16[1024,2048]{1,0:T(8,128)(2,1)} async-done(((bf16[256,2048]{1,0:T(8,128)(2,1)}), bf16[1024,2048]{1,0:T(8,128)(2,1)}) %all-gather.31.cloned.1.call-update) | async-done | bytes 4194320 | tf_op jit(solution)/shard_map/all_gather | solution.py:202
  1005.4 18.8 fusion.94
  1024.3 62.0 %all-gather.33.cloned.1.call-done = bf16[1024,2048]{1,0:T(8,128)(2,1)} async-done(((bf16[256,2048]{1,0:T(8,128)(2,1)}), bf16[1024,2048]{1,0:T(8,128)(2,1)}) %all-gather.33.cloned.1.call-update) | async-done | bytes 4194320 | tf_op jit(solution)/shard_map/all_gather | solution.py:266
  1086.3 44.8 %all-gather.55.cloned.1.call-done = bf16[1,1408,2048]{2,1,0:T(8,128)(2,1)} async-done(((bf16[1,1408,256]{2,1,0:T(8,128)(2,1)}), bf16[1,1408,2048]{2,1,0:T(8,128)(2,1)}) %all-gather.55.cloned.1.call-update) | async-done | bytes 5767184 | tf_op jit(solution)/shard_map/all_gather | solution.py:165
  1147.6 16.3 bitcast_convert_fusion.1
  1182.2 58.7 %reduce-scatter.25.cloned.1.call-done = bf16[256,2048]{1,0:T(8,128)(2,1)} async-done(((bf16[1024,2048]{1,0:T(8,128)(2,1)}), bf16[256,2048]{1,0:T(8,128)(2,1)}) %reduce-scatter.25.cloned.1.call-update) | async-done | bytes 1048592 | tf_op jit(solution)/shard_map/reduce_scatter | solution.py:285
  1243.7 76.7 %reduce-scatter.23.cloned.1.call-done = bf16[256,2048]{1,0:T(8,128)(2,1)} async-done(((bf16[1024,2048]{1,0:T(8,128)(2,1)}), bf16[256,2048]{1,0:T(8,128)(2,1)}) %reduce-scatter.23.cloned.1.call-update) | async-done | bytes 1048592 | tf_op jit(solution)/shard_map/reduce_scatter | solution.py:213
  1325.1 81.3 %all-gather.35.cloned.1.call-done = bf16[1024,2048]{1,0:T(8,128)(2,1)} async-done(((bf16[256,2048]{1,0:T(8,128)(2,1)}), bf16[1024,2048]{1,0:T(8,128)(2,1)}) %all-gather.35.cloned.1.call-update) | async-done | bytes 4194320 | tf_op jit(solution)/shard_map/all_gather | solution.py:295
  1414.7 183.7 %while.56 = (s32[]{:T(128)}, f32[1024,8,64]{0,2,1:T(8,128)}, f32[1024,8,64]{0,2,1:T(8,128)S(1)}, f32[2,512,8,64]{1,0,3,2:T(2,128)}, s32[2]{0:T(128)S(1)}, /*inde...) while((s32[]{:T(128)}, f32[1024,8,64]{0,2,1:T(8,128)}, ...), condition=%wide.region_25.26_spmd.clone, body=%wide.region_23.25_spmd.clone.sunk | while | flops 2747542528 | bytes 239134992 | solution.py:141
  1438.1 22.9 fusion.302
  1461.0 23.3 bitcast_add_fusion.8
  1486.7 19.6 dynamic_update_slice.48
  1529.4 22.9 fusion.302
  1552.4 23.9 bitcast_add_fusion.8
  1578.6 19.6 dynamic_update_slice.48
  1618.9 75.4 %reduce-scatter.27.cloned.1.call-done = bf16[256,2048]{1,0:T(8,128)(2,1)} async-done(((bf16[1024,2048]{1,0:T(8,128)(2,1)}), bf16[256,2048]{1,0:T(8,128)(2,1)}) %reduce-scatter.27.cloned.1.call-update) | async-done | bytes 1048592 | tf_op jit(solution)/shard_map/reduce_scatter | solution.py:318
  1699.9 81.4 %all-gather.37.cloned.1.call-done = bf16[1024,2048]{1,0:T(8,128)(2,1)} async-done(((bf16[256,2048]{1,0:T(8,128)(2,1)}), bf16[1024,2048]{1,0:T(8,128)(2,1)}) %all-gather.37.cloned.1.call-update) | async-done | bytes 4194320 | tf_op jit(solution)/shard_map/all_gather | solution.py:266
  1814.6 75.4 %reduce-scatter.29.cloned.1.call-done = bf16[256,2048]{1,0:T(8,128)(2,1)} async-done(((bf16[1024,2048]{1,0:T(8,128)(2,1)}), bf16[256,2048]{1,0:T(8,128)(2,1)}) %reduce-scatter.29.cloned.1.call-update) | async-done | bytes 1048592 | tf_op jit(solution)/shard_map/reduce_scatter | solution.py:285
  1934.4 19.2 convolution_convert_fusion
  1969.0 19.3 convolution_convert_fusion.1
  2011.4 197.9 %while.57 = (s32[]{:T(128)}, f32[1024,8,64]{0,2,1:T(8,128)}, f32[1024,8,64]{0,2,1:T(8,128)}, f32[2,512,8,64]{1,0,3,2:T(2,128)}, s32[2]{0:T(128)S(1)}, /*index=5*...) while((s32[]{:T(128)}, f32[1024,8,64]{0,2,1:T(8,128)}, ...), condition=%wide.region_34.35_spmd.clone, body=%wide.region_32.34_spmd.clone.sunk | while | flops 2747542528 | bytes 239134992 | solution.py:141
  2035.0 27.3 %fusion.315 = f32[1,512,8,64]{1,3,2,0:T(8,128)} fusion(bf16[1024,8,64]{0,2,1:T(8,128)(2,1)S(1)} %get-tuple-element.900, f32[8,512,1024]{2,1,0:T(8,128)} %copy-done.1, f32[8,512,1024]{2,1,0:T(8,128)} %fusion.314, pred[512,1024]{1,0:T(8,128)(4,1)S(1)} %fusion.313), kind=kOutput, calls=%fused_computation.87.clone.1 | convolution fusion | flops 558109696 | bytes 36175872 | tf_op jit(solution)/shard_map/while/body/eval_jaxpr/hqk,khd->qhd/dot_general | solution.py:127
  2062.3 24.7 bitcast_add_fusion.10
  2089.3 19.5 dynamic_update_slice.49
  2135.3 26.6 fusion.315
  2161.9 25.3 bitcast_add_fusion.10
  2189.6 19.7 dynamic_update_slice.49
  2259.7 22.6 reduce-scatter.41.cloned.1.call-done
  2291.5 35.7 %reduce-scatter.39.cloned.1.call-done = bf16[512,256]{1,0:T(8,128)(2,1)} async-done(((bf16[512,2048]{1,0:T(8,128)(2,1)}), bf16[512,256]{1,0:T(8,128)(2,1)}) %reduce-scatter.39.cloned.1.call-update) | async-done | bytes 262160 | tf_op jit(solution)/shard_map/reduce_scatter | solution.py:334
  2327.2 44.5 %reduce-scatter.37.cloned.1.call-done = bf16[512,256]{1,0:T(8,128)(2,1)} async-done(((bf16[512,2048]{1,0:T(8,128)(2,1)}), bf16[512,256]{1,0:T(8,128)(2,1)}) %reduce-scatter.37.cloned.1.call-update) | async-done | bytes 262160 | tf_op jit(solution)/shard_map/reduce_scatter | solution.py:334
  2373.8 77.0 %reduce-scatter.31.cloned.1.call-done = bf16[256,2048]{1,0:T(8,128)(2,1)} async-done(((bf16[1024,2048]{1,0:T(8,128)(2,1)}), bf16[256,2048]{1,0:T(8,128)(2,1)}) %reduce-scatter.31.cloned.1.call-update) | async-done | bytes 1048592 | tf_op jit(solution)/shard_map/reduce_scatter | solution.py:318
  2457.8 58.6 %reduce-scatter.35.cloned.1.call-done = bf16[256,3,512]{2,0,1:T(8,128)(2,1)} async-done(((bf16[2048,3,512]{2,0,1:T(8,128)(2,1)}), bf16[256,3,512]{2,0,1:T(8,128)(2,1)}) %reduce-scatter.35.cloned.1.call-update) | async-done | bytes 786448 | tf_op jit(solution)/shard_map/reduce_scatter | solution.py:331
  2516.4 65.6 %reduce-scatter.33.cloned.1.call-done = bf16[256,3,512]{2,0,1:T(8,128)(2,1)} async-done(((bf16[2048,3,512]{2,0,1:T(8,128)(2,1)}), bf16[256,3,512]{2,0,1:T(8,128)(2,1)}) %reduce-scatter.33.cloned.1.call-update) | async-done | bytes 786448 | tf_op jit(solution)/shard_map/reduce_scatter | solution.py:331
  2585.2 125.2 %all-reduce.3.cloned.1.call-done = (f32[2,2,2048]{2,1,0:T(2,128)}, f32[2,2,2048]{2,1,0:T(2,128)}, f32[2,3,2048]{2,0,1:T(2,128)}) async-done(((f32[2,2,2048]{2,1,0:T(2,128)}, f32[2,2,2048]{2,1,0:T(2,128)}, f32[2,3,2048]{2,0,1:T(2,128)}), (f32[2,2,2048]{2,1,0:T(2,128)}, f32[2,2,2048]{2,1,0:T(2,128)}, f32[2,3,2048]{2,0,1:T(2,128)})) %all-reduce.3.cloned.1.call-update) | async-done | bytes 114704 | tf_op jit(solution)/shard_map/psum | solution.py:348
  (483 shorter events, 594.2 us)
Async XLA Ops:
  7.2 92.5 %all-gather.25.cloned.1.call-start = ((), (), s32[]{:S(2)}) async-start(), calls=%async_computation.16 | async-start | bytes 5242880 | tf_op jit(solution)/shard_map/all_gather | solution.py:172
  16.0 131.3 %all-gather.41.cloned.1.call-start = ((), (), s32[]{:S(2)}) async-start(), calls=%async_computation.40 | async-start | bytes 7077888 | tf_op jit(solution)/shard_map/all_gather | solution.py:162
  18.4 189.3 %all-gather.43.cloned.1.call-start = ((), (), s32[]{:S(2)}) async-start(), calls=%async_computation.41 | async-start | bytes 2359296 | tf_op jit(solution)/shard_map/all_gather | solution.py:163
  19.3 271.7 %reduce-scatter.17.cloned.1.call-start = ((), (), s32[]{:S(2)}) async-start(), calls=%async_computation.17 | async-start | bytes 5242880 | tf_op jit(solution)/shard_map/reduce_scatter | solution.py:191
  20.9 149.7 %copy-start.47 = (f32[1024,8]{0,1:T(8,128)}, f32[1024,8]{0,1:T(8,128)S(1)}, u32[]{:S(2)}) copy-start(f32[1024,8]{0,1:T(8,128)S(1)} %get-tuple-element.487) | copy-start | bytes 98308
  20.9 149.7 %copy-start.61 = (f32[1024,8]{0,1:T(8,128)}, f32[1024,8]{0,1:T(8,128)S(1)}, u32[]{:S(2)}) copy-start(f32[1024,8]{0,1:T(8,128)S(1)} %get-tuple-element.486) | copy-start | bytes 98308
  214.1 147.6 %all-gather.45.cloned.1.call-start = ((), (), s32[]{:S(2)}) async-start(), calls=%async_computation.42 | async-start | bytes 12976128 | tf_op jit(solution)/shard_map/all_gather | solution.py:164
  220.1 224.6 %all-gather.27.cloned.1.call-start = ((), (), s32[]{:S(2)}) async-start(), calls=%async_computation.18 | async-start | bytes 5242880 | tf_op jit(solution)/shard_map/all_gather | solution.py:202
  297.4 192.7 %all-gather.47.cloned.1.call-start = ((), (), s32[]{:S(2)}) async-start(), calls=%async_computation.43 | async-start | bytes 6488064 | tf_op jit(solution)/shard_map/all_gather | solution.py:165
  298.7 279.3 %reduce-scatter.19.cloned.1.call-start = ((), (), s32[]{:S(2)}) async-start(), calls=%async_computation.19 | async-start | bytes 5242880 | tf_op jit(solution)/shard_map/reduce_scatter | solution.py:213
  501.0 126.0 %all-gather.49.cloned.1.call-start = ((), (), s32[]{:S(2)}) async-start(), calls=%async_computation.44 | async-start | bytes 7077888 | tf_op jit(solution)/shard_map/all_gather | solution.py:162
  503.4 77.6 %copy-start.67 = (f32[1,1,2048]{2,1,0:T(1,128)S(1)}, f32[1,1,2048]{2,1,0:T(1,128)}, u32[]{:S(2)}) copy-start(f32[1,1,2048]{2,1,0:T(1,128)} %get-tuple-element.480) | copy-start | bytes 24580
  503.4 77.6 %copy-start.79 = (f32[1,1,2048]{2,1,0:T(1,128)S(1)}, f32[1,1,2048]{2,1,0:T(1,128)}, u32[]{:S(2)}) copy-start(f32[1,1,2048]{2,1,0:T(1,128)} %get-tuple-element.484) | copy-start | bytes 24580
  503.4 206.4 %all-gather.29.cloned.1.call-start = ((), (), s32[]{:S(2)}) async-start(), calls=%async_computation.20 | async-start | bytes 5242880 | tf_op jit(solution)/shard_map/all_gather | solution.py:172
  580.0 141.8 %copy-start.88 = (f32[256]{0:T(256)}, f32[256]{0:T(256)S(1)}, u32[]{:S(2)}) copy-start(f32[256]{0:T(256)S(1)} %add_rsqrt_fusion.1) | copy-start | bytes 3076
  582.4 188.0 %all-gather.51.cloned.1.call-start = ((), (), s32[]{:S(2)}) async-start(), calls=%async_computation.45 | async-start | bytes 2359296 | tf_op jit(solution)/shard_map/all_gather | solution.py:163
  583.2 269.1 %reduce-scatter.21.cloned.1.call-start = ((), (), s32[]{:S(2)}) async-start(), calls=%async_computation.21 | async-start | bytes 5242880 | tf_op jit(solution)/shard_map/reduce_scatter | solution.py:191
  776.9 145.7 %all-gather.53.cloned.1.call-start = ((), (), s32[]{:S(2)}) async-start(), calls=%async_computation.46 | async-start | bytes 12976128 | tf_op jit(solution)/shard_map/all_gather | solution.py:164
  779.5 75.6 %copy-start.69 = (f32[1,1,2048]{2,1,0:T(1,128)S(1)}, f32[1,1,2048]{2,1,0:T(1,128)}, u32[]{:S(2)}) copy-start(f32[1,1,2048]{2,1,0:T(1,128)} %get-tuple-element.477) | copy-start | bytes 24580
  779.5 225.9 %all-gather.31.cloned.1.call-start = ((), (), s32[]{:S(2)}) async-start(), calls=%async_computation.22 | async-start | bytes 5242880 | tf_op jit(solution)/shard_map/all_gather | solution.py:202
  856.6 229.7 %all-gather.33.cloned.1.call-start = ((), (), s32[]{:S(2)}) async-start(), calls=%async_computation.24 | async-start | bytes 5242880 | tf_op jit(solution)/shard_map/all_gather | solution.py:266
  857.1 273.9 %all-gather.55.cloned.1.call-start = ((), (), s32[]{:S(2)}) async-start(), calls=%async_computation.47 | async-start | bytes 6488064 | tf_op jit(solution)/shard_map/all_gather | solution.py:165
  857.7 383.2 %reduce-scatter.25.cloned.1.call-start = ((), (), s32[]{:S(2)}) async-start(), calls=%async_computation.25 | async-start | bytes 5242880 | tf_op jit(solution)/shard_map/reduce_scatter | solution.py:285
  1164.0 156.4 %reduce-scatter.23.cloned.1.call-start = ((), (), s32[]{:S(2)}) async-start(), calls=%async_computation.23 | async-start | bytes 5242880 | tf_op jit(solution)/shard_map/reduce_scatter | solution.py:213
  1182.1 138.3 %copy-start.23 = (bf16[256,2048]{1,0:T(8,128)(2,1)S(1)}, bf16[256,2048]{1,0:T(8,128)(2,1)}, u32[]{:S(2)}) copy-start(bf16[256,2048]{1,0:T(8,128)(2,1)} %param.27) | copy-start | bytes 3145732
  1182.1 224.4 %all-gather.35.cloned.1.call-start = ((), (), s32[]{:S(2)}) async-start(), calls=%async_computation.26 | async-start | bytes 5242880 | tf_op jit(solution)/shard_map/all_gather | solution.py:295
  1325.1 369.3 %reduce-scatter.27.cloned.1.call-start = ((), (), s32[]{:S(2)}) async-start(), calls=%async_computation.27 | async-start | bytes 5242880 | tf_op jit(solution)/shard_map/reduce_scatter | solution.py:318
  1325.1 89.6 %copy-start.58 = (f32[2,8,512,1]{2,1,3,0:T(8,128)S(1)}, f32[2,8,512,1]{2,1,3,0:T(8,128)}, u32[]{:S(2)}) copy-start(f32[2,8,512,1]{2,1,3,0:T(8,128)} %copy-done.57) | copy-start | bytes 98308
  1618.9 162.4 %all-gather.37.cloned.1.call-start = ((), (), s32[]{:S(2)}) async-start(), calls=%async_computation.28 | async-start | bytes 5242880 | tf_op jit(solution)/shard_map/all_gather | solution.py:266
  1699.9 190.2 %reduce-scatter.29.cloned.1.call-start = ((), (), s32[]{:S(2)}) async-start(), calls=%async_computation.29 | async-start | bytes 5242880 | tf_op jit(solution)/shard_map/reduce_scatter | solution.py:285
  1814.6 181.7 %all-gather.39.cloned.1.call-start = ((), (), s32[]{:S(2)}) async-start(), calls=%async_computation.30 | async-start | bytes 5242880 | tf_op jit(solution)/shard_map/all_gather | solution.py:295
  1896.0 359.9 %reduce-scatter.47.cloned.1.call-start = ((), (), s32[]{:S(2)}) async-start(), calls=%async_computation.39 | async-start | bytes 6488064 | tf_op jit(solution)/shard_map/reduce_scatter | solution.py:340
  1906.7 349.2 %reduce-scatter.45.cloned.1.call-start = ((), (), s32[]{:S(2)}) async-start(), calls=%async_computation.38 | async-start | bytes 6488064 | tf_op jit(solution)/shard_map/reduce_scatter | solution.py:340
  1919.2 340.5 %reduce-scatter.43.cloned.1.call-start = ((), (), s32[]{:S(2)}) async-start(), calls=%async_computation.37 | async-start | bytes 12976128 | tf_op jit(solution)/shard_map/reduce_scatter | solution.py:337
  1953.6 328.7 %reduce-scatter.41.cloned.1.call-start = ((), (), s32[]{:S(2)}) async-start(), calls=%async_computation.36 | async-start | bytes 12976128 | tf_op jit(solution)/shard_map/reduce_scatter | solution.py:337
  1988.4 338.8 %reduce-scatter.39.cloned.1.call-start = ((), (), s32[]{:S(2)}) async-start(), calls=%async_computation.35 | async-start | bytes 2359296 | tf_op jit(solution)/shard_map/reduce_scatter | solution.py:334
  1996.2 375.5 %reduce-scatter.37.cloned.1.call-start = ((), (), s32[]{:S(2)}) async-start(), calls=%async_computation.34 | async-start | bytes 2359296 | tf_op jit(solution)/shard_map/reduce_scatter | solution.py:334
  2002.2 448.6 %reduce-scatter.31.cloned.1.call-start = ((), (), s32[]{:S(2)}) async-start(), calls=%async_computation.31 | async-start | bytes 5242880 | tf_op jit(solution)/shard_map/reduce_scatter | solution.py:318
  2228.5 287.9 %reduce-scatter.35.cloned.1.call-start = ((), (), s32[]{:S(2)}) async-start(), calls=%async_computation.33 | async-start | bytes 7077888 | tf_op jit(solution)/shard_map/reduce_scatter | solution.py:331
  2241.7 340.3 %reduce-scatter.33.cloned.1.call-start = ((), (), s32[]{:S(2)}) async-start(), calls=%async_computation.32 | async-start | bytes 7077888 | tf_op jit(solution)/shard_map/reduce_scatter | solution.py:331
  2254.9 455.5 %all-reduce.3.cloned.1.call-start = ((), (), s32[]{:S(2)}) async-start(), calls=%async_computation.48 | async-start | bytes 229376 | tf_op jit(solution)/shard_map/psum | solution.py:348
  2284.5 166.3 %copy-start.4 = (bf16[256,2048]{1,0:T(8,128)(2,1)S(1)}, bf16[256,2048]{1,0:T(8,128)(2,1)}, u32[]{:S(2)}) copy-start(bf16[256,2048]{1,0:T(8,128)(2,1)} %param.18) | copy-start | bytes 3145732
  2284.5 166.3 %copy-start.64 = (f32[1,1,2048]{2,1,0:T(1,128)S(1)}, f32[1,1,2048]{2,1,0:T(1,128)}, u32[]{:S(2)}) copy-start(f32[1,1,2048]{2,1,0:T(1,128)} %copy-done.63) | copy-start | bytes 24580
  2284.5 166.3 %copy-start.85 = (f32[256]{0:T(256)S(1)}, f32[256]{0:T(256)}, u32[]{:S(2)}) copy-start(f32[256]{0:T(256)} %copy-done.84) | copy-start | bytes 3076
  2284.5 166.2 %copy-start.91 = (f32[256]{0:T(256)S(1)}, f32[256]{0:T(256)}, u32[]{:S(2)}) copy-start(f32[256]{0:T(256)} %copy-done.90) | copy-start | bytes 3076
  2291.5 161.6 %copy-start.75 = (f32[2048]{0:T(1024)S(1)}, f32[2048]{0:T(1024)}, u32[]{:S(2)}) copy-start(f32[2048]{0:T(1024)} %get-tuple-element.313) | copy-start | bytes 24580
  2291.5 161.6 %copy-start.74 = (f32[2048]{0:T(1024)S(1)}, f32[2048]{0:T(1024)}, u32[]{:S(2)}) copy-start(f32[2048]{0:T(1024)} %get-tuple-element.326) | copy-start | bytes 24580
  2291.5 162.9 %copy-start.21 = (f32[256,2048]{1,0:T(8,128)S(1)}, f32[256,2048]{1,0:T(8,128)}, u32[]{:S(2)}) copy-start(f32[256,2048]{1,0:T(8,128)} %get-tuple-element.413) | copy-start | bytes 6291460
  (85 other events, 1326.4 us)
Sparse Core Ops, SparseCore 0:
  16.1 83.4 all-gather.24
  102.1 45.1 all-gather.40
  149.8 28.1 all-gather.42
  214.2 76.7 reduce-scatter.16
  293.5 68.1 all-gather.44
  363.8 80.7 all-gather.26
  447.2 42.8 all-gather.46
  501.1 76.7 reduce-scatter.18
  579.8 47.1 all-gather.48
  629.0 80.7 all-gather.28
  711.7 26.7 all-gather.50
  777.0 75.2 reduce-scatter.20
  854.3 68.2 all-gather.52
  924.6 80.7 all-gather.30
  1006.9 79.2 all-gather.32
  1088.2 42.8 all-gather.54
  1164.1 76.7 reduce-scatter.24
  1243.0 77.2 reduce-scatter.22
  1325.2 81.2 all-gather.34
  1619.0 75.2 reduce-scatter.26
  1700.0 81.2 all-gather.36
  1814.7 75.2 reduce-scatter.28
  1896.1 81.2 all-gather.38
  1981.1 57.5 reduce-scatter.46
  2042.1 59.0 reduce-scatter.44
  2104.9 86.8 reduce-scatter.42
  2195.5 86.7 reduce-scatter.40
  2285.9 41.1 reduce-scatter.38
  2330.5 41.2 reduce-scatter.36
  2374.0 76.7 reduce-scatter.30
  2454.1 62.2 reduce-scatter.34
  2520.2 61.7 reduce-scatter.32
  2588.4 121.9 all-reduce.2
where the time goes:
time: 2740 us; the launch traced here: 2720 us
  waiting for transfers between devices  1740 us (64%)
  matrix products  596 us (22%)
  local copies, waits for them, and re-layouts  255 us (9%)
  other arithmetic  105 us (4%)
    all_gather x4, waiting for transfers between devices, per_device(): lax.all_gather(grad.astype(jnp.bfloat16), 'tensor', axis=0, tiled=True)  225 us
    all_gather x2, waiting for transfers between devices, per_device(): rows_a = lax.all_gather(normed_a, 'tensor', axis=0, tiled=True)  161 us
    reduce_scatter x2, waiting for transfers between devices, per_device(): lax.psum_scatter(back_attn(jnp.int32(0), local_rows * lax.axis_size('tens...  152 us
    reduce_scatter x2, waiting for transfers between devices, per_device(): lax.psum_scatter(project_mlp(jnp.int32(0), local_rows * lax.axis_size('te...  151 us
    reduce_scatter x2, waiting for transfers between devices, per_device(): lax.psum_scatter(project_attn(jnp.int32(0), local_rows * lax.axis_size('t...  144 us
    all_gather x2, waiting for transfers between devices, per_device(): rows_b = lax.all_gather(normed_b, 'tensor', axis=0, tiled=True)  134 us
    reduce_scatter x2, waiting for transfers between devices, per_device(): lax.psum_scatter(back_mlp(jnp.int32(0), local_rows * lax.axis_size('tenso...  134 us
    all_gather x2, waiting for transfers between devices, per_device(): lax.all_gather(w_gate_up[layer_index], 'dp', axis=0, tiled=True)  128 us
  transfers between devices with their start and end apart: 33, of which 27 were waited for; matrix products, arithmetic and copies ran while one was open for 22% of the time, Pallas kernels for 0%

commit v1 on v0

--- a/solution.py
+++ b/solution.py
@@ -1,20 +1,1012 @@
+import functools
 import math
 
 import jax
 import jax.numpy as jnp
 from jax import lax
+from jax.experimental import pallas as pl
+from jax.experimental.pallas import tpu as pltpu
 from jax.sharding import PartitionSpec as P
 
 HD = 64
 ROT = 16
 LAYERS = 2
-
+PAIR = 2 * HD
+MESH = pl.DeviceIdType.MESH
+F32 = jnp.float32
+BF16 = jnp.bfloat16
+VMEM_LIMIT = 62 * 2**20
 
 norm_eps = 1e-05
 theta_log = math.log(10000.0)
 masked_score = -1e30
-contract_rows = (((0,), (0,)), ((), ()))
-contract_cols = (((1,), (1,)), ((), ()))
+rows_rows = (((0,), (0,)), ((), ()))
+cols_cols = (((1,), (1,)), ((), ()))
+rows_cols = (((1,), (0,)), ((), ()))
+
+
+def matmul(left, right, dims=rows_cols):
+    return lax.dot_general(left, right, dims, preferred_element_type=F32)
+
+
+def line_order(step, place, count):
+    short = jnp.minimum(place, count - 1 - place)
+    away = (step + 1) // 2
+    nearest = jnp.where(step % 2 == 1, place - away, place + away)
+    others = jnp.where(place < count - 1 - place, step, count - 1 - step)
+    return jnp.where(step <= 2 * short, nearest, others)
+
+
+def line_barrier(place, count):
+    barrier = pltpu.get_barrier_semaphore()
+
+    @pl.when(place > 0)
+    def _():
+        pl.semaphore_signal(barrier, inc=1, device_id={"tensor": place - 1}, device_id_type=MESH)
+
+    @pl.when(place < count - 1)
+    def _():
+        pl.semaphore_signal(barrier, inc=1, device_id={"tensor": place + 1}, device_id_type=MESH)
+
+    middle = (place > 0) & (place < count - 1)
+
+    @pl.when(middle)
+    def _():
+        pl.semaphore_wait(barrier, 2)
+
+    @pl.when(jnp.logical_not(middle))
+    def _():
+        pl.semaphore_wait(barrier, 1)
+
+
+def gather_rows(place, count, held, send_sem, recv_sem, process):
+    def hop(block, right):
+        return pltpu.make_async_remote_copy(
+            src_ref=held.at[block],
+            dst_ref=held.at[block],
+            send_sem=send_sem.at[0 if right else 1, block],
+            recv_sem=recv_sem.at[block],
+            device_id={"tensor": place + 1 if right else place - 1},
+            device_id_type=MESH,
+        )
+
+    def one(step, carry):
+        block = line_order(step, place, count)
+
+        @pl.when(step > 0)
+        def _():
+            hop(block, True).wait_recv()
+
+        @pl.when((block <= place) & (place < count - 1))
+        def _():
+            hop(block, True).start()
+
+        @pl.when((block >= place) & (place > 0))
+        def _():
+            hop(block, False).start()
+
+        process(block)
+        return carry
+
+    lax.fori_loop(0, count, one, 0)
+
+    def drain(block, carry):
+        @pl.when((block <= place) & (place < count - 1))
+        def _():
+            hop(block, True).wait_send()
+
+        @pl.when((block >= place) & (place > 0))
+        def _():
+            hop(block, False).wait_send()
+
+        return carry
+
+    lax.fori_loop(0, count, drain, 0)
+
+
+def scatter_sums(place, count, partial, term, total, sending, arrived, send_sem, recv_sem):
+    chunk = min(32, total.shape[0])
+
+    def hop(owner, right):
+        if right:
+            slot, target = owner, place + 1
+        else:
+            slot, target = jnp.where(owner == place - 1, count, owner), place - 1
+        return pltpu.make_async_remote_copy(
+            src_ref=sending.at[owner],
+            dst_ref=arrived.at[slot],
+            send_sem=send_sem.at[owner],
+            recv_sem=recv_sem.at[slot],
+            device_id={"tensor": target},
+            device_id_type=MESH,
+        )
+
+    def landed(slot):
+        return pltpu.make_async_remote_copy(
+            src_ref=sending.at[place],
+            dst_ref=arrived.at[slot],
+            send_sem=send_sem.at[place],
+            recv_sem=recv_sem.at[slot],
+            device_id={"tensor": place},
+            device_id_type=MESH,
+        )
+
+    def add(slot):
+        def rows(number, carry):
+            at = pl.ds(pl.multiple_of(number * chunk, chunk), chunk)
+            total[at, :] = total[at, :] + arrived[slot, at, :].astype(F32)
+            return carry
+
+        lax.fori_loop(0, total.shape[0] // chunk, rows, 0)
+
+    def pack(owner):
+        def rows(number, carry):
+            at = pl.ds(pl.multiple_of(number * chunk, chunk), chunk)
+            sending[owner, at, :] = total[at, :].astype(sending.dtype)
+            return carry
+
+        lax.fori_loop(0, total.shape[0] // chunk, rows, 0)
+
+    def pack_sum(owner):
+        def rows(number, carry):
+            at = pl.ds(pl.multiple_of(number * chunk, chunk), chunk)
+            sending[owner, at, :] = (total[at, :] + arrived[owner, at, :].astype(F32)).astype(
+                sending.dtype
+            )
+            return carry
+
+        lax.fori_loop(0, total.shape[0] // chunk, rows, 0)
+
+    def one(step, carry):
+        owner = line_order(count - 1 - step, place, count)
+        term(owner)
+        onward = ((owner > place) & (place > 0)) | ((owner < place) & (place < count - 1))
+
+        @pl.when(onward)
+        def _():
+            landed(owner).wait_recv()
+            pack_sum(owner)
+
+        @pl.when((owner != place) & jnp.logical_not(onward))
+        def _():
+            pack(owner)
+
+        @pl.when(owner > place)
+        def _():
+            hop(owner, True).start()
+
+        @pl.when(owner < place)
+        def _():
+            hop(owner, False).start()
+
+        return carry
+
+    lax.fori_loop(0, count, one, 0)
+
+    @pl.when(place > 0)
+    def _():
+        landed(place).wait_recv()
+        add(place)
+
+    @pl.when(place < count - 1)
+    def _():
+        landed(count).wait_recv()
+        add(count)
+
+    def drain(owner, carry):
+        @pl.when(owner > place)
+        def _():
+            hop(owner, True).wait_send()
+
+        @pl.when(owner < place)
+        def _():
+            hop(owner, False).wait_send()
+
+        return carry
+
+    lax.fori_loop(0, count, drain, 0)
+
+
+def each_tile(width, tile, run):
+    def one(number, carry):
+        run(pl.multiple_of(number * tile, tile), tile)
+        return carry
+
+    lax.fori_loop(0, width // tile, one, 0)
+    if width % tile:
+        run(width // tile * tile, width % tile)
+
+
+def each_rows(count, chunk, run):
+    def one(number, carry):
+        run(pl.ds(pl.multiple_of(number * chunk, chunk), chunk))
+        return carry
+
+    lax.fori_loop(0, count // chunk, one, 0)
+
+
+def norm_rows(values):
+    average = jnp.mean(values, axis=-1, keepdims=True)
+    centred = values - average
+    variance = jnp.mean(centred * centred, axis=-1, keepdims=True)
+    inverse = lax.rsqrt(variance + norm_eps)
+    return centred * inverse, inverse
+
+
+def add_and_norm(total, before, gain, shift, after, normed):
+    def rows(at):
+        hidden = before[at, :] + total[at, :]
+        after[at, :] = hidden
+        scaled, _ = norm_rows(hidden)
+        normed[at, :] = (scaled * gain[...] + shift[...]).astype(BF16)
+
+    each_rows(total.shape[0], 16, rows)
+
+
+def norm_back_rows(total, grad, hidden, gain, out, out_low, gain_sum, shift_sum):
+    gain_sum[...] = jnp.zeros_like(gain_sum)
+    shift_sum[...] = jnp.zeros_like(shift_sum)
+
+    def rows(at):
+        grad_normed = total[at, :]
+        scaled, inverse = norm_rows(hidden[at, :])
+        weighted = grad_normed * gain[...]
+        first = jnp.mean(weighted, axis=-1, keepdims=True)
+        product = grad_normed * scaled
+        second = jnp.mean(weighted * scaled, axis=-1, keepdims=True)
+        result = grad[at, :] + inverse * (weighted - first - scaled * second)
+        out[at, :] = result
+        out_low[at, :] = result.astype(BF16)
+        gain_sum[...] += jnp.sum(product, axis=0, keepdims=True)
+        shift_sum[...] += jnp.sum(grad_normed, axis=0, keepdims=True)
+
+    each_rows(total.shape[0], 16, rows)
+
+
+def line_scratch(count, rows, width):
+    return [
+        pltpu.VMEM((rows, width), F32),
+        pltpu.VMEM((count, rows, width), BF16),
+        pltpu.VMEM((count + 1, rows, width), BF16),
+        pltpu.SemaphoreType.DMA((count,)),
+        pltpu.SemaphoreType.DMA((count + 1,)),
+    ]
+
+
+def gather_scratch(count, rows, width):
+    return [
+        pltpu.VMEM((count, rows, width), BF16),
+        pltpu.SemaphoreType.DMA((2, count)),
+        pltpu.SemaphoreType.DMA((count,)),
+        pltpu.SemaphoreType.DMA((count,)),
+    ]
+
+
+vmem = pl.BlockSpec(memory_space=pltpu.VMEM)
+hbm = pl.BlockSpec(memory_space=pl.ANY)
+
+
+def line_call(body, out_shape, out_specs, in_specs, scratch, number, flops, moved):
+    return pl.pallas_call(
+        body,
+        out_shape=out_shape,
+        in_specs=in_specs,
+        out_specs=out_specs,
+        scratch_shapes=scratch,
+        compiler_params=pltpu.CompilerParams(
+            collective_id=number, has_side_effects=True, vmem_limit_bytes=VMEM_LIMIT
+        ),
+        cost_estimate=pl.CostEstimate(flops=flops, bytes_accessed=moved, transcendentals=0),
+    )
+
+
+def qkv_kernel(
+    count, own, weight, bias, cos, sin_up, sin_down, rows_out, mixed_out,
+    held, send_sem, recv_sem, out_sem, weight_held, mixed, weight_sem, mixed_sem,
+):
+    place = lax.axis_index("tensor")
+    load = pltpu.make_async_copy(weight, weight_held, weight_sem)
+    load.start()
+    line_barrier(place, count)
+    held[place] = own[...]
+    rows = own.shape[0]
+    width = mixed.shape[3]
+    tile = min(256, width)
+
+    def save(block):
+        return (
+            pltpu.make_async_copy(held.at[block], rows_out.at[block], out_sem.at[block]),
+            pltpu.make_async_copy(mixed.at[:, block], mixed_out.at[:, block], mixed_sem.at[block]),
+        )
+
+    def process(block):
+        @pl.when(block == place)
+        def _():
+            load.wait()
+
+        at = pl.ds(pl.multiple_of(block * rows, rows), rows)
+
+        def columns(kind):
+            def run(start, size):
+                source = pl.ds(pl.multiple_of(kind * width + start, 128), size)
+                target = pl.ds(start, size)
+                result = matmul(held[block], weight_held[:, source]) + bias[:, source]
+                if kind < 2:
+                    result = (
+                        result * cos[at, :size]
+                        + pltpu.roll(result, size - ROT // 2, 1) * sin_up[at, :size]
+                        + pltpu.roll(result, ROT // 2, 1) * sin_down[at, :size]
+                    )
+                if kind == 0:
+                    result = result * (1.0 / math.sqrt(HD))
+                mixed[kind, block, :, target] = result.astype(BF16)
+
+            return run
+
+        for kind in range(3):
+            each_tile(width, tile, columns(kind))
+        for copy in save(block):
+            copy.start()
+
+    gather_rows(place, count, held, send_sem, recv_sem, process)
+    for block in range(count):
+        for copy in save(block):
+            copy.wait()
+
+
+def gather_qkv(count, own, weight, bias, tables, width):
+    rows, depth = own.shape
+    flops = 2 * count * rows * depth * 3 * width
+    return line_call(
+        functools.partial(qkv_kernel, count),
+        (
+            jax.ShapeDtypeStruct((count, rows, depth), BF16),
+            jax.ShapeDtypeStruct((3, count, rows, width), BF16),
+        ),
+        (hbm, hbm),
+        [vmem, hbm, vmem, vmem, vmem, vmem],
+        gather_scratch(count, rows, depth)
+        + [
+            pltpu.VMEM((depth, 3 * width), BF16),
+            pltpu.VMEM((3, count, rows, width), BF16),
+            pltpu.SemaphoreType.DMA,
+            pltpu.SemaphoreType.DMA((count,)),
+        ],
+        0,
+        flops,
+        weight.size * 2 + own.size * 2 * count * 4,
+    )(own, weight, bias, *tables)
+
+
+def project_kernel(
+    count, source, weight, before, gain, shift, after, normed,
+    total, sending, arrived, send_sem, recv_sem,
+):
+    place = lax.axis_index("tensor")
+    line_barrier(place, count)
+    rows = before.shape[0]
+
+    def term(owner):
+        at = pl.ds(pl.multiple_of(owner * rows, rows), rows)
+
+        def run(start, size):
+            total[:, pl.ds(start, size)] = matmul(source[at, :], weight[:, pl.ds(start, size)])
+
+        each_tile(total.shape[1], 512, run)
+
+    scatter_sums(
+        place, count, None, term, total, sending, arrived, send_sem, recv_sem
+    )
+    add_and_norm(total, before, gain, shift, after, normed)
+
+
+def project_scatter(count, source, weight, before, gain, shift):
+    rows, depth = before.shape
+    return line_call(
+        functools.partial(project_kernel, count),
+        (
+            jax.ShapeDtypeStruct((rows, depth), F32),
+            jax.ShapeDtypeStruct((rows, depth), BF16),
+        ),
+        (vmem, vmem),
+        [vmem] * 5,
+        line_scratch(count, rows, depth),
+        1,
+        2 * source.size * depth,
+        weight.size * 2 + before.size * 12,
+    )(source, weight, before, gain, shift)
+
+
+def feed_kernel(
+    count, own, before, gain, shift, w_up, w_down,
+    after, normed, rows_out, act_out, slope_out, silu_out,
+    held, send_sem, recv_sem, out_sem,
+    total, sending, arrived, sum_send, sum_recv,
+    up_held, down_held, act, slope, silu, weight_sem, act_sem,
+):
+    place = lax.axis_index("tensor")
+    load_up = pltpu.make_async_copy(w_up, up_held, weight_sem.at[0])
+    load_down = pltpu.make_async_copy(w_down, down_held, weight_sem.at[1])
+    load_up.start()
+    load_down.start()
+    line_barrier(place, count)
+    held[place] = own[...]
+    width = act.shape[2]
+
+    def save(block):
+        return (
+            pltpu.make_async_copy(held.at[block], rows_out.at[block], out_sem.at[block]),
+            pltpu.make_async_copy(act.at[block], act_out.at[block], act_sem.at[0, block]),
+            pltpu.make_async_copy(slope.at[block], slope_out.at[block], act_sem.at[1, block]),
+            pltpu.make_async_copy(silu.at[block], silu_out.at[block], act_sem.at[2, block]),
+        )
+
+    def process(block):
+        @pl.when(block == place)
+        def _():
+            load_up.wait()
+
+        def run(start, size):
+            at = pl.ds(start, size)
+            gate = matmul(held[block], up_held[:, at])
+            up = matmul(held[block], up_held[:, pl.ds(pl.multiple_of(width + start, 128), size)])
+            sigmoid = jax.nn.sigmoid(gate)
+            soft = gate * sigmoid
+            act[block, :, at] = (soft * up).astype(BF16)
+            silu[block, :, at] = soft.astype(BF16)
+            slope[block, :, at] = (up * sigmoid * (1.0 + gate * (1.0 - sigmoid))).astype(BF16)
+
+        each_tile(width, 256, run)
+        for copy in save(block):
+            copy.start()
+
+    gather_rows(place, count, held, send_sem, recv_sem, process)
+    load_down.wait()
+
+    def term(owner):
+        def run(start, size):
+            at = pl.ds(start, size)
+            total[:, at] = matmul(act[owner], down_held[:, at])
+
+        each_tile(total.shape[1], 512, run)
+
+    scatter_sums(place, count, None, term, total, sending, arrived, sum_send, sum_recv)
+    add_and_norm(total, before, gain, shift, after, normed)
+    for block in range(count):
+        for copy in save(block):
+            copy.wait()
+
+
+def feed_forward(count, own, before, gain, shift, w_up, w_down):
+    rows, depth = own.shape
+    width = w_down.shape[0]
+    wide = jax.ShapeDtypeStruct((count, rows, width), BF16)
+    return line_call(
+        functools.partial(feed_kernel, count),
+        (
+            jax.ShapeDtypeStruct((rows, depth), F32),
+            jax.ShapeDtypeStruct((rows, depth), BF16),
+            jax.ShapeDtypeStruct((count, rows, depth), BF16),
+            wide,
+            wide,
+            wide,
+        ),
+        (vmem, vmem, hbm, hbm, hbm, hbm),
+        [vmem, vmem, vmem, vmem, hbm, hbm],
+        gather_scratch(count, rows, depth)
+        + line_scratch(count, rows, depth)
+        + [
+            pltpu.VMEM((depth, 2 * width), BF16),
+            pltpu.VMEM((width, depth), BF16),
+            pltpu.VMEM((count, rows, width), BF16),
+            pltpu.VMEM((count, rows, width), BF16),
+            pltpu.VMEM((count, rows, width), BF16),
+            pltpu.SemaphoreType.DMA((2,)),
+            pltpu.SemaphoreType.DMA((3, count)),
+        ],
+        2,
+        6 * count * rows * depth * width,
+        (w_up.size + w_down.size) * 2 + own.size * 60,
+    )(own, before, gain, shift, w_up, w_down)
+
+
+def feed_back_kernel(
+    count, own, grad, hidden, gain, w_up, w_down, slope_in, silu_in,
+    out, out_low, gain_sum, shift_sum, rows_out, wide_out,
+    held, send_sem, recv_sem, out_sem,
+    total, sending, arrived, sum_send, sum_recv,
+    up_held, down_held, wide, slope, silu, weight_sem, wide_sem,
+):
+    place = lax.axis_index("tensor")
+    loads = (
+        pltpu.make_async_copy(w_down, down_held, weight_sem.at[0]),
+        pltpu.make_async_copy(slope_in, slope, weight_sem.at[1]),
+        pltpu.make_async_copy(silu_in, silu, weight_sem.at[2]),
+    )
+    load_up = pltpu.make_async_copy(w_up, up_held, weight_sem.at[3])
+    for load in loads:
+        load.start()
+    load_up.start()
+    line_barrier(place, count)
+    held[place] = own[...]
+    width = slope.shape[2]
+
+    def save(block):
+        return (
+            pltpu.make_async_copy(held.at[block], rows_out.at[block], out_sem.at[block]),
+            pltpu.make_async_copy(wide.at[block], wide_out.at[block], wide_sem.at[block]),
+        )
+
+    def process(block):
+        @pl.when(block == place)
+        def _():
+            for load in loads:
+                load.wait()
+
+        def run(start, size):
+            at = pl.ds(start, size)
+            grad_act = matmul(held[block], down_held[at, :], cols_cols)
+            wide[block, :, at] = (grad_act * slope[block, :, at].astype(F32)).astype(BF16)
+            wide[block, :, pl.ds(pl.multiple_of(width + start, 128), size)] = (
+                grad_act * silu[block, :, at].astype(F32)
+            ).astype(BF16)
+
+        each_tile(width, 256, run)
+        for copy in save(block):
+            copy.start()
+
+    gather_rows(place, count, held, send_sem, recv_sem, process)
+    load_up.wait()
+
+    def term(owner):
+        def run(start, size):
+            at = pl.ds(start, size)
+            total[:, at] = matmul(wide[owner], up_held[at, :], cols_cols)
+
+        each_tile(total.shape[1], 256, run)
+
+    scatter_sums(place, count, None, term, total, sending, arrived, sum_send, sum_recv)
+    norm_back_rows(total, grad, hidden, gain, out, out_low, gain_sum, shift_sum)
+    for block in range(count):
+        for copy in save(block):
+            copy.wait()
+
+
+def feed_backward(count, own, grad, hidden, gain, w_up, w_down, slope, silu):
+    rows, depth = own.shape
+    width = w_down.shape[0]
+    return line_call(
+        functools.partial(feed_back_kernel, count),
+        (
+            jax.ShapeDtypeStruct((rows, depth), F32),
+            jax.ShapeDtypeStruct((rows, depth), BF16),
+            jax.ShapeDtypeStruct((1, depth), F32),
+            jax.ShapeDtypeStruct((1, depth), F32),
+            jax.ShapeDtypeStruct((count, rows, depth), BF16),
+            jax.ShapeDtypeStruct((count, rows, 2 * width), BF16),
+        ),
+        (vmem, vmem, vmem, vmem, hbm, hbm),
+        [vmem, vmem, vmem, vmem, hbm, hbm, hbm, hbm],
+        gather_scratch(count, rows, depth)
+        + line_scratch(count, rows, depth)
+        + [
+            pltpu.VMEM((depth, 2 * width), BF16),
+            pltpu.VMEM((width, depth), BF16),
+            pltpu.VMEM((count, rows, 2 * width), BF16),
+            pltpu.VMEM((count, rows, width), BF16),
+            pltpu.VMEM((count, rows, width), BF16),
+            pltpu.SemaphoreType.DMA((4,)),
+            pltpu.SemaphoreType.DMA((count,)),
+        ],
+        3,
+        6 * count * rows * depth * width,
+        (w_up.size + w_down.size) * 2 + own.size * 60,
+    )(own, grad, hidden, gain, w_up, w_down, slope, silu)
+
+
+def grad_attended_kernel(
+    count, own, weight, rows_out, result_out,
+    held, send_sem, recv_sem, out_sem, weight_held, result, weight_sem, result_sem,
+):
+    place = lax.axis_index("tensor")
+    load = pltpu.make_async_copy(weight, weight_held, weight_sem)
+    load.start()
+    line_barrier(place, count)
+    held[place] = own[...]
+
+    def save(block):
+        return (
+            pltpu.make_async_copy(held.at[block], rows_out.at[block], out_sem.at[block]),
+            pltpu.make_async_copy(result.at[block], result_out.at[block], result_sem.at[block]),
+        )
+
+    def process(block):
+        @pl.when(block == place)
+        def _():
+            load.wait()
+
+        def run(start, size):
+            at = pl.ds(start, size)
+            result[block, :, at] = matmul(held[block], weight_held[at, :], cols_cols).astype(BF16)
+
+        each_tile(result.shape[2], 256, run)
+        for copy in save(block):
+            copy.start()
+
+    gather_rows(place, count, held, send_sem, recv_sem, process)
+    for block in range(count):
+        for copy in save(block):
+            copy.wait()
+
+
+def gather_grad_attended(count, own, weight):
+    rows, depth = own.shape
+    width = weight.shape[0]
+    return line_call(
+        functools.partial(grad_attended_kernel, count),
+        (
+            jax.ShapeDtypeStruct((count, rows, depth), BF16),
+            jax.ShapeDtypeStruct((count, rows, width), BF16),
+        ),
+        (hbm, hbm),
+        [vmem, hbm],
+        gather_scratch(count, rows, depth)
+        + [
+            pltpu.VMEM((width, depth), BF16),
+            pltpu.VMEM((count, rows, width), BF16),
+            pltpu.SemaphoreType.DMA,
+            pltpu.SemaphoreType.DMA((count,)),
+        ],
+        4,
+        2 * count * rows * depth * width,
+        weight.size * 2 + own.size * 40,
+    )(own, weight)
+
+
+def input_back_kernel(
+    count, source, weight, grad, hidden, gain, out, out_low, gain_sum, shift_sum,
+    total, sending, arrived, send_sem, recv_sem,
+):
+    place = lax.axis_index("tensor")
+    line_barrier(place, count)
+    width = source.shape[2]
+    rows = total.shape[0]
+
+    def term(owner):
+        at_rows = pl.ds(pl.multiple_of(owner * rows, rows), rows)
+
+        def run(start, size):
+            at = pl.ds(start, size)
+            result = matmul(source[0, at_rows, :], weight[at, :width], cols_cols)
+            for kind in range(1, 3):
+                result = result + matmul(
+                    source[kind, at_rows, :],
+                    weight[at, kind * width : (kind + 1) * width],
+                    cols_cols,
+                )
+            total[:, at] = result
+
+        each_tile(total.shape[1], 256, run)
+
+    scatter_sums(place, count, None, term, total, sending, arrived, send_sem, recv_sem)
+    norm_back_rows(total, grad, hidden, gain, out, out_low, gain_sum, shift_sum)
+
+
+def input_backward(count, source, weight, grad, hidden, gain):
+    rows, depth = grad.shape
+    return line_call(
+        functools.partial(input_back_kernel, count),
+        (
+            jax.ShapeDtypeStruct((rows, depth), F32),
+            jax.ShapeDtypeStruct((rows, depth), BF16),
+            jax.ShapeDtypeStruct((1, depth), F32),
+            jax.ShapeDtypeStruct((1, depth), F32),
+        ),
+        (vmem, vmem, vmem, vmem),
+        [vmem] * 5,
+        line_scratch(count, rows, depth),
+        5,
+        2 * source.size * depth,
+        weight.size * 2 + grad.size * 20,
+    )(source, weight, grad, hidden, gain)
+
+
+def usable(first, start, keys, queries):
+    key_index = lax.broadcasted_iota(jnp.int32, (keys, queries), 0)
+    query_index = start + lax.broadcasted_iota(jnp.int32, (keys, queries), 1)
+    return (key_index >= first) & (key_index <= query_index)
+
+
+def head_lanes(values, head):
+    lane = lax.broadcasted_iota(jnp.int32, values.shape, 1)
+    return jnp.where((lane // HD) == head, values, jnp.zeros_like(values))
+
+
+def attend_kernel(block, positions, queries, keys, values, attended, logsums):
+    length = keys.shape[0]
+    values_across = jnp.transpose(values[...])
+    for start in range(0, length, block):
+        seen = start + block
+        at = slice(start, seen)
+        own = queries[at, :]
+        index = start + lax.broadcasted_iota(jnp.int32, (1, block), 1)
+        allowed = usable(index - positions[:, at], start, seen, block)
+        halves = []
+        for head in range(2):
+            scores = matmul(keys[:seen, :], head_lanes(own, head), cols_cols)
+            scores = jnp.where(allowed, scores, masked_score)
+            highest = jnp.max(scores, axis=0, keepdims=True)
+            weights = jnp.exp(scores - highest)
+            sums = jnp.sum(weights, axis=0, keepdims=True)
+            result = matmul(values_across[:, :seen], weights.astype(BF16))
+            halves.append(result[head * HD : (head + 1) * HD, :] / sums)
+            logsums[head : head + 1, at] = highest + jnp.log(sums)
+        attended[at, :] = jnp.transpose(jnp.concatenate(halves, axis=0)).astype(BF16)
+
+
+def pair_spec(length, kind):
+    return pl.BlockSpec((None, length, PAIR), lambda pair: (kind, 0, pair))
+
+
+def attend(mixed, positions):
+    _, length, width = mixed.shape
+    pairs = width // PAIR
+    block = min(256, length)
+    return pl.pallas_call(
+        functools.partial(attend_kernel, block),
+        grid=(pairs,),
+        out_shape=(
+            jax.ShapeDtypeStruct((length, width), BF16),
+            jax.ShapeDtypeStruct((pairs, 2, length), F32),
+        ),
+        in_specs=[
+            pl.BlockSpec((1, length), lambda pair: (0, 0)),
+            pair_spec(length, 0),
+            pair_spec(length, 1),
+            pair_spec(length, 2),
+        ],
+        out_specs=(
+            pl.BlockSpec((length, PAIR), lambda pair: (0, pair)),
+            pl.BlockSpec((None, 2, length), lambda pair: (pair, 0, 0)),
+        ),
+        compiler_params=pltpu.CompilerParams(vmem_limit_bytes=VMEM_LIMIT),
+        cost_estimate=pl.CostEstimate(
+            flops=8 * length * length * width,
+            bytes_accessed=8 * length * width,
+            transcendentals=length * length * width // HD,
+        ),
+    )(positions, mixed, mixed, mixed)
+
+
+def unrotate(values, cos, sin_up, sin_down):
+    return (
+        values * cos
+        - pltpu.roll(values, PAIR - ROT // 2, 1) * sin_up
+        - pltpu.roll(values, ROT // 2, 1) * sin_down
+    )
+
+
+def attend_back_kernel(
+    block, positions, queries, keys, values, attended, grad_attended, logsums,
+    cos, sin_up, sin_down, grad_mixed, bias_sum, grad_keys, grad_values,
+):
+    length = keys.shape[0]
+    keys_across = jnp.transpose(keys[...])
+    grad_keys[...] = jnp.zeros_like(grad_keys)
+    grad_values[...] = jnp.zeros_like(grad_values)
+    bias_sum[...] = jnp.zeros_like(bias_sum)
+    for start in range(0, length, block):
+        seen = start + block
+        at = slice(start, seen)
+        own = queries[at, :]
+        grad_own = grad_attended[at, :]
+        inner = jnp.transpose(grad_own.astype(F32) * attended[at, :].astype(F32))
+        index = start + lax.broadcasted_iota(jnp.int32, (1, block), 1)
+        allowed = usable(index - positions[:, at], start, seen, block)
+        halves = []
+        for head in range(2):
+            own_head = head_lanes(own, head)
+            grad_head = head_lanes(grad_own, head)
+            scores = matmul(keys[:seen, :], own_head, cols_cols)
+            weights = jnp.where(allowed, jnp.exp(scores - logsums[head : head + 1, at]), 0.0)
+            grad_weights = matmul(values[:seen, :], grad_head, cols_cols)
+            row_inner = jnp.sum(inner[head * HD : (head + 1) * HD, :], axis=0, keepdims=True)
+            grad_scores = (weights * (grad_weights - row_inner)).astype(BF16)
+            grad_values[:seen, :] += matmul(weights.astype(BF16), grad_head)
+            grad_keys[:seen, :] += matmul(grad_scores, own_head)
+            result = matmul(keys_across[:, :seen], grad_scores)
+            halves.append(result[head * HD : (head + 1) * HD, :])
+        grad_own_queries = jnp.transpose(jnp.concatenate(halves, axis=0)) * (1.0 / math.sqrt(HD))
+        low = unrotate(grad_own_queries, cos[at, :], sin_up[at, :], sin_down[at, :]).astype(BF16)
+        grad_mixed[0, at, :] = low
+        bias_sum[0:1, :] += jnp.sum(low.astype(F32), axis=0, keepdims=True)
+    for start in range(0, length, block):
+        at = slice(start, start + block)
+        low = unrotate(grad_keys[at, :], cos[at, :], sin_up[at, :], sin_down[at, :]).astype(BF16)
+        grad_mixed[1, at, :] = low
+        bias_sum[1:2, :] += jnp.sum(low.astype(F32), axis=0, keepdims=True)
+        low = grad_values[at, :].astype(BF16)
+        grad_mixed[2, at, :] = low
+        bias_sum[2:3, :] += jnp.sum(low.astype(F32), axis=0, keepdims=True)
+
+
+def attend_backward(mixed, positions, attended, grad_attended, logsums, tables):
+    _, length, width = mixed.shape
+    pairs = width // PAIR
+    block = min(256, length)
+    across = pl.BlockSpec((length, PAIR), lambda pair: (0, pair))
+    table = pl.BlockSpec((length, PAIR), lambda pair: (0, 0))
+    return pl.pallas_call(
+        functools.partial(attend_back_kernel, block),
+        grid=(pairs,),
+        out_shape=(
+            jax.ShapeDtypeStruct((3, length, width), BF16),
+            jax.ShapeDtypeStruct((3, width), F32),
+        ),
+        in_specs=[
+            pl.BlockSpec((1, length), lambda pair: (0, 0)),
+            pair_spec(length, 0),
+            pair_spec(length, 1),
+            pair_spec(length, 2),
+            across,
+            across,
+            pl.BlockSpec((None, 2, length), lambda pair: (pair, 0, 0)),
+            table,
+            table,
+            table,
+        ],
+        out_specs=(
+            pl.BlockSpec((3, length, PAIR), lambda pair: (0, 0, pair)),
+            pl.BlockSpec((3, PAIR), lambda pair: (0, pair)),
+        ),
+        scratch_shapes=[pltpu.VMEM((length, PAIR), F32), pltpu.VMEM((length, PAIR), F32)],
+        compiler_params=pltpu.CompilerParams(vmem_limit_bytes=VMEM_LIMIT),
+        cost_estimate=pl.CostEstimate(
+            flops=20 * length * length * width,
+            bytes_accessed=16 * length * width,
+            transcendentals=length * length * width // HD,
+        ),
+    )(positions, mixed, mixed, mixed, attended, grad_attended, logsums, *tables)
+
+
+def rotary_tables(positions, width):
+    half_rot = ROT // 2
+    frequency = jnp.exp(-(jnp.arange(half_rot, dtype=F32) * 2.0 / ROT) * theta_log)
+    angles = positions.astype(F32)[:, None] * frequency[None, :]
+    cos, sin = jnp.cos(angles), jnp.sin(angles)
+    length = positions.shape[0]
+    rest = jnp.ones((length, HD - ROT), F32)
+    none, gap = jnp.zeros((length, half_rot), F32), jnp.zeros((length, HD - ROT), F32)
+    copies = width // HD
+    return (
+        jnp.tile(jnp.concatenate([cos, cos, rest], axis=1), (1, copies)),
+        jnp.tile(jnp.concatenate([-sin, none, gap], axis=1), (1, copies)),
+        jnp.tile(jnp.concatenate([none, sin, gap], axis=1), (1, copies)),
+    )
+
+
+def all_sum(values, axes):
+    for axis in axes:
+        size = lax.axis_size(axis)
+        if size & (size - 1):
+            values = lax.psum(values, axis)
+            continue
+        step = 1
+        while step < size:
+            values = values + lax.ppermute(values, axis, [(i, i ^ step) for i in range(size)])
+            step *= 2
+    return values
+
+
+def per_device(
+    tokens, positions, norm_gain, norm_bias, w_qkv, b_qkv, w_out, w_gate_up, w_down, cotangent
+):
+    count = lax.axis_size("tensor")
+    tensor_rank = lax.axis_index("tensor")
+    width = w_qkv.shape[3]
+    ff_local = w_gate_up.shape[3]
+    rows, depth = tokens.shape
+    length = positions.shape[0]
+    tables = rotary_tables(positions, min(256, width))
+    pair_tables = tuple(table[:, :PAIR] for table in tables)
+    positions_row = positions.reshape(1, length)
+    gathered = []
+    for layer in range(LAYERS):
+        gathered.append(
+            (
+                lax.all_gather(
+                    w_qkv[layer].reshape(-1, 3 * width), "dp", axis=0, tiled=True
+                ),
+                lax.all_gather(w_out[layer], "dp", axis=1, tiled=True),
+                lax.all_gather(
+                    w_gate_up[layer].reshape(-1, 2 * ff_local), "dp", axis=0, tiled=True
+                ),
+                lax.all_gather(w_down[layer], "dp", axis=1, tiled=True),
+            )
+        )
+    hidden = tokens.astype(F32)
+    scaled, _ = norm_rows(hidden)
+    normed = (scaled * norm_gain[0, 0] + norm_bias[0, 0]).astype(BF16)
+    kept = []
+    for layer in range(LAYERS):
+        full_qkv, full_out, full_gu, full_down = gathered[layer]
+        bias = lax.dynamic_slice_in_dim(b_qkv[layer], tensor_rank * width, width, 1)
+        rows_a, mixed = gather_qkv(
+            count, normed, full_qkv, bias.reshape(1, 3 * width), tables, width
+        )
+        mixed = mixed.reshape(3, length, width)
+        attended, logsums = attend(mixed, positions_row)
+        hidden_mid, normed_b = project_scatter(
+            count, attended, full_out, hidden, norm_gain[layer, 1:2], norm_bias[layer, 1:2]
+        )
+        following = min(layer + 1, LAYERS - 1)
+        hidden_next, normed, rows_b, act, slope, silu = feed_forward(
+            count,
+            normed_b,
+            hidden_mid,
+            norm_gain[following, 0:1],
+            norm_bias[following, 0:1],
+            full_gu,
+            full_down,
+        )
+        kept.append(
+            (hidden, rows_a, mixed, attended, logsums, hidden_mid, rows_b, act, slope, silu)
+        )
+        hidden = hidden_next
+    activations = hidden.astype(BF16)
+    grad_low = cotangent
+    grad = cotangent.astype(F32)
+    scattered = [None] * LAYERS
+    small = [None] * LAYERS
+    for layer in reversed(range(LAYERS)):
+        hidden, rows_a, mixed, attended, logsums, hidden_mid, rows_b, act, slope, silu = kept[layer]
+        full_qkv, full_out, full_gu, full_down = gathered[layer]
+        grad, grad_mid_low, gain_b, shift_b, grad_rows_b, wide = feed_backward(
+            count, grad_low, grad, hidden_mid, norm_gain[layer, 1:2], full_gu, full_down, slope, silu
+        )
+        down_part = matmul(
+            act.reshape(length, ff_local), grad_rows_b.reshape(length, depth), rows_rows
+        ).astype(BF16)
+        down_grad = lax.psum_scatter(down_part, "dp", scatter_dimension=1, tiled=True)
+        gu_part = matmul(
+            rows_b.reshape(length, depth), wide.reshape(length, 2 * ff_local), rows_rows
+        ).astype(BF16)
+        gu_grad = lax.psum_scatter(gu_part, "dp", scatter_dimension=0, tiled=True)
+        grad_rows_a, grad_attended = gather_grad_attended(count, grad_mid_low, full_out)
+        out_part = matmul(attended, grad_rows_a.reshape(length, depth), rows_rows).astype(BF16)
+        out_grad = lax.psum_scatter(out_part, "dp", scatter_dimension=1, tiled=True)
+        grad_mixed, bias_sum = attend_backward(
+            mixed, positions_row, attended, grad_attended.reshape(length, width), logsums, pair_tables
+        )
+        flat_mixed = grad_mixed.transpose(1, 0, 2).reshape(length, 3 * width)
+        qkv_part = matmul(rows_a.reshape(length, depth), flat_mixed, rows_rows).astype(BF16)
+        qkv_grad = lax.psum_scatter(qkv_part, "dp", scatter_dimension=0, tiled=True)
+        grad, grad_low, gain_a, shift_a = input_backward(
+            count, grad_mixed, full_qkv, grad, hidden, norm_gain[layer, 0:1]
+        )
+        bias_full = lax.dynamic_update_slice(
+            jnp.zeros((3, b_qkv.shape[2]), F32), bias_sum, (jnp.int32(0), tensor_rank * width)
+        )
+        small[layer] = jnp.concatenate([gain_a, gain_b, shift_a, shift_b, bias_full], axis=0)
+        scattered[layer] = (
+            qkv_grad.astype(F32).reshape(-1, 3, width),
+            out_grad.astype(F32),
+            gu_grad.astype(F32).reshape(-1, 2, ff_local),
+            down_grad.astype(F32),
+        )
+    sums = all_sum(jnp.stack(small), ("dp", "tensor"))
+    stacks = [jnp.stack([scattered[layer][kind] for layer in range(LAYERS)]) for kind in range(4)]
+    return (
+        activations,
+        grad,
+        sums[:, 0:2],
+        sums[:, 2:4],
+        stacks[0],
+        sums[:, 4:7],
+        stacks[1],
+        stacks[2],
+        stacks[3],
+    )
 
 
 def norm_parts(hidden):
@@ -33,7 +1025,7 @@
     return (grad_input, jnp.sum(grad_normed * scaled, axis=0), jnp.sum(grad_normed, axis=0))
 
 
-def rotary_tables(positions):
+def plain_tables(positions):
     half_rot = ROT // 2
     frequency = jnp.exp(-(jnp.arange(half_rot, dtype=jnp.float32) * 2.0 / ROT) * theta_log)
     angles = positions.astype(jnp.float32)[:, None] * frequency[None, :]
@@ -55,11 +1047,11 @@
 
 
 def inner_rows(left, right):
-    return lax.dot_general(left, right, contract_rows, preferred_element_type=jnp.float32)
+    return lax.dot_general(left, right, rows_rows, preferred_element_type=jnp.float32)
 
 
 def inner_cols(left, right):
-    return lax.dot_general(left, right, contract_cols, preferred_element_type=jnp.float32)
+    return lax.dot_general(left, right, cols_cols, preferred_element_type=jnp.float32)
 
 
 def block_scores(queries, key_rows, positions, number, block_rows, score_scale):
@@ -144,7 +1136,7 @@
     return (grad_queries.reshape(queries.shape), grad_keys, grad_values)
 
 
-def per_device(
+def per_device_plain(
     tokens, positions, norm_gain, norm_bias, w_qkv, b_qkv, w_out, w_gate_up, w_down, cotangent
 ):
     tensor_rank = lax.axis_index("tensor")
@@ -154,7 +1146,7 @@
     local_rows = tokens.shape[0]
     seq_len = positions.shape[0]
     score_scale = 1.0 / math.sqrt(HD)
-    cos_table, sin_table = rotary_tables(positions)
+    cos_table, sin_table = plain_tables(positions)
     hidden = tokens.astype(jnp.float32)
     kept_state = []
     for layer_index in range(LAYERS):
@@ -385,6 +1377,10 @@
         P(None, "dp", None, "tensor"),
         P(None, "tensor", "dp"),
     )
+    def run(*operands):
+        fits = operands[7].shape[3] % 128 == 0 and operands[4].shape[3] % PAIR == 0
+        return (per_device if fits else per_device_plain)(*operands)
+
     return jax.shard_map(
-        per_device, mesh=mesh, in_specs=in_specs, out_specs=out_specs, check_vma=False
+        run, mesh=mesh, in_specs=in_specs, out_specs=out_specs, check_vma=False
     )

time: 2740 us -> 1760 us (0.64)
  waiting for transfers between devices: 1740 us -> 282 us
  Pallas kernels: 0 us -> 1280 us
  matrix products: 596 us -> 92.2 us
  local copies, waits for them, and re-layouts: 255 us -> 47.3 us
  other arithmetic: 105 us -> 19.8 us
    pallas_call x0 -> x16, Pallas kernels: none -> 1280 us  [the longest x2 309 us: feed_backward(): line_call(functools.partial(feed_back_kernel, count), (jax.ShapeDtypeStru...]
    all_gather x16 -> x8, waiting for transfers between devices: 805 us -> 24.3 us  [the longest x2 24.2 us: per_device(): lax.all_gather(w_qkv[layer].reshape(-1, 3 * width), 'dp', axis=0, tiled=T...]
    reduce_scatter x16 -> x8, waiting for transfers between devices: 808 us -> 235 us  [the longest x2 171 us: per_device(): gu_grad = lax.psum_scatter(gu_part, 'dp', scatter_dimension=0, tiled=True)]
    dot_general x52 -> x8, matrix products: 596 us -> 92.2 us  [matmul(): return lax.dot_general(left, right, dims, preferred_element_type=F32)]
    psum x1 -> x0, waiting for transfers between devices: 125 us -> none  [per_device(): lax.psum((jnp.stack(gain_rows), jnp.stack(shift_rows), jnp.stack(qkv_shif...]
    dynamic_update_slice x10 -> x2, local copies, waits for them, and re-layouts: 87.7 us -> 0.02 us  [per_device(): lax.dynamic_update_slice(jnp.zeros((3, b_qkv.shape[2]), F32), bias_sum, (...]
    reduce_sum x18 -> x2, other arithmetic: 42 us -> 0.64 us  [the longest x1 0.42 us: norm_rows(): variance = jnp.mean(centred * centred, axis=-1, keepdims=True)]
    unnamed x194 -> x57, local copies, waits for them, and re-layouts: 49.2 us -> 12.1 us
  transfers between devices with their start and end apart: 33 -> 21, of which waited for: 27 -> 10; matrix products, arithmetic and copies ran while one was open for 22% -> 8% of each run, Pallas kernels for 0% -> 52%
where the time goes in v1:
time: 1760 us; the launch traced here: 1750 us
  Pallas kernels  1280 us (73%)
  waiting for transfers between devices  282 us (16%)
  matrix products  92.2 us (5%)
  local copies, waits for them, and re-layouts  47.3 us (3%)
  other arithmetic  19.8 us (1%)
    pallas_call x2, Pallas kernels, feed_backward(): line_call(functools.partial(feed_back_kernel, count), (jax.ShapeDtypeStru...  309 us
    pallas_call x2, Pallas kernels, feed_forward(): line_call(functools.partial(feed_kernel, count), (jax.ShapeDtypeStruct((r...  297 us
    reduce_scatter x2, waiting for transfers between devices, per_device(): gu_grad = lax.psum_scatter(gu_part, 'dp', scatter_dimension=0, tiled=True)  171 us
    pallas_call x2, Pallas kernels, input_backward(): line_call(functools.partial(input_back_kernel, count), (jax.ShapeDtypeStr...  164 us
    pallas_call x2, Pallas kernels, gather_qkv(): line_call(functools.partial(qkv_kernel, count), (jax.ShapeDtypeStruct((co...  157 us
    pallas_call x2, Pallas kernels, project_scatter(): line_call(functools.partial(project_kernel, count), (jax.ShapeDtypeStruct...  150 us
    pallas_call x2, Pallas kernels, gather_grad_attended(): line_call(functools.partial(grad_attended_kernel, count), (jax.ShapeDtype...  132 us
    dot_general x8, matrix products, matmul(): return lax.dot_general(left, right, dims, preferred_element_type=F32)  92.2 us
  transfers between devices with their start and end apart: 21, of which 10 were waited for; matrix products, arithmetic and copies ran while one was open for 8% of the time, Pallas kernels for 52%

profile of v1, /device:TPU:0, one launch (start us, length us, event | category | flops | bytes accessed | tf_op | source)
XLA Modules:
  0.0 1751.6 jit_solution(17444315714095869599)
XLA Ops:
  12.5 3.7 fusion.2
  34.4 24.2 %all-gather.13.cloned.1.call-done.weight = bf16[2048,1536]{1,0:T(8,128)(2,1)} async-done(((bf16[256,1536]{1,0:T(8,128)(2,1)}), bf16[2048,1536]{1,0:T(8,128)(2,1)}) %all-gather.13.cloned.1.call-update) | async-done | bytes 6291472 | tf_op jit(solution)/shard_map/all_gather | solution.py:917
  58.6 83.4 %shard_map.169 = (bf16[4,256,2048]{2,1,0:T(8,128)(2,1)}, bf16[3,4,256,512]{3,2,1,0:T(8,128)(2,1)}) custom-call(bf16[256,2048]{1,0:T(8,128)(2,1)} %add_convert_fusion.own, bf16[2048,1536]{1,0:T(8,128)(2,1)} %all-gather.13.cloned.1.call-done.weight, f32[1,1536]{1,0:T(1,128)} %bitcast.106, f32[1024,256]{1,0:T(8,128)} %copy-done.4, f32[1024,256]{1,0:T(8,128)} %copy-done.3, ...), custom_call_target="tpu_custom_call" | custom-call | flops 6442450944 | bytes 23068672 | tf_op jit(solution)/shard_map/pallas_call | solution.py:360
  142.0 18.3 %shard_map.170 = (bf16[1024,512]{1,0:T(8,128)(2,1)}, f32[4,2,1024]{2,1,0:T(2,128)}) custom-call(s32[1,1024]{1,0:T(1,128)} %bitcast.107, bf16[3,1024,512]{2,1,0:T(8,128)(2,1)} %bitcast.123, bf16[3,1024,512]{2,1,0:T(8,128)(2,1)} %bitcast.124, bf16[3,1024,512]{2,1,0:T(8,128)(2,1)} %bitcast.125), custom_call_target="tpu_custom_call" | custom-call | flops 4294967296 | bytes 4194304 | tf_op jit(solution)/shard_map/pallas_call | solution.py:755
  160.3 78.0 %shard_map.171 = (f32[256,2048]{1,0:T(8,128)}, bf16[256,2048]{1,0:T(8,128)(2,1)}) custom-call(bf16[1024,512]{1,0:T(8,128)(2,1)} %get-tuple-element.60.source.attended, bf16[512,2048]{1,0:T(8,128)(2,1)} %bitcast.115, f32[256,2048]{1,0:T(8,128)} %convert_element_type.47.before.hidden, f32[1,2048]{1,0:T(1,128)} %get-tuple-element.142.gain, ...), custom_call_target="tpu_custom_call" | custom-call | flops 2147483648 | bytes 8388608 | tf_op jit(solution)/shard_map/pallas_call | solution.py:405
  238.4 150.1 %shard_map.172 = (f32[256,2048]{1,0:T(8,128)}, bf16[256,2048]{1,0:T(8,128)(2,1)}, bf16[4,256,2048]{2,1,0:T(8,128)(2,1)}, bf16[4,256,1408]{2,1,0:T(8,128)(2,1)}, ...) custom-call(bf16[256,2048]{1,0:T(8,128)(2,1)} %get-tuple-element.61.own, ...), custom_call_target="tpu_custom_call" | custom-call | flops 17716740096 | bytes 48758784 | tf_op jit(solution)/shard_map/pallas_call | solution.py:484
  388.5 73.3 %shard_map.173 = (bf16[4,256,2048]{2,1,0:T(8,128)(2,1)}, bf16[3,4,256,512]{3,2,1,0:T(8,128)(2,1)}) custom-call(bf16[256,2048]{1,0:T(8,128)(2,1)} %get-tuple-element.63.own, bf16[2048,1536]{1,0:T(8,128)(2,1)} %all-gather.17.cloned.1.call-done.weight, f32[1,1536]{1,0:T(1,128)} %bitcast.105, f32[1024,256]{1,0:T(8,128)} %copy-done.4, f32[1024,256]{1,0:T(8,128)} %copy-done.3, ...), custom_call_target="tpu_custom_call" | custom-call | flops 6442450944 | bytes 23068672 | tf_op jit(solution)/shard_map/pallas_call | solution.py:360
  461.9 18.4 %shard_map.174 = (bf16[1024,512]{1,0:T(8,128)(2,1)}, f32[4,2,1024]{2,1,0:T(2,128)}) custom-call(s32[1,1024]{1,0:T(1,128)} %bitcast.108, bf16[3,1024,512]{2,1,0:T(8,128)(2,1)} %bitcast.129, bf16[3,1024,512]{2,1,0:T(8,128)(2,1)} %bitcast.130, bf16[3,1024,512]{2,1,0:T(8,128)(2,1)} %bitcast.131), custom_call_target="tpu_custom_call" | custom-call | flops 4294967296 | bytes 4194304 | tf_op jit(solution)/shard_map/pallas_call | solution.py:755
  480.2 72.2 %shard_map.175 = (f32[256,2048]{1,0:T(8,128)}, bf16[256,2048]{1,0:T(8,128)(2,1)}) custom-call(bf16[1024,512]{1,0:T(8,128)(2,1)} %get-tuple-element.65.source.attended, bf16[512,2048]{1,0:T(8,128)(2,1)} %bitcast.117, f32[256,2048]{1,0:T(8,128)} %get-tuple-element.66.before.hidden, f32[1,2048]{1,0:T(1,128)} %get-tuple-element.144.gain, ...), custom_call_target="tpu_custom_call" | custom-call | flops 2147483648 | bytes 8388608 | tf_op jit(solution)/shard_map/pallas_call | solution.py:405
  552.5 147.3 %shard_map.176 = (f32[256,2048]{1,0:T(8,128)}, bf16[256,2048]{1,0:T(8,128)(2,1)}, bf16[4,256,2048]{2,1,0:T(8,128)(2,1)}, bf16[4,256,1408]{2,1,0:T(8,128)(2,1)}, ...) custom-call(bf16[256,2048]{1,0:T(8,128)(2,1)} %get-tuple-element.67.own, ...), custom_call_target="tpu_custom_call" | custom-call | flops 17716740096 | bytes 48758784 | tf_op jit(solution)/shard_map/pallas_call | solution.py:484
  699.8 153.9 %shard_map.177 = (f32[256,2048]{1,0:T(8,128)}, bf16[256,2048]{1,0:T(8,128)(2,1)}, f32[1,2048]{1,0:T(1,128)}, f32[1,2048]{1,0:T(1,128)}, bf16[4,256,2048]{2,1,0:T(8,128)(2,1)}, /*index=5*/bf16[4,256,2816]{2,1,0:T(8,128)(2,1)}) custom-call(bf16[256,2048]{1,0:T(8,128)(2,1)} %own.1, f32[256,2048]{1,0:T(8,128)} %convert_element_type.51.grad, ...), custom_call_target="tpu_custom_call" | custom-call | flops 17716740096 | bytes 48758784 | tf_op jit(solution)/shard_map/pallas_call | solution.py:578
  853.8 66.0 %shard_map.178 = (bf16[4,256,2048]{2,1,0:T(8,128)(2,1)}, bf16[4,256,512]{2,1,0:T(8,128)(2,1)}) custom-call(bf16[256,2048]{1,0:T(8,128)(2,1)} %get-tuple-element.72.own, bf16[512,2048]{1,0:T(8,128)(2,1)} %bitcast.118), custom_call_target="tpu_custom_call" | custom-call | flops 2147483648 | bytes 23068672 | tf_op jit(solution)/shard_map/pallas_call | solution.py:645
  919.8 5.9 convolution_convert_fusion.2
  925.8 18.7 %shard_map.179 = (bf16[3,1024,512]{2,1,0:T(8,128)(2,1)}, f32[3,512]{1,0:T(4,128)}) custom-call(s32[1,1024]{1,0:T(1,128)} %bitcast.109, bf16[3,1024,512]{2,1,0:T(8,128)(2,1)} %bitcast.132, bf16[3,1024,512]{2,1,0:T(8,128)(2,1)} %bitcast.133, bf16[3,1024,512]{2,1,0:T(8,128)(2,1)} %bitcast.134, bf16[1024,512]{1,0:T(8,128)(2,1)} %get-tuple-element.65.source.attended, ...), custom_call_target="tpu_custom_call" | custom-call | flops 10737418240 | bytes 8388608 | tf_op jit(solution)/shard_map/pallas_call | solution.py:839
  944.5 81.6 %shard_map.180 = (f32[256,2048]{1,0:T(8,128)}, bf16[256,2048]{1,0:T(8,128)(2,1)}, f32[1,2048]{1,0:T(1,128)}, f32[1,2048]{1,0:T(1,128)}) custom-call(bf16[3,1024,512]{2,1,0:T(8,128)(2,1)} %get-tuple-element.75.source, bf16[2048,1536]{1,0:T(8,128)(2,1)} %all-gather.17.cloned.1.call-done.weight, f32[256,2048]{1,0:T(8,128)} %get-tuple-element.76.grad, ...), custom_call_target="tpu_custom_call" | custom-call | flops 6442450944 | bytes 16777216 | tf_op jit(solution)/shard_map/pallas_call | solution.py:697
  1026.1 155.4 %shard_map.181 = (f32[256,2048]{1,0:T(8,128)}, bf16[256,2048]{1,0:T(8,128)(2,1)}, f32[1,2048]{1,0:T(1,128)}, f32[1,2048]{1,0:T(1,128)}, bf16[4,256,2048]{2,1,0:T(8,128)(2,1)}, /*index=5*/bf16[4,256,2816]{2,1,0:T(8,128)(2,1)}) custom-call(bf16[256,2048]{1,0:T(8,128)(2,1)} %get-tuple-element.77.own, f32[256,2048]{1,0:T(8,128)} %get-tuple-element.78.grad, ...), custom_call_target="tpu_custom_call" | custom-call | flops 17716740096 | bytes 48758784 | tf_op jit(solution)/shard_map/pallas_call | solution.py:578
  1181.6 65.8 %shard_map.182 = (bf16[4,256,2048]{2,1,0:T(8,128)(2,1)}, bf16[4,256,512]{2,1,0:T(8,128)(2,1)}) custom-call(bf16[256,2048]{1,0:T(8,128)(2,1)} %get-tuple-element.81.own, bf16[512,2048]{1,0:T(8,128)(2,1)} %bitcast.116), custom_call_target="tpu_custom_call" | custom-call | flops 2147483648 | bytes 23068672 | tf_op jit(solution)/shard_map/pallas_call | solution.py:645
  1247.4 5.9 convolution_convert_fusion.3
  1253.8 10.5 bitcast_convert_fusion.3
  1264.4 1.8 copy-done.24
  1266.2 10.7 bitcast_convert_fusion.2
  1277.0 1.8 copy-done.1
  1278.8 3.0 copy.45
  1281.8 11.5 convolution_convert_fusion
  1293.6 18.8 %shard_map.183 = (bf16[3,1024,512]{2,1,0:T(8,128)(2,1)}, f32[3,512]{1,0:T(4,128)}) custom-call(s32[1,1024]{1,0:T(1,128)} %bitcast.110, bf16[3,1024,512]{2,1,0:T(8,128)(2,1)} %bitcast.126, bf16[3,1024,512]{2,1,0:T(8,128)(2,1)} %bitcast.127, bf16[3,1024,512]{2,1,0:T(8,128)(2,1)} %bitcast.128, bf16[1024,512]{1,0:T(8,128)(2,1)} %get-tuple-element.60.source.attended, ...), custom_call_target="tpu_custom_call" | custom-call | flops 10737418240 | bytes 8388608 | tf_op jit(solution)/shard_map/pallas_call | solution.py:839
  1312.3 3.2 copy.43
  1315.6 11.2 convolution_convert_fusion.1
  1327.1 18.3 %bitcast_convert_fusion.1 = bf16[2048,2816]{1,0:T(8,128)(2,1)} fusion(bf16[4,256,2048]{2,1,0:T(8,128)(2,1)} %get-tuple-element.101, bf16[4,256,2816]{2,1,0:T(8,128)(2,1)} %get-tuple-element.102), kind=kOutput, calls=%fused_computation.1 | convolution fusion | flops 11816927232 | bytes 21495808 | tf_op jit(solution)/shard_map/dot_general | solution.py:29
  1345.7 18.2 %bitcast_convert_fusion = bf16[2048,2816]{1,0:T(8,128)(2,1)} fusion(bf16[4,256,2048]{2,1,0:T(8,128)(2,1)} %get-tuple-element.103, bf16[4,256,2816]{2,1,0:T(8,128)(2,1)} %get-tuple-element.104), kind=kOutput, calls=%fused_computation | convolution fusion | flops 11816927232 | bytes 21495808 | tf_op jit(solution)/shard_map/dot_general | solution.py:29
  1364.8 82.3 %shard_map.184 = (f32[256,2048]{1,0:T(8,128)}, bf16[256,2048]{1,0:T(8,128)(2,1)}, f32[1,2048]{1,0:T(1,128)}, f32[1,2048]{1,0:T(1,128)}) custom-call(bf16[3,1024,512]{2,1,0:T(8,128)(2,1)} %get-tuple-element.84.source, bf16[2048,1536]{1,0:T(8,128)(2,1)} %all-gather.13.cloned.1.call-done.weight, f32[256,2048]{1,0:T(8,128)} %get-tuple-element.85.grad, ...), custom_call_target="tpu_custom_call" | custom-call | flops 6442450944 | bytes 16777216 | tf_op jit(solution)/shard_map/pallas_call | solution.py:697
  1449.6 1.9 collective-permute-start.1
  1451.5 7.1 collective-permute-done.1
  1459.7 7.6 collective-permute-done.2
  1467.3 1.6 collective-permute-start.3
  1469.0 3.4 collective-permute-done.3
  1472.4 5.0 collective-permute-start.4
  1478.5 2.2 collective-permute-done.4
  1482.1 2.1 maximum_convert_fusion.3
  1484.2 3.1 maximum_convert_fusion.2
  1488.0 2.3 copy.46
  1490.3 63.1 %reduce-scatter.9.cloned.1.call-done = bf16[256,1536]{1,0:T(8,128)(2,1)} async-done(((bf16[2048,1536]{1,0:T(8,128)(2,1)}), bf16[256,1536]{1,0:T(8,128)(2,1)}) %reduce-scatter.9.cloned.1.call-update) | async-done | bytes 786448 | tf_op jit(solution)/shard_map/reduce_scatter | solution.py:983
  1553.4 2.3 copy.44
  1557.3 2.4 copy.51
  1559.6 83.9 %reduce-scatter.17.cloned.1.call-done = bf16[256,2816]{1,0:T(8,128)(2,1)} async-done(((bf16[2048,2816]{1,0:T(8,128)(2,1)}), bf16[256,2816]{1,0:T(8,128)(2,1)}) %reduce-scatter.17.cloned.1.call-update) | async-done | bytes 1441808 | tf_op jit(solution)/shard_map/reduce_scatter | solution.py:974
  1643.6 3.2 stack_reshape.18
  1646.8 86.9 %reduce-scatter.19.cloned.1.call-done = bf16[256,2816]{1,0:T(8,128)(2,1)} async-done(((bf16[2048,2816]{1,0:T(8,128)(2,1)}), bf16[256,2816]{1,0:T(8,128)(2,1)}) %reduce-scatter.19.cloned.1.call-update) | async-done | bytes 1441808 | tf_op jit(solution)/shard_map/reduce_scatter | solution.py:974
  1733.7 3.2 stack_reshape.19
  1737.0 6.2 maximum_convert_fusion
  (152 shorter events, 35.2 us)
Async XLA Ops:
  7.2 3.1 copy-start.9
  7.2 51.4 %all-gather.13.cloned.1.call-start = ((), (), s32[]{:S(2)}) async-start(), calls=%async_computation.8 | async-start | bytes 7077888 | tf_op jit(solution)/shard_map/all_gather | solution.py:917
  9.0 2.2 copy-start.7
  10.2 150.1 %all-gather.21.cloned.1.call-start = ((), (), s32[]{:S(2)}) async-start(), calls=%async_computation.20 | async-start | bytes 2359296 | tf_op jit(solution)/shard_map/all_gather | solution.py:920
  11.1 227.2 %all-gather.23.cloned.1.call-start = ((), (), s32[]{:S(2)}) async-start(), calls=%async_computation.21 | async-start | bytes 6488064 | tf_op jit(solution)/shard_map/all_gather | solution.py:924
  12.4 225.9 %all-gather.15.cloned.1.call-start = ((), (), s32[]{:S(2)}) async-start(), calls=%async_computation.9 | async-start | bytes 12976128 | tf_op jit(solution)/shard_map/all_gather | solution.py:921
  17.5 371.0 %all-gather.17.cloned.1.call-start = ((), (), s32[]{:S(2)}) async-start(), calls=%async_computation.10 | async-start | bytes 7077888 | tf_op jit(solution)/shard_map/all_gather | solution.py:917
  19.0 2.9 copy-start.21
  19.0 461.2 %all-gather.25.cloned.1.call-start = ((), (), s32[]{:S(2)}) async-start(), calls=%async_computation.22 | async-start | bytes 2359296 | tf_op jit(solution)/shard_map/all_gather | solution.py:920
  19.6 532.9 %all-gather.27.cloned.1.call-start = ((), (), s32[]{:S(2)}) async-start(), calls=%async_computation.23 | async-start | bytes 6488064 | tf_op jit(solution)/shard_map/all_gather | solution.py:924
  20.4 532.1 %all-gather.19.cloned.1.call-start = ((), (), s32[]{:S(2)}) async-start(), calls=%async_computation.11 | async-start | bytes 12976128 | tf_op jit(solution)/shard_map/all_gather | solution.py:921
  21.7 1460.4 %reduce-scatter.15.cloned.1.call-start = ((), (), s32[]{:S(2)}) async-start(), calls=%async_computation.15 | async-start | bytes 2359296 | tf_op jit(solution)/shard_map/reduce_scatter | solution.py:977
  22.7 2.7 copy-start.2
  24.1 1.2 copy-start.3
  24.1 2.5 copy-start
  25.8 4.0 copy-start.4
  25.8 2.4 copy-start.8
  26.6 3.1 copy-start.10
  28.2 3.5 copy-start.11
  28.2 4.1 copy-start.12
  853.8 66.0 %copy-start.23 = (bf16[1024,512]{1,0:T(8,128)(2,1)S(1)}, bf16[1024,512]{1,0:T(8,128)(2,1)}, u32[]{:S(2)}) copy-start(bf16[1024,512]{1,0:T(8,128)(2,1)} %get-tuple-element.65.source.attended) | copy-start | bytes 3145732
  925.7 556.3 %reduce-scatter.13.cloned.1.call-start = ((), (), s32[]{:S(2)}) async-start(), calls=%async_computation.14 | async-start | bytes 2359296 | tf_op jit(solution)/shard_map/reduce_scatter | solution.py:977
  1181.6 65.9 %copy-start.22 = (bf16[1024,512]{1,0:T(8,128)(2,1)S(1)}, bf16[1024,512]{1,0:T(8,128)(2,1)}, u32[]{:S(2)}) copy-start(bf16[1024,512]{1,0:T(8,128)(2,1)} %get-tuple-element.60.source.attended) | copy-start | bytes 3145732
  1253.4 230.8 %reduce-scatter.21.cloned.1.call-start = ((), (), s32[]{:S(2)}) async-start(), calls=%async_computation.18 | async-start | bytes 6488064 | tf_op jit(solution)/shard_map/reduce_scatter | solution.py:970
  1264.3 1.9 copy-start.24
  1264.4 219.8 %reduce-scatter.23.cloned.1.call-start = ((), (), s32[]{:S(2)}) async-start(), calls=%async_computation.19 | async-start | bytes 6488064 | tf_op jit(solution)/shard_map/reduce_scatter | solution.py:970
  1276.9 1.9 copy-start.1
  1276.9 211.1 %reduce-scatter.11.cloned.1.call-start = ((), (), s32[]{:S(2)}) async-start(), calls=%async_computation.13 | async-start | bytes 7077888 | tf_op jit(solution)/shard_map/reduce_scatter | solution.py:983
  1293.3 260.1 %reduce-scatter.9.cloned.1.call-start = ((), (), s32[]{:S(2)}) async-start(), calls=%async_computation.12 | async-start | bytes 7077888 | tf_op jit(solution)/shard_map/reduce_scatter | solution.py:983
  1326.8 316.7 %reduce-scatter.17.cloned.1.call-start = ((), (), s32[]{:S(2)}) async-start(), calls=%async_computation.16 | async-start | bytes 12976128 | tf_op jit(solution)/shard_map/reduce_scatter | solution.py:974
  1345.4 388.3 %reduce-scatter.19.cloned.1.call-start = ((), (), s32[]{:S(2)}) async-start(), calls=%async_computation.17 | async-start | bytes 12976128 | tf_op jit(solution)/shard_map/reduce_scatter | solution.py:974
  1364.0 0.7 copy-start.19
  1364.0 0.7 copy-start.13
  1364.0 0.7 copy-start.14
  1364.0 0.7 copy-start.17
  1364.0 0.7 copy-start.18
  1364.0 0.8 copy-start.20
  1364.8 82.3 %copy-start.15 = (f32[1,2048]{1,0:T(1,128)S(1)}, f32[1,2048]{1,0:T(1,128)}, u32[]{:S(2)}) copy-start(f32[1,2048]{1,0:T(1,128)} %get-tuple-element.88) | copy-start | bytes 24580
  1364.8 82.3 %copy-start.16 = (f32[1,2048]{1,0:T(1,128)S(1)}, f32[1,2048]{1,0:T(1,128)}, u32[]{:S(2)}) copy-start(f32[1,2048]{1,0:T(1,128)} %get-tuple-element.90) | copy-start | bytes 24580
  1447.1 30.2 %copy-start.5 = (f32[256,2048]{1,0:T(8,128)S(1)}, f32[256,2048]{1,0:T(8,128)}, u32[]{:S(2)}) copy-start(f32[256,2048]{1,0:T(8,128)} %get-tuple-element.69) | copy-start | bytes 6291460
  1448.1 1.4 collective-permute-start
  1449.6 9.0 collective-permute-start.1
  1458.6 8.7 collective-permute-start.2
  1467.3 5.0 collective-permute-start.3
  1472.4 8.3 collective-permute-start.4
  1737.0 6.2 copy-start.6
Sparse Core Ops, SparseCore 0:
  10.3 48.2 all-gather.12
  60.5 28.1 all-gather.20
  90.6 44.4 all-gather.22
  137.4 67.5 all-gather.14
  206.8 45.5 all-gather.16
  254.1 28.1 all-gather.24
  284.2 44.3 all-gather.26
  331.0 67.6 all-gather.18
  925.9 40.6 reduce-scatter.14
  1253.5 40.6 reduce-scatter.12
  1297.6 59.0 reduce-scatter.20
  1361.0 59.0 reduce-scatter.22
  1423.4 64.5 reduce-scatter.10
  1491.6 61.7 reduce-scatter.8
  1556.8 86.7 reduce-scatter.16
  1646.9 86.7 reduce-scatter.18

commit v2 on v0

--- a/solution.py
+++ b/solution.py
@@ -1,20 +1,1301 @@
+import functools
 import math
 
 import jax
 import jax.numpy as jnp
 from jax import lax
+from jax.experimental import pallas as pl
+from jax.experimental.pallas import tpu as pltpu
 from jax.sharding import PartitionSpec as P
 
 HD = 64
 ROT = 16
 LAYERS = 2
-
+PAIR = 2 * HD
+MESH = pl.DeviceIdType.MESH
+F32 = jnp.float32
+BF16 = jnp.bfloat16
+VMEM_LIMIT = 62 * 2**20
 
 norm_eps = 1e-05
 theta_log = math.log(10000.0)
 masked_score = -1e30
-contract_rows = (((0,), (0,)), ((), ()))
-contract_cols = (((1,), (1,)), ((), ()))
+rows_rows = (((0,), (0,)), ((), ()))
+cols_cols = (((1,), (1,)), ((), ()))
+rows_cols = (((1,), (0,)), ((), ()))
+
+
+def matmul(left, right, dims=rows_cols):
+    return lax.dot_general(left, right, dims, preferred_element_type=F32)
+
+
+def line_barrier(place, count):
+    barrier = pltpu.get_barrier_semaphore()
+
+    @pl.when(place > 0)
+    def _():
+        pl.semaphore_signal(barrier, inc=1, device_id={"tensor": place - 1}, device_id_type=MESH)
+
+    @pl.when(place < count - 1)
+    def _():
+        pl.semaphore_signal(barrier, inc=1, device_id={"tensor": place + 1}, device_id_type=MESH)
+
+    middle = (place > 0) & (place < count - 1)
+
+    @pl.when(middle)
+    def _():
+        pl.semaphore_wait(barrier, 2)
+
+    @pl.when(jnp.logical_not(middle))
+    def _():
+        pl.semaphore_wait(barrier, 1)
+
+
+def each_tile(width, tile, run):
+    def one(number, carry):
+        run(pl.multiple_of(number * tile, tile), tile)
+        return carry
+
+    lax.fori_loop(0, width // tile, one, 0)
+    if width % tile:
+        run(width // tile * tile, width % tile)
+
+
+class Line:
+    def __init__(self, count, pieces, shares, sending, arrived, sum_send, sum_recv, held, send_sem, recv_sem):
+        self.count, self.pieces = count, pieces
+        self.shares, self.sending, self.arrived = shares, sending, arrived
+        self.sum_send, self.sum_recv = sum_send, sum_recv
+        self.held, self.send_sem, self.recv_sem = held, send_sem, recv_sem
+        self.place = lax.axis_index("tensor")
+        self.rows = (held if held is not None else sending).shape[1] // pieces
+
+    def at(self, piece):
+        return pl.ds(pl.multiple_of(piece * self.rows, self.rows), self.rows)
+
+    def sum_hop(self, piece, owner):
+        right = owner > self.place
+        target = jnp.where(right, self.place + 1, self.place - 1)
+        slot = jnp.where(right | (owner != target), owner, self.count)
+        return pltpu.make_async_remote_copy(
+            src_ref=self.sending.at[owner, self.at(piece)],
+            dst_ref=self.arrived.at[slot, self.at(piece)],
+            send_sem=self.sum_send.at[owner, piece],
+            recv_sem=self.sum_recv.at[slot, piece],
+            device_id={"tensor": target},
+            device_id_type=MESH,
+        )
+
+    def sum_landed(self, piece, slot):
+        return pltpu.make_async_remote_copy(
+            src_ref=self.sending.at[0, self.at(piece)],
+            dst_ref=self.arrived.at[slot, self.at(piece)],
+            send_sem=self.sum_send.at[0, piece],
+            recv_sem=self.sum_recv.at[slot, piece],
+            device_id={"tensor": self.place},
+            device_id_type=MESH,
+        )
+
+    def row_hop(self, piece, block, right):
+        return pltpu.make_async_remote_copy(
+            src_ref=self.held.at[block, self.at(piece)],
+            dst_ref=self.held.at[block, self.at(piece)],
+            send_sem=self.send_sem.at[jnp.where(right, 0, 1), block, piece],
+            recv_sem=self.recv_sem.at[block, piece],
+            device_id={"tensor": jnp.where(right, self.place + 1, self.place - 1)},
+            device_id_type=MESH,
+        )
+
+    def sides(self, away, run):
+        def one(side, carry):
+            block = jnp.where(side == 0, self.place + away, self.place - away)
+
+            @pl.when((block >= 0) & (block < self.count))
+            def _():
+                run(block, side == 0)
+
+            return carry
+
+        lax.fori_loop(0, 2, one, 0)
+
+    def chunks(self, run):
+        chunk = min(16, self.rows)
+
+        def one(number, carry):
+            run(pl.multiple_of(number * chunk, chunk), chunk)
+            return carry
+
+        lax.fori_loop(0, self.rows // chunk, one, 0)
+
+    def pass_on(self, piece, owner, right):
+        side = piece % 2
+        first = pl.multiple_of(piece * self.rows, self.rows)
+        onward = jnp.where(right, self.place > 0, self.place < self.count - 1)
+
+        @pl.when(onward)
+        def _():
+            self.sum_landed(piece, owner).wait_recv()
+
+            def rows(start, size):
+                at = pl.ds(pl.multiple_of(first + start, size), size)
+                self.sending[owner, at, :] = (
+                    self.shares[side, owner, pl.ds(start, size), :]
+                    + self.arrived[owner, at, :].astype(F32)
+                ).astype(BF16)
+
+            self.chunks(rows)
+
+        @pl.when(jnp.logical_not(onward))
+        def _():
+            def rows(start, size):
+                at = pl.ds(pl.multiple_of(first + start, size), size)
+                self.sending[owner, at, :] = self.shares[side, owner, pl.ds(start, size), :].astype(BF16)
+
+            self.chunks(rows)
+
+        self.sum_hop(piece, owner).start()
+
+    def collect(self, piece):
+        side = piece % 2
+        first = pl.multiple_of(piece * self.rows, self.rows)
+
+        def add(slot):
+            self.sum_landed(piece, slot).wait_recv()
+
+            def rows(start, size):
+                at = pl.ds(pl.multiple_of(first + start, size), size)
+                mine = pl.ds(start, size)
+                self.shares[side, self.place, mine, :] = self.shares[
+                    side, self.place, mine, :
+                ] + self.arrived[slot, at, :].astype(F32)
+
+            self.chunks(rows)
+
+        @pl.when(self.place > 0)
+        def _():
+            add(self.place)
+
+        @pl.when(self.place < self.count - 1)
+        def _():
+            add(self.count)
+
+    def own_rows(self, piece, run):
+        side = piece % 2
+        first = pl.multiple_of(piece * self.rows, self.rows)
+
+        def rows(start, size):
+            at = pl.ds(pl.multiple_of(first + start, size), size)
+            run(at, self.shares[side, self.place, pl.ds(start, size), :])
+
+        self.chunks(rows)
+
+    def run(self, term, finish, process):
+        count, pieces, place = self.count, self.pieces, self.place
+        scatter, gather = term is not None, process is not None
+        if scatter:
+            term(0)
+
+        def period(number, carry):
+            if scatter:
+
+                @pl.when(number < pieces)
+                def _():
+                    self.sides(count - 1, lambda owner, right: self.pass_on(number, owner, right))
+
+            @pl.when(number >= 1)
+            def _():
+                piece = number - 1
+                if scatter:
+                    self.collect(piece)
+                finish(piece)
+                if gather:
+
+                    @pl.when(place < count - 1)
+                    def _():
+                        self.row_hop(piece, place, True).start()
+
+                    @pl.when(place > 0)
+                    def _():
+                        self.row_hop(piece, place, False).start()
+
+            if scatter:
+
+                @pl.when(number + 1 < pieces)
+                def _():
+                    term(number + 1)
+
+            def slot(step, inner):
+                if scatter:
+
+                    @pl.when((number < pieces) & (step < count - 1))
+                    def _():
+                        self.sides(
+                            count - 1 - step,
+                            lambda owner, right: self.pass_on(number, owner, right),
+                        )
+
+                if gather:
+
+                    @pl.when(number >= 1)
+                    def _():
+                        def forward(block, right):
+                            self.row_hop(number - 1, block, True).wait_recv()
+                            onward = jnp.where(right, place > 0, place < count - 1)
+
+                            @pl.when(onward)
+                            def _():
+                                self.row_hop(number - 1, block, jnp.logical_not(right)).start()
+
+                        self.sides(step, forward)
+
+                    @pl.when((step == 1) & (number >= 2))
+                    def _():
+                        process(number - 2)
+
+                return inner
+
+            lax.fori_loop(1, count, slot, 0)
+            return carry
+
+        lax.fori_loop(0, pieces + 1, period, 0)
+        if gather:
+            process(pieces - 1)
+
+    def drain(self):
+        def piece_sends(piece, carry):
+            def owner_sends(owner, inner):
+                if self.sending is not None:
+
+                    @pl.when(owner != self.place)
+                    def _():
+                        self.sum_hop(piece, owner).wait_send()
+
+                if self.held is not None:
+
+                    @pl.when((owner <= self.place) & (self.place < self.count - 1))
+                    def _():
+                        self.row_hop(piece, owner, True).wait_send()
+
+                    @pl.when((owner >= self.place) & (self.place > 0))
+                    def _():
+                        self.row_hop(piece, owner, False).wait_send()
+
+                return inner
+
+            lax.fori_loop(0, self.count, owner_sends, 0)
+            return carry
+
+        lax.fori_loop(0, self.pieces, piece_sends, 0)
+
+
+def norm_rows(values):
+    average = jnp.mean(values, axis=-1, keepdims=True)
+    centred = values - average
+    variance = jnp.mean(centred * centred, axis=-1, keepdims=True)
+    inverse = lax.rsqrt(variance + norm_eps)
+    return centred * inverse, inverse
+
+
+def scatter_scratch(count, pieces, rows, width):
+    return [
+        pltpu.VMEM((2, count, rows // pieces, width), F32),
+        pltpu.VMEM((count, rows, width), BF16),
+        pltpu.VMEM((count + 1, rows, width), BF16),
+        pltpu.SemaphoreType.DMA((count, pieces)),
+        pltpu.SemaphoreType.DMA((count + 1, pieces)),
+    ]
+
+
+def gather_scratch(count, pieces, rows, width):
+    return [
+        pltpu.VMEM((count, rows, width), BF16),
+        pltpu.SemaphoreType.DMA((2, count, pieces)),
+        pltpu.SemaphoreType.DMA((count, pieces)),
+    ]
+
+
+vmem = pl.BlockSpec(memory_space=pltpu.VMEM)
+hbm = pl.BlockSpec(memory_space=pl.ANY)
+
+
+class Loads:
+    def __init__(self, pairs, sems):
+        self.copies = [
+            pltpu.make_async_copy(source, target, sems.at[number])
+            for number, (source, target) in enumerate(pairs)
+        ]
+        for copy in self.copies:
+            copy.start()
+
+    def wait(self, *numbers):
+        for number in numbers:
+            self.copies[number].wait()
+
+
+class Saves:
+    def __init__(self, pairs, sems, line):
+        self.pairs, self.sems, self.line = pairs, sems, line
+
+    def copy(self, number, piece):
+        source, target = self.pairs[number]
+        rows = self.line.at(piece)
+        where = (slice(None),) * (len(source.shape) - 2) + (rows,)
+        return pltpu.make_async_copy(
+            source.at[where], target.at[where], self.sems.at[number, piece]
+        )
+
+    def start(self, piece):
+        for number in range(len(self.pairs)):
+            self.copy(number, piece).start()
+
+    def wait(self):
+        for number in range(len(self.pairs)):
+            for piece in range(self.line.pieces):
+                self.copy(number, piece).wait()
+
+
+def flat_rows(ref, rows, columns=slice(None)):
+    values = ref[:, rows, columns]
+    return values.reshape(values.shape[0] * values.shape[1], values.shape[2])
+
+
+def put_rows(ref, rows, columns, values):
+    count = ref.shape[0]
+    ref[:, rows, columns] = values.reshape(count, values.shape[0] // count, values.shape[1])
+
+
+def line_call(body, out_shape, out_specs, in_specs, scratch, number, flops, moved):
+    return pl.pallas_call(
+        body,
+        out_shape=out_shape,
+        in_specs=in_specs,
+        out_specs=out_specs,
+        scratch_shapes=scratch,
+        compiler_params=pltpu.CompilerParams(
+            collective_id=number, has_side_effects=True, vmem_limit_bytes=VMEM_LIMIT
+        ),
+        cost_estimate=pl.CostEstimate(flops=flops, bytes_accessed=moved, transcendentals=0),
+    )
+
+
+def pieces_of(rows):
+    return 4 if rows % 64 == 0 else 1
+
+
+def query_key_value(line, weight, bias, tables, mixed):
+    cos, sin_up, sin_down = tables
+    width = mixed.shape[3]
+
+    def process(piece):
+        rows = line.at(piece)
+
+        def columns(kind):
+            def run(start, size):
+                source = pl.ds(pl.multiple_of(kind * width + start, 128), size)
+                result = matmul(flat_rows(line.held, rows), weight[:, source]) + bias[:, source]
+                if kind < 2:
+                    result = (
+                        result * flat_rows(cos, rows, slice(0, size))
+                        + pltpu.roll(result, size - ROT // 2, 1) * flat_rows(sin_up, rows, slice(0, size))
+                        + pltpu.roll(result, ROT // 2, 1) * flat_rows(sin_down, rows, slice(0, size))
+                    )
+                if kind == 0:
+                    result = result * (1.0 / math.sqrt(HD))
+                put_rows(mixed.at[kind], rows, pl.ds(start, size), result.astype(BF16))
+
+            return run
+
+        for kind in range(3):
+            each_tile(width, min(256, width), columns(kind))
+
+    return process
+
+
+def gate_and_up(line, weight, act, slope, silu):
+    width = act.shape[2]
+
+    def process(piece):
+        rows = line.at(piece)
+
+        def run(start, size):
+            at = pl.ds(start, size)
+            own = flat_rows(line.held, rows)
+            gate = matmul(own, weight[:, at])
+            up = matmul(own, weight[:, pl.ds(pl.multiple_of(width + start, 128), size)])
+            sigmoid = jax.nn.sigmoid(gate)
+            soft = gate * sigmoid
+            put_rows(act, rows, at, (soft * up).astype(BF16))
+            put_rows(silu, rows, at, soft.astype(BF16))
+            put_rows(slope, rows, at, (up * sigmoid * (1.0 + gate * (1.0 - sigmoid))).astype(BF16))
+
+        each_tile(width, 256, run)
+
+    return process
+
+
+def grad_gate_and_up(line, weight, slope, silu, wide):
+    width = slope.shape[2]
+
+    def process(piece):
+        rows = line.at(piece)
+
+        def run(start, size):
+            at = pl.ds(start, size)
+            grad_act = matmul(flat_rows(line.held, rows), weight[at, :], cols_cols)
+            put_rows(wide, rows, at, (grad_act * flat_rows(slope, rows, at).astype(F32)).astype(BF16))
+            put_rows(
+                wide,
+                rows,
+                pl.ds(pl.multiple_of(width + start, 128), size),
+                (grad_act * flat_rows(silu, rows, at).astype(F32)).astype(BF16),
+            )
+
+        each_tile(width, 256, run)
+
+    return process
+
+
+def through_transposed(line, weight, result):
+    def process(piece):
+        rows = line.at(piece)
+
+        def run(start, size):
+            at = pl.ds(start, size)
+            put_rows(
+                result, rows, at, matmul(flat_rows(line.held, rows), weight[at, :], cols_cols).astype(BF16)
+            )
+
+        each_tile(result.shape[2], 256, run)
+
+    return process
+
+
+def share_of(line, source, weight):
+    def term(piece):
+        rows = line.at(piece)
+
+        def run(start, size):
+            at = pl.ds(start, size)
+            put_rows(
+                line.shares.at[piece % 2],
+                slice(None),
+                at,
+                matmul(flat_rows(source, rows), weight[:, at]),
+            )
+
+        each_tile(line.shares.shape[3], 256, run)
+
+    return term
+
+
+def share_transposed(line, sources, weight):
+    width = sources[0].shape[2]
+
+    def term(piece):
+        rows = line.at(piece)
+
+        def run(start, size):
+            at = pl.ds(start, size)
+            result = matmul(flat_rows(sources[0], rows), weight[at, :width], cols_cols)
+            for number in range(1, len(sources)):
+                result = result + matmul(
+                    flat_rows(sources[number], rows),
+                    weight[at, number * width : (number + 1) * width],
+                    cols_cols,
+                )
+            put_rows(line.shares.at[piece % 2], slice(None), at, result)
+
+        each_tile(line.shares.shape[3], 256, run)
+
+    return term
+
+
+def add_and_norm(line, before, gain, shift, after):
+    def finish(piece):
+        def rows(at, total):
+            hidden = before[at, :] + total
+            after[at, :] = hidden
+            scaled, _ = norm_rows(hidden)
+            line.held[line.place, at, :] = (scaled * gain[...] + shift[...]).astype(BF16)
+
+        line.own_rows(piece, rows)
+
+    return finish
+
+
+def norm_backward(line, grad, hidden, gain, out, gain_sum, shift_sum):
+    gain_sum[...] = jnp.zeros_like(gain_sum)
+    shift_sum[...] = jnp.zeros_like(shift_sum)
+
+    def finish(piece):
+        def rows(at, grad_normed):
+            scaled, inverse = norm_rows(hidden[at, :])
+            weighted = grad_normed * gain[...]
+            first = jnp.mean(weighted, axis=-1, keepdims=True)
+            second = jnp.mean(weighted * scaled, axis=-1, keepdims=True)
+            result = grad[at, :] + inverse * (weighted - first - scaled * second)
+            out[at, :] = result
+            if line.held is not None:
+                line.held[line.place, at, :] = result.astype(BF16)
+            gain_sum[...] += jnp.sum(grad_normed * scaled, axis=0, keepdims=True)
+            shift_sum[...] += jnp.sum(grad_normed, axis=0, keepdims=True)
+
+        line.own_rows(piece, rows)
+
+    return finish
+
+
+def split(refs, *sizes):
+    parts, start = [], 0
+    for size in sizes:
+        parts.append(refs[start : start + size])
+        start += size
+    return parts
+
+
+def first_kernel(count, pieces, *refs):
+    (own, weight, bias, *tables), (rows_out, mixed_out), gather, rest = split(refs, 6, 2, 3, 4)
+    weight_held, mixed, load_sem, save_sem = rest
+    line = Line(count, pieces, None, None, None, None, None, *gather)
+    loads = Loads([(weight, weight_held)], load_sem)
+    line_barrier(line.place, count)
+    saves = Saves([(line.held, rows_out), (mixed, mixed_out)], save_sem, line)
+    compute = query_key_value(line, weight_held, bias, tables, mixed)
+
+    def finish(piece):
+        rows = line.at(piece)
+        line.held[line.place, rows, :] = own[rows, :]
+
+    def process(piece):
+        @pl.when(piece == 0)
+        def _():
+            loads.wait(0)
+
+        compute(piece)
+        saves.start(piece)
+
+    line.run(None, finish, process)
+    line.drain()
+    saves.wait()
+
+
+def first(count, own, weight, bias, tables, width):
+    rows, depth = own.shape
+    pieces = pieces_of(rows)
+    return line_call(
+        functools.partial(first_kernel, count, pieces),
+        (
+            jax.ShapeDtypeStruct((count, rows, depth), BF16),
+            jax.ShapeDtypeStruct((3, count, rows, width), BF16),
+        ),
+        (hbm, hbm),
+        [vmem, hbm, vmem, vmem, vmem, vmem],
+        gather_scratch(count, pieces, rows, depth)
+        + [
+            pltpu.VMEM(weight.shape, BF16),
+            pltpu.VMEM((3, count, rows, width), BF16),
+            pltpu.SemaphoreType.DMA((1,)),
+            pltpu.SemaphoreType.DMA((2, pieces)),
+        ],
+        0,
+        2 * count * rows * weight.size,
+        weight.size * 2 + own.size * 2 * count * 4,
+    )(own, weight, bias, *tables)
+
+
+def middle_kernel(count, pieces, *refs):
+    ins, outs, scatter, gather, rest = split(refs, 6, 5, 5, 3, 8)
+    source, w_out, before, gain, shift, w_up = ins
+    after, rows_out, act_out, slope_out, silu_out = outs
+    source_held, out_held, up_held, act, slope, silu, load_sem, save_sem = rest
+    line = Line(count, pieces, *scatter, *gather)
+    loads = Loads([(source, source_held), (w_out, out_held), (w_up, up_held)], load_sem)
+    line_barrier(line.place, count)
+    saves = Saves(
+        [(line.held, rows_out), (act, act_out), (slope, slope_out), (silu, silu_out)], save_sem, line
+    )
+    compute = gate_and_up(line, up_held, act, slope, silu)
+
+    def process(piece):
+        @pl.when(piece == 0)
+        def _():
+            loads.wait(2)
+
+        compute(piece)
+        saves.start(piece)
+
+    loads.wait(0, 1)
+    line.run(
+        share_of(line, source_held, out_held), add_and_norm(line, before, gain, shift, after), process
+    )
+    line.drain()
+    saves.wait()
+
+
+def middle(count, source, w_out, before, gain, shift, w_up):
+    rows, depth = before.shape
+    pieces = pieces_of(rows)
+    width = w_up.shape[1] // 2
+    wide = jax.ShapeDtypeStruct((count, rows, width), BF16)
+    return line_call(
+        functools.partial(middle_kernel, count, pieces),
+        (
+            jax.ShapeDtypeStruct((rows, depth), F32),
+            jax.ShapeDtypeStruct((count, rows, depth), BF16),
+            wide,
+            wide,
+            wide,
+        ),
+        (vmem, hbm, hbm, hbm, hbm),
+        [hbm, hbm, vmem, vmem, vmem, hbm],
+        scatter_scratch(count, pieces, rows, depth)
+        + gather_scratch(count, pieces, rows, depth)
+        + [
+            pltpu.VMEM(source.shape, BF16),
+            pltpu.VMEM(w_out.shape, BF16),
+            pltpu.VMEM(w_up.shape, BF16),
+            pltpu.VMEM(wide.shape, BF16),
+            pltpu.VMEM(wide.shape, BF16),
+            pltpu.VMEM(wide.shape, BF16),
+            pltpu.SemaphoreType.DMA((3,)),
+            pltpu.SemaphoreType.DMA((4, pieces)),
+        ],
+        1,
+        2 * count * rows * (w_out.size + w_up.size),
+        (w_out.size + w_up.size) * 2 + before.size * 60,
+    )(source, w_out, before, gain, shift, w_up)
+
+
+def between_kernel(count, pieces, *refs):
+    ins, outs, scatter, gather, rest = split(refs, 10, 3, 5, 3, 6)
+    source, w_down, before, gain, shift, weight, bias, *tables = ins
+    after, rows_out, mixed_out = outs
+    source_held, down_held, weight_held, mixed, load_sem, save_sem = rest
+    line = Line(count, pieces, *scatter, *gather)
+    loads = Loads([(source, source_held), (w_down, down_held), (weight, weight_held)], load_sem)
+    line_barrier(line.place, count)
+    saves = Saves([(line.held, rows_out), (mixed, mixed_out)], save_sem, line)
+    compute = query_key_value(line, weight_held, bias, tables, mixed)
+
+    def process(piece):
+        @pl.when(piece == 0)
+        def _():
+            loads.wait(2)
+
+        compute(piece)
+        saves.start(piece)
+
+    loads.wait(0, 1)
+    line.run(
+        share_of(line, source_held, down_held), add_and_norm(line, before, gain, shift, after), process
+    )
+    line.drain()
+    saves.wait()
+
+
+def between(count, source, w_down, before, gain, shift, weight, bias, tables):
+    rows, depth = before.shape
+    pieces = pieces_of(rows)
+    mixed = (3, count, rows, weight.shape[1] // 3)
+    return line_call(
+        functools.partial(between_kernel, count, pieces),
+        (
+            jax.ShapeDtypeStruct((rows, depth), F32),
+            jax.ShapeDtypeStruct((count, rows, depth), BF16),
+            jax.ShapeDtypeStruct(mixed, BF16),
+        ),
+        (vmem, hbm, hbm),
+        [hbm, hbm, vmem, vmem, vmem, hbm, vmem, vmem, vmem, vmem],
+        scatter_scratch(count, pieces, rows, depth)
+        + gather_scratch(count, pieces, rows, depth)
+        + [
+            pltpu.VMEM(source.shape, BF16),
+            pltpu.VMEM(w_down.shape, BF16),
+            pltpu.VMEM(weight.shape, BF16),
+            pltpu.VMEM(mixed, BF16),
+            pltpu.SemaphoreType.DMA((3,)),
+            pltpu.SemaphoreType.DMA((2, pieces)),
+        ],
+        2,
+        2 * count * rows * (w_down.size + weight.size),
+        (w_down.size + weight.size) * 2 + before.size * 60,
+    )(source, w_down, before, gain, shift, weight, bias, *tables)
+
+
+def turn_kernel(count, pieces, *refs):
+    ins, outs, scatter, gather, rest = split(refs, 6, 3, 5, 3, 7)
+    source, w_down, before, own, slope_in, silu_in = ins
+    after, rows_out, wide_out = outs
+    source_held, down_held, slope, silu, wide, load_sem, save_sem = rest
+    line = Line(count, pieces, *scatter, *gather)
+    loads = Loads(
+        [(source, source_held), (w_down, down_held), (slope_in, slope), (silu_in, silu)], load_sem
+    )
+    line_barrier(line.place, count)
+    saves = Saves([(line.held, rows_out), (wide, wide_out)], save_sem, line)
+    compute = grad_gate_and_up(line, down_held, slope, silu, wide)
+
+    def finish(piece):
+        def rows(at, total):
+            after[at, :] = (before[at, :] + total).astype(BF16)
+            line.held[line.place, at, :] = own[at, :]
+
+        line.own_rows(piece, rows)
+
+    def process(piece):
+        @pl.when(piece == 0)
+        def _():
+            loads.wait(2, 3)
+
+        compute(piece)
+        saves.start(piece)
+
+    loads.wait(0, 1)
+    line.run(share_of(line, source_held, down_held), finish, process)
+    line.drain()
+    saves.wait()
+
+
+def turn(count, source, w_down, before, own, slope, silu):
+    rows, depth = before.shape
+    pieces = pieces_of(rows)
+    width = w_down.shape[0]
+    return line_call(
+        functools.partial(turn_kernel, count, pieces),
+        (
+            jax.ShapeDtypeStruct((rows, depth), BF16),
+            jax.ShapeDtypeStruct((count, rows, depth), BF16),
+            jax.ShapeDtypeStruct((count, rows, 2 * width), BF16),
+        ),
+        (vmem, hbm, hbm),
+        [hbm, hbm, vmem, vmem, hbm, hbm],
+        scatter_scratch(count, pieces, rows, depth)
+        + gather_scratch(count, pieces, rows, depth)
+        + [
+            pltpu.VMEM(source.shape, BF16),
+            pltpu.VMEM(w_down.shape, BF16),
+            pltpu.VMEM(slope.shape, BF16),
+            pltpu.VMEM(silu.shape, BF16),
+            pltpu.VMEM((count, rows, 2 * width), BF16),
+            pltpu.SemaphoreType.DMA((4,)),
+            pltpu.SemaphoreType.DMA((2, pieces)),
+        ],
+        3,
+        4 * count * rows * w_down.size,
+        w_down.size * 2 + before.size * 60,
+    )(source, w_down, before, own, slope, silu)
+
+
+def middle_back_kernel(count, pieces, *refs):
+    ins, outs, scatter, gather, rest = split(refs, 6, 5, 5, 3, 6)
+    source, w_up, grad, hidden, gain, w_out = ins
+    out, gain_sum, shift_sum, rows_out, result_out = outs
+    source_held, up_held, out_held, result, load_sem, save_sem = rest
+    line = Line(count, pieces, *scatter, *gather)
+    loads = Loads([(source, source_held), (w_up, up_held), (w_out, out_held)], load_sem)
+    line_barrier(line.place, count)
+    saves = Saves([(line.held, rows_out), (result, result_out)], save_sem, line)
+    compute = through_transposed(line, out_held, result)
+
+    def process(piece):
+        @pl.when(piece == 0)
+        def _():
+            loads.wait(2)
+
+        compute(piece)
+        saves.start(piece)
+
+    loads.wait(0, 1)
+    line.run(
+        share_transposed(line, [source_held], up_held),
+        norm_backward(line, grad, hidden, gain, out, gain_sum, shift_sum),
+        process,
+    )
+    line.drain()
+    saves.wait()
+
+
+def middle_back(count, source, w_up, grad, hidden, gain, w_out):
+    rows, depth = grad.shape
+    pieces = pieces_of(rows)
+    width = w_out.shape[0]
+    return line_call(
+        functools.partial(middle_back_kernel, count, pieces),
+        (
+            jax.ShapeDtypeStruct((rows, depth), F32),
+            jax.ShapeDtypeStruct((1, depth), F32),
+            jax.ShapeDtypeStruct((1, depth), F32),
+            jax.ShapeDtypeStruct((count, rows, depth), BF16),
+            jax.ShapeDtypeStruct((count, rows, width), BF16),
+        ),
+        (vmem, vmem, vmem, hbm, hbm),
+        [hbm, hbm, vmem, vmem, vmem, hbm],
+        scatter_scratch(count, pieces, rows, depth)
+        + gather_scratch(count, pieces, rows, depth)
+        + [
+            pltpu.VMEM(source.shape, BF16),
+            pltpu.VMEM(w_up.shape, BF16),
+            pltpu.VMEM(w_out.shape, BF16),
+            pltpu.VMEM((count, rows, width), BF16),
+            pltpu.SemaphoreType.DMA((3,)),
+            pltpu.SemaphoreType.DMA((2, pieces)),
+        ],
+        4,
+        2 * count * rows * (w_up.size + w_out.size),
+        (w_up.size + w_out.size) * 2 + grad.size * 60,
+    )(source, w_up, grad, hidden, gain, w_out)
+
+
+def between_back_kernel(count, pieces, *refs):
+    ins, outs, scatter, gather, rest = split(refs, 8, 5, 5, 3, 8)
+    source, weight, grad, hidden, gain, w_down, slope_in, silu_in = ins
+    out, gain_sum, shift_sum, rows_out, wide_out = outs
+    source_held, weight_held, down_held, slope, silu, wide, load_sem, save_sem = rest
+    line = Line(count, pieces, *scatter, *gather)
+    loads = Loads(
+        [
+            (source, source_held),
+            (weight, weight_held),
+            (w_down, down_held),
+            (slope_in, slope),
+            (silu_in, silu),
+        ],
+        load_sem,
+    )
+    line_barrier(line.place, count)
+    saves = Saves([(line.held, rows_out), (wide, wide_out)], save_sem, line)
+    compute = grad_gate_and_up(line, down_held, slope, silu, wide)
+
+    def process(piece):
+        @pl.when(piece == 0)
+        def _():
+            loads.wait(2, 3, 4)
+
+        compute(piece)
+        saves.start(piece)
+
+    loads.wait(0, 1)
+    line.run(
+        share_transposed(line, [source_held.at[kind] for kind in range(3)], weight_held),
+        norm_backward(line, grad, hidden, gain, out, gain_sum, shift_sum),
+        process,
+    )
+    line.drain()
+    saves.wait()
+
+
+def between_back(count, source, weight, grad, hidden, gain, w_down, slope, silu):
+    rows, depth = grad.shape
+    pieces = pieces_of(rows)
+    width = w_down.shape[0]
+    return line_call(
+        functools.partial(between_back_kernel, count, pieces),
+        (
+            jax.ShapeDtypeStruct((rows, depth), F32),
+            jax.ShapeDtypeStruct((1, depth), F32),
+            jax.ShapeDtypeStruct((1, depth), F32),
+            jax.ShapeDtypeStruct((count, rows, depth), BF16),
+            jax.ShapeDtypeStruct((count, rows, 2 * width), BF16),
+        ),
+        (vmem, vmem, vmem, hbm, hbm),
+        [hbm, hbm, vmem, vmem, vmem, hbm, hbm, hbm],
+        scatter_scratch(count, pieces, rows, depth)
+        + gather_scratch(count, pieces, rows, depth)
+        + [
+            pltpu.VMEM(source.shape, BF16),
+            pltpu.VMEM(weight.shape, BF16),
+            pltpu.VMEM(w_down.shape, BF16),
+            pltpu.VMEM(slope.shape, BF16),
+            pltpu.VMEM(silu.shape, BF16),
+            pltpu.VMEM((count, rows, 2 * width), BF16),
+            pltpu.SemaphoreType.DMA((5,)),
+            pltpu.SemaphoreType.DMA((2, pieces)),
+        ],
+        5,
+        2 * count * rows * (w_down.size + weight.size),
+        (w_down.size + weight.size) * 2 + grad.size * 60,
+    )(source, weight, grad, hidden, gain, w_down, slope, silu)
+
+
+def last_kernel(count, pieces, *refs):
+    ins, outs, scatter, rest = split(refs, 5, 3, 5, 3)
+    source, weight, grad, hidden, gain = ins
+    source_held, weight_held, load_sem = rest
+    line = Line(count, pieces, *scatter, None, None, None)
+    loads = Loads([(source, source_held), (weight, weight_held)], load_sem)
+    line_barrier(line.place, count)
+    loads.wait(0, 1)
+    line.run(
+        share_transposed(line, [source_held.at[kind] for kind in range(3)], weight_held),
+        norm_backward(line, grad, hidden, gain, *outs),
+        None,
+    )
+    line.drain()
+
+
+def last(count, source, weight, grad, hidden, gain):
+    rows, depth = grad.shape
+    pieces = pieces_of(rows)
+    return line_call(
+        functools.partial(last_kernel, count, pieces),
+        (
+            jax.ShapeDtypeStruct((rows, depth), F32),
+            jax.ShapeDtypeStruct((1, depth), F32),
+            jax.ShapeDtypeStruct((1, depth), F32),
+        ),
+        (vmem, vmem, vmem),
+        [hbm, hbm, vmem, vmem, vmem],
+        scatter_scratch(count, pieces, rows, depth)
+        + [
+            pltpu.VMEM(source.shape, BF16),
+            pltpu.VMEM(weight.shape, BF16),
+            pltpu.SemaphoreType.DMA((2,)),
+        ],
+        6,
+        2 * count * rows * weight.size,
+        weight.size * 2 + grad.size * 20,
+    )(source, weight, grad, hidden, gain)
+
+
+def usable(first, start, keys, queries):
+    key_index = lax.broadcasted_iota(jnp.int32, (keys, queries), 0)
+    query_index = start + lax.broadcasted_iota(jnp.int32, (keys, queries), 1)
+    return (key_index >= first) & (key_index <= query_index)
+
+
+def head_lanes(values, head):
+    lane = lax.broadcasted_iota(jnp.int32, values.shape, 1)
+    return jnp.where((lane // HD) == head, values, jnp.zeros_like(values))
+
+
+def attend_kernel(block, positions, queries, keys, values, attended, logsums):
+    length = keys.shape[0]
+    values_across = jnp.transpose(values[...])
+    for start in range(0, length, block):
+        seen = start + block
+        at = slice(start, seen)
+        own = queries[at, :]
+        index = start + lax.broadcasted_iota(jnp.int32, (1, block), 1)
+        allowed = usable(index - positions[:, at], start, seen, block)
+        halves = []
+        for head in range(2):
+            scores = matmul(keys[:seen, :], head_lanes(own, head), cols_cols)
+            scores = jnp.where(allowed, scores, masked_score)
+            highest = jnp.max(scores, axis=0, keepdims=True)
+            weights = jnp.exp(scores - highest)
+            sums = jnp.sum(weights, axis=0, keepdims=True)
+            result = matmul(values_across[:, :seen], weights.astype(BF16))
+            halves.append(result[head * HD : (head + 1) * HD, :] / sums)
+            logsums[head : head + 1, at] = highest + jnp.log(sums)
+        attended[at, :] = jnp.transpose(jnp.concatenate(halves, axis=0)).astype(BF16)
+
+
+def pair_spec(length, kind):
+    return pl.BlockSpec((None, length, PAIR), lambda pair: (kind, 0, pair))
+
+
+def attend(mixed, positions):
+    _, length, width = mixed.shape
+    pairs = width // PAIR
+    block = min(256, length)
+    return pl.pallas_call(
+        functools.partial(attend_kernel, block),
+        grid=(pairs,),
+        out_shape=(
+            jax.ShapeDtypeStruct((length, width), BF16),
+            jax.ShapeDtypeStruct((pairs, 2, length), F32),
+        ),
+        in_specs=[
+            pl.BlockSpec((1, length), lambda pair: (0, 0)),
+            pair_spec(length, 0),
+            pair_spec(length, 1),
+            pair_spec(length, 2),
+        ],
+        out_specs=(
+            pl.BlockSpec((length, PAIR), lambda pair: (0, pair)),
+            pl.BlockSpec((None, 2, length), lambda pair: (pair, 0, 0)),
+        ),
+        compiler_params=pltpu.CompilerParams(vmem_limit_bytes=VMEM_LIMIT),
+        cost_estimate=pl.CostEstimate(
+            flops=8 * length * length * width,
+            bytes_accessed=8 * length * width,
+            transcendentals=length * length * width // HD,
+        ),
+    )(positions, mixed, mixed, mixed)
+
+
+def unrotate(values, cos, sin_up, sin_down):
+    return (
+        values * cos
+        - pltpu.roll(values, PAIR - ROT // 2, 1) * sin_up
+        - pltpu.roll(values, ROT // 2, 1) * sin_down
+    )
+
+
+def attend_back_kernel(
+    block, positions, queries, keys, values, attended, grad_attended, logsums,
+    cos, sin_up, sin_down, grad_mixed, bias_sum, grad_keys, grad_values,
+):
+    length = keys.shape[0]
+    keys_across = jnp.transpose(keys[...])
+    grad_keys[...] = jnp.zeros_like(grad_keys)
+    grad_values[...] = jnp.zeros_like(grad_values)
+    bias_sum[...] = jnp.zeros_like(bias_sum)
+    for start in range(0, length, block):
+        seen = start + block
+        at = slice(start, seen)
+        own = queries[at, :]
+        grad_own = grad_attended[at, :]
+        inner = jnp.transpose(grad_own.astype(F32) * attended[at, :].astype(F32))
+        index = start + lax.broadcasted_iota(jnp.int32, (1, block), 1)
+        allowed = usable(index - positions[:, at], start, seen, block)
+        halves = []
+        for head in range(2):
+            own_head = head_lanes(own, head)
+            grad_head = head_lanes(grad_own, head)
+            scores = matmul(keys[:seen, :], own_head, cols_cols)
+            weights = jnp.where(allowed, jnp.exp(scores - logsums[head : head + 1, at]), 0.0)
+            grad_weights = matmul(values[:seen, :], grad_head, cols_cols)
+            row_inner = jnp.sum(inner[head * HD : (head + 1) * HD, :], axis=0, keepdims=True)
+            grad_scores = (weights * (grad_weights - row_inner)).astype(BF16)
+            grad_values[:seen, :] += matmul(weights.astype(BF16), grad_head)
+            grad_keys[:seen, :] += matmul(grad_scores, own_head)
+            result = matmul(keys_across[:, :seen], grad_scores)
+            halves.append(result[head * HD : (head + 1) * HD, :])
+        grad_own_queries = jnp.transpose(jnp.concatenate(halves, axis=0)) * (1.0 / math.sqrt(HD))
+        low = unrotate(grad_own_queries, cos[at, :], sin_up[at, :], sin_down[at, :]).astype(BF16)
+        grad_mixed[0, at, :] = low
+        bias_sum[0:1, :] += jnp.sum(low.astype(F32), axis=0, keepdims=True)
+    for start in range(0, length, block):
+        at = slice(start, start + block)
+        low = unrotate(grad_keys[at, :], cos[at, :], sin_up[at, :], sin_down[at, :]).astype(BF16)
+        grad_mixed[1, at, :] = low
+        bias_sum[1:2, :] += jnp.sum(low.astype(F32), axis=0, keepdims=True)
+        low = grad_values[at, :].astype(BF16)
+        grad_mixed[2, at, :] = low
+        bias_sum[2:3, :] += jnp.sum(low.astype(F32), axis=0, keepdims=True)
+
+
+def attend_backward(mixed, positions, attended, grad_attended, logsums, tables):
+    _, length, width = mixed.shape
+    pairs = width // PAIR
+    block = min(256, length)
+    across = pl.BlockSpec((length, PAIR), lambda pair: (0, pair))
+    table = pl.BlockSpec((length, PAIR), lambda pair: (0, 0))
+    return pl.pallas_call(
+        functools.partial(attend_back_kernel, block),
+        grid=(pairs,),
+        out_shape=(
+            jax.ShapeDtypeStruct((3, length, width), BF16),
+            jax.ShapeDtypeStruct((3, width), F32),
+        ),
+        in_specs=[
+            pl.BlockSpec((1, length), lambda pair: (0, 0)),
+            pair_spec(length, 0),
+            pair_spec(length, 1),
+            pair_spec(length, 2),
+            across,
+            across,
+            pl.BlockSpec((None, 2, length), lambda pair: (pair, 0, 0)),
+            table,
+            table,
+            table,
+        ],
+        out_specs=(
+            pl.BlockSpec((3, length, PAIR), lambda pair: (0, 0, pair)),
+            pl.BlockSpec((3, PAIR), lambda pair: (0, pair)),
+        ),
+        scratch_shapes=[pltpu.VMEM((length, PAIR), F32), pltpu.VMEM((length, PAIR), F32)],
+        compiler_params=pltpu.CompilerParams(vmem_limit_bytes=VMEM_LIMIT),
+        cost_estimate=pl.CostEstimate(
+            flops=20 * length * length * width,
+            bytes_accessed=16 * length * width,
+            transcendentals=length * length * width // HD,
+        ),
+    )(positions, mixed, mixed, mixed, attended, grad_attended, logsums, *tables)
+
+
+def rotary_tables(positions, width):
+    half_rot = ROT // 2
+    frequency = jnp.exp(-(jnp.arange(half_rot, dtype=F32) * 2.0 / ROT) * theta_log)
+    angles = positions.astype(F32)[:, None] * frequency[None, :]
+    cos, sin = jnp.cos(angles), jnp.sin(angles)
+    length = positions.shape[0]
+    rest = jnp.ones((length, HD - ROT), F32)
+    none, gap = jnp.zeros((length, half_rot), F32), jnp.zeros((length, HD - ROT), F32)
+    copies = width // HD
+    return (
+        jnp.tile(jnp.concatenate([cos, cos, rest], axis=1), (1, copies)),
+        jnp.tile(jnp.concatenate([-sin, none, gap], axis=1), (1, copies)),
+        jnp.tile(jnp.concatenate([none, sin, gap], axis=1), (1, copies)),
+    )
+
+
+def all_sum(values, axes):
+    for axis in axes:
+        size = lax.axis_size(axis)
+        if size & (size - 1):
+            values = lax.psum(values, axis)
+            continue
+        step = 1
+        while step < size:
+            values = values + lax.ppermute(values, axis, [(i, i ^ step) for i in range(size)])
+            step *= 2
+    return values
+
+
+def owner_sum(part, axis):
+    return lax.psum_scatter(part, "dp", scatter_dimension=axis, tiled=True)
+
+
+def after(values, *others):
+    return lax.optimization_barrier((values, *others))
+
+
+def per_device(
+    tokens, positions, norm_gain, norm_bias, w_qkv, b_qkv, w_out, w_gate_up, w_down, cotangent
+):
+    count = lax.axis_size("tensor")
+    tensor_rank = lax.axis_index("tensor")
+    width = w_qkv.shape[3]
+    ff_local = w_gate_up.shape[3]
+    rows, depth = tokens.shape
+    length = positions.shape[0]
+    tables = rotary_tables(positions, min(256, width))
+    pair_tables = tuple(table[:, :PAIR] for table in tables)
+    positions_row = positions.reshape(1, length)
+
+    def whole(weight, axis):
+        return lax.all_gather(weight, "dp", axis=axis, tiled=True)
+
+    flat = [
+        [
+            w_qkv[layer].reshape(-1, 3 * width),
+            w_out[layer],
+            w_gate_up[layer].reshape(-1, 2 * ff_local),
+            w_down[layer],
+        ]
+        for layer in range(LAYERS)
+    ]
+    axes = (0, 1, 0, 1)
+    gathered = [[whole(flat[0][kind], axes[kind]) for kind in range(3)] + [None]]
+    hidden = tokens.astype(F32)
+    scaled, _ = norm_rows(hidden)
+    normed = (scaled * norm_gain[0, 0] + norm_bias[0, 0]).astype(BF16)
+    block_tables = tuple(table.reshape(count, rows, -1) for table in tables)
+    biases = [
+        lax.dynamic_slice_in_dim(b_qkv[layer], tensor_rank * width, width, 1).reshape(1, 3 * width)
+        for layer in range(LAYERS)
+    ]
+    rows_a, mixed = first(count, normed, gathered[0][0], biases[0], block_tables, width)
+    mixed, flat[0][3] = after(mixed, flat[0][3])
+    gathered[0][3] = whole(flat[0][3], axes[3])
+    kept = []
+    for layer in range(LAYERS):
+        mixed = mixed.reshape(3, length, width)
+        attended, logsums = attend(mixed, positions_row)
+        if layer + 1 < LAYERS:
+            attended, *flat[layer + 1] = after(attended, *flat[layer + 1])
+            gathered.append([whole(flat[layer + 1][kind], axes[kind]) for kind in range(4)])
+        full_qkv, full_out, full_gu, full_down = gathered[layer]
+        hidden_mid, rows_b, act, slope, silu = middle(
+            count,
+            attended.reshape(count, rows, width),
+            full_out,
+            hidden,
+            norm_gain[layer, 1:2],
+            norm_bias[layer, 1:2],
+            full_gu,
+        )
+        kept.append((hidden, rows_a, mixed, attended, logsums, hidden_mid, rows_b, act, slope, silu))
+        if layer + 1 < LAYERS:
+            hidden, rows_a, mixed = between(
+                count,
+                act,
+                full_down,
+                hidden_mid,
+                norm_gain[layer + 1, 0:1],
+                norm_bias[layer + 1, 0:1],
+                gathered[layer + 1][0],
+                biases[layer + 1],
+                block_tables,
+            )
+        else:
+            activations, grad_rows_b, wide = turn(
+                count, act, full_down, hidden_mid, cotangent, slope, silu
+            )
+    grad = cotangent.astype(F32)
+    scattered = [None] * LAYERS
+    small = [None] * LAYERS
+    for layer in reversed(range(LAYERS)):
+        hidden, rows_a, mixed, attended, logsums, hidden_mid, rows_b, act, slope, silu = kept[layer]
+        full_qkv, full_out, full_gu, full_down = gathered[layer]
+        later = scattered[layer + 1] if layer + 1 < LAYERS else None
+        gu_part = matmul(
+            rows_b.reshape(length, depth), wide.reshape(length, 2 * ff_local), rows_rows
+        ).astype(BF16)
+        down_part = matmul(
+            act.reshape(length, ff_local), grad_rows_b.reshape(length, depth), rows_rows
+        ).astype(BF16)
+        wide, down_part, gu_part = after(wide, down_part, gu_part)
+        gu_grad, down_grad = owner_sum(gu_part, 0), owner_sum(down_part, 1)
+        if later:
+            wide, later[2] = after(wide, later[2])
+        grad, gain_b, shift_b, grad_rows_a, grad_attended = middle_back(
+            count, wide, full_gu, grad, hidden_mid, norm_gain[layer, 1:2], full_out
+        )
+        out_part = matmul(attended, grad_rows_a.reshape(length, depth), rows_rows).astype(BF16)
+        grad_attended, out_part = after(grad_attended, out_part)
+        out_grad = owner_sum(out_part, 1)
+        if later:
+            grad_attended, later[3] = after(grad_attended, later[3])
+        grad_mixed, bias_sum = attend_backward(
+            mixed, positions_row, attended, grad_attended.reshape(length, width), logsums, pair_tables
+        )
+        flat_mixed = grad_mixed.transpose(1, 0, 2).reshape(length, 3 * width)
+        qkv_part = matmul(rows_a.reshape(length, depth), flat_mixed, rows_rows).astype(BF16)
+        grad_mixed, qkv_part = after(grad_mixed, qkv_part)
+        qkv_grad = owner_sum(qkv_part, 0)
+        if later:
+            grad_mixed, later[0], later[1] = after(grad_mixed, later[0], later[1])
+        source = grad_mixed.reshape(3, count, rows, width)
+        if layer:
+            below = kept[layer - 1]
+            grad, gain_a, shift_a, grad_rows_b, wide = between_back(
+                count,
+                source,
+                full_qkv,
+                grad,
+                hidden,
+                norm_gain[layer, 0:1],
+                gathered[layer - 1][3],
+                below[8],
+                below[9],
+            )
+        else:
+            grad, gain_a, shift_a = last(count, source, full_qkv, grad, hidden, norm_gain[layer, 0:1])
+        bias_full = lax.dynamic_update_slice(
+            jnp.zeros((3, b_qkv.shape[2]), F32), bias_sum, (jnp.int32(0), tensor_rank * width)
+        )
+        small[layer] = jnp.concatenate([gain_a, gain_b, shift_a, shift_b, bias_full], axis=0)
+        scattered[layer] = [qkv_grad, out_grad, gu_grad, down_grad]
+    sums = all_sum(jnp.stack(small), ("dp", "tensor"))
+    shapes = ((-1, 3, width), (width, -1), (-1, 2, ff_local), (ff_local, -1))
+    stacks = [
+        jnp.stack([scattered[layer][kind].astype(F32).reshape(shape) for layer in range(LAYERS)])
+        for kind, shape in enumerate(shapes)
+    ]
+    return (
+        activations,
+        grad,
+        sums[:, 0:2],
+        sums[:, 2:4],
+        stacks[0],
+        sums[:, 4:7],
+        stacks[1],
+        stacks[2],
+        stacks[3],
+    )
 
 
 def norm_parts(hidden):
@@ -33,7 +1314,7 @@
     return (grad_input, jnp.sum(grad_normed * scaled, axis=0), jnp.sum(grad_normed, axis=0))
 
 
-def rotary_tables(positions):
+def plain_tables(positions):
     half_rot = ROT // 2
     frequency = jnp.exp(-(jnp.arange(half_rot, dtype=jnp.float32) * 2.0 / ROT) * theta_log)
     angles = positions.astype(jnp.float32)[:, None] * frequency[None, :]
@@ -55,11 +1336,11 @@
 
 
 def inner_rows(left, right):
-    return lax.dot_general(left, right, contract_rows, preferred_element_type=jnp.float32)
+    return lax.dot_general(left, right, rows_rows, preferred_element_type=jnp.float32)
 
 
 def inner_cols(left, right):
-    return lax.dot_general(left, right, contract_cols, preferred_element_type=jnp.float32)
+    return lax.dot_general(left, right, cols_cols, preferred_element_type=jnp.float32)
 
 
 def block_scores(queries, key_rows, positions, number, block_rows, score_scale):
@@ -144,7 +1425,7 @@
     return (grad_queries.reshape(queries.shape), grad_keys, grad_values)
 
 
-def per_device(
+def per_device_plain(
     tokens, positions, norm_gain, norm_bias, w_qkv, b_qkv, w_out, w_gate_up, w_down, cotangent
 ):
     tensor_rank = lax.axis_index("tensor")
@@ -154,7 +1435,7 @@
     local_rows = tokens.shape[0]
     seq_len = positions.shape[0]
     score_scale = 1.0 / math.sqrt(HD)
-    cos_table, sin_table = rotary_tables(positions)
+    cos_table, sin_table = plain_tables(positions)
     hidden = tokens.astype(jnp.float32)
     kept_state = []
     for layer_index in range(LAYERS):
@@ -385,6 +1666,10 @@
         P(None, "dp", None, "tensor"),
         P(None, "tensor", "dp"),
     )
+    def run(*operands):
+        fits = operands[7].shape[3] % 128 == 0 and operands[4].shape[3] % PAIR == 0
+        return (per_device if fits else per_device_plain)(*operands)
+
     return jax.shard_map(
-        per_device, mesh=mesh, in_specs=in_specs, out_specs=out_specs, check_vma=False
-    )
+        run, mesh=mesh, in_specs=in_specs, out_specs=out_specs, check_vma=False
+    )

time: 2740 us -> 1370 us (0.50)
  waiting for transfers between devices: 1740 us -> 38.4 us
  Pallas kernels: 0 us -> 1140 us
  matrix products: 596 us -> 91.8 us
  local copies, waits for them, and re-layouts: 255 us -> 56.6 us
  other arithmetic: 105 us -> 18.6 us
    pallas_call x0 -> x13, Pallas kernels: none -> 1140 us  [the longest x2 279 us: middle_back(): line_call(functools.partial(middle_back_kernel, count, pieces), (jax.Shap...]
    reduce_scatter x16 -> x8, waiting for transfers between devices: 808 us -> 0.1 us  [owner_sum(): return lax.psum_scatter(part, 'dp', scatter_dimension=axis, tiled=True)]
    all_gather x16 -> x8, waiting for transfers between devices: 805 us -> 25.9 us  [whole(): return lax.all_gather(weight, 'dp', axis=axis, tiled=True)]
    dot_general x52 -> x8, matrix products: 596 us -> 91.8 us  [matmul(): return lax.dot_general(left, right, dims, preferred_element_type=F32)]
    psum x1 -> x0, waiting for transfers between devices: 125 us -> none  [per_device(): lax.psum((jnp.stack(gain_rows), jnp.stack(shift_rows), jnp.stack(qkv_shif...]
    dynamic_update_slice x10 -> x2, local copies, waits for them, and re-layouts: 87.7 us -> 0.02 us  [per_device(): lax.dynamic_update_slice(jnp.zeros((3, b_qkv.shape[2]), F32), bias_sum, (...]
    reduce_sum x18 -> x2, other arithmetic: 42 us -> 0.64 us  [the longest x1 0.42 us: norm_rows(): variance = jnp.mean(centred * centred, axis=-1, keepdims=True)]
    unnamed x194 -> x65, local copies, waits for them, and re-layouts: 49.2 us -> 17.1 us
  transfers between devices with their start and end apart: 33 -> 21, of which waited for: 27 -> 5; matrix products, arithmetic and copies ran while one was open for 22% -> 9% of each run, Pallas kernels for 0% -> 74%
where the time goes in v2:
time: 1370 us
  Pallas kernels  1140 us (83%)
  matrix products  91.8 us (7%)
  local copies, waits for them, and re-layouts  56.6 us (4%)
  waiting for transfers between devices  38.4 us (3%)
  other arithmetic  18.6 us (1%)
  between operations  14.8 us (1%)
    pallas_call x2, Pallas kernels, middle_back(): line_call(functools.partial(middle_back_kernel, count, pieces), (jax.Shap...  279 us
    pallas_call x2, Pallas kernels, middle(): line_call(functools.partial(middle_kernel, count, pieces), (jax.ShapeDtyp...  246 us
    pallas_call x1, Pallas kernels, between_back(): line_call(functools.partial(between_back_kernel, count, pieces), (jax.Sha...  126 us
    pallas_call x1, Pallas kernels, turn(): line_call(functools.partial(turn_kernel, count, pieces), (jax.ShapeDtypeS...  126 us
    pallas_call x1, Pallas kernels, between(): line_call(functools.partial(between_kernel, count, pieces), (jax.ShapeDty...  125 us
    dot_general x8, matrix products, matmul(): return lax.dot_general(left, right, dims, preferred_element_type=F32)  91.8 us
    pallas_call x1, Pallas kernels, first(): line_call(functools.partial(first_kernel, count, pieces), (jax.ShapeDtype...  85.9 us
    pallas_call x1, Pallas kernels, last(): line_call(functools.partial(last_kernel, count, pieces), (jax.ShapeDtypeS...  77.6 us
  transfers between devices with their start and end apart: 21, of which 5 were waited for; matrix products, arithmetic and copies ran while one was open for 9% of the time, Pallas kernels for 74%

profile of v2, /device:TPU:0, one launch (start us, length us, event | category | flops | bytes accessed | tf_op | source)
XLA Modules:
  0.0 1365.0 jit_solution(7544955109437598076)
XLA Ops:
  7.2 2.4 fusion.3
  12.1 4.6 fusion.2
  19.3 1.4 copy.32.refs_3_.refs_7_
  21.7 1.4 copy.33.refs_4_.refs_8_
  23.3 1.4 tile.38
  24.7 2.6 copy.34.refs_5_.refs_9_
  29.8 1.4 add_convert_fusion.refs_0_
  31.3 2.5 slice_bitcast_fusion
  33.8 25.8 %all-gather.10.cloned.1.call-done.refs_1_ = bf16[2048,1536]{1,0:T(8,128)(2,1)} async-done(((bf16[256,1536]{1,0:T(8,128)(2,1)}), bf16[2048,1536]{1,0:T(8,128)(2,1)}) %all-gather.10.cloned.1.call-update) | async-done | bytes 6291472 | tf_op jit(solution)/shard_map/all_gather | solution.py:1169
  59.6 85.9 %shard_map.169 = (bf16[4,256,2048]{2,1,0:T(8,128)(2,1)}, bf16[3,4,256,512]{3,2,1,0:T(8,128)(2,1)}) custom-call(bf16[256,2048]{1,0:T(8,128)(2,1)} %add_convert_fusion.refs_0_, bf16[2048,1536]{1,0:T(8,128)(2,1)} %all-gather.10.cloned.1.call-done.refs_1_, f32[1,1536]{1,0:T(1,128)} %bitcast.120, f32[4,256,256]{2,1,0:T(8,128)} %copy.32.refs_3_.refs_7_, ...), custom_call_target="tpu_custom_call" | custom-call | flops 6442450944 | bytes 23068672 | tf_op jit(solution)/shard_map/pallas_call | solution.py:585
  145.8 1.5 copy.58
  148.6 18.3 %shard_map.170 = (bf16[1024,512]{1,0:T(8,128)(2,1)}, f32[4,2,1024]{2,1,0:T(2,128)}) custom-call(s32[1,1024]{1,0:T(1,128)} %bitcast.122, bf16[3,1024,512]{2,1,0:T(8,128)(2,1)} %bitcast.132, bf16[3,1024,512]{2,1,0:T(8,128)(2,1)} %bitcast.133, bf16[3,1024,512]{2,1,0:T(8,128)(2,1)} %bitcast.134), custom_call_target="tpu_custom_call" | custom-call | flops 4294967296 | bytes 4194304 | tf_op jit(solution)/shard_map/pallas_call | solution.py:1001
  170.2 1.6 convert_element_type.44.refs_2_.refs_3_
  172.4 124.2 %shard_map.171 = (f32[256,2048]{1,0:T(8,128)}, bf16[4,256,2048]{2,1,0:T(8,128)(2,1)}, bf16[4,256,1408]{2,1,0:T(8,128)(2,1)}, bf16[4,256,1408]{2,1,0:T(8,128)(2,1)}, bf16[4,256,1408]{2,1,0:T(8,128)(2,1)}) custom-call(bf16[4,256,512]{2,1,0:T(8,128)(2,1)} %bitcast.144, bf16[512,2048]{1,0:T(8,128)(2,1)} %bitcast.126, ...), custom_call_target="tpu_custom_call" | custom-call | flops 13958643712 | bytes 45088768 | tf_op jit(solution)/shard_map/pallas_call | solution.py:640
  296.6 125.0 %shard_map.172 = (f32[256,2048]{1,0:T(8,128)}, bf16[4,256,2048]{2,1,0:T(8,128)(2,1)}, bf16[3,4,256,512]{3,2,1,0:T(8,128)(2,1)}) custom-call(bf16[4,256,1408]{2,1,0:T(8,128)(2,1)} %get-tuple-element.85.refs_0_, bf16[1408,2048]{1,0:T(8,128)(2,1)} %all-gather.14.cloned.1.call-done.refs_1_.refs_5_, f32[256,2048]{1,0:T(8,128)} %get-tuple-element.87.refs_2_.refs_3_, ...), custom_call_target="tpu_custom_call" | custom-call | flops 12348030976 | bytes 43515904 | tf_op jit(solution)/shard_map/pallas_call | solution.py:700
  421.6 18.3 %shard_map.173 = (bf16[1024,512]{1,0:T(8,128)(2,1)}, f32[4,2,1024]{2,1,0:T(2,128)}) custom-call(s32[1,1024]{1,0:T(1,128)} %bitcast.123, bf16[3,1024,512]{2,1,0:T(8,128)(2,1)} %bitcast.138, bf16[3,1024,512]{2,1,0:T(8,128)(2,1)} %bitcast.139, bf16[3,1024,512]{2,1,0:T(8,128)(2,1)} %bitcast.140), custom_call_target="tpu_custom_call" | custom-call | flops 4294967296 | bytes 4194304 | tf_op jit(solution)/shard_map/pallas_call | solution.py:1001
  440.0 121.8 %shard_map.174 = (f32[256,2048]{1,0:T(8,128)}, bf16[4,256,2048]{2,1,0:T(8,128)(2,1)}, bf16[4,256,1408]{2,1,0:T(8,128)(2,1)}, bf16[4,256,1408]{2,1,0:T(8,128)(2,1)}, bf16[4,256,1408]{2,1,0:T(8,128)(2,1)}) custom-call(bf16[4,256,512]{2,1,0:T(8,128)(2,1)} %bitcast.145, bf16[512,2048]{1,0:T(8,128)(2,1)} %all-gather.18.cloned.1.call-done.refs_1_.refs_5_, ...), custom_call_target="tpu_custom_call" | custom-call | flops 13958643712 | bytes 45088768 | tf_op jit(solution)/shard_map/pallas_call | solution.py:640
  561.8 126.0 %shard_map.175 = (bf16[256,2048]{1,0:T(8,128)(2,1)}, bf16[4,256,2048]{2,1,0:T(8,128)(2,1)}, bf16[4,256,2816]{2,1,0:T(8,128)(2,1)}) custom-call(bf16[4,256,1408]{2,1,0:T(8,128)(2,1)} %get-tuple-element.94.refs_0_, bf16[1408,2048]{1,0:T(8,128)(2,1)} %all-gather.22.cloned.1.call-done.refs_1_, f32[256,2048]{1,0:T(8,128)} %get-tuple-element.96.refs_2_.refs_3_, ...), custom_call_target="tpu_custom_call" | custom-call | flops 11811160064 | bytes 37224448 | tf_op jit(solution)/shard_map/pallas_call | solution.py:763
  687.8 10.4 bitcast_convert_fusion.3
  698.2 18.2 %bitcast_convert_fusion.1 = bf16[2048,2816]{1,0:T(8,128)(2,1)} fusion(bf16[4,256,2048]{2,1,0:T(8,128)(2,1)} %get-tuple-element.102, bf16[4,256,2816]{2,1,0:T(8,128)(2,1)} %get-tuple-element.103.refs_0_), kind=kOutput, calls=%fused_computation.1 | convolution fusion | flops 11816927232 | bytes 21495808 | tf_op jit(solution)/shard_map/dot_general | solution.py:29
  717.7 1.6 convert_element_type.49.refs_2_
  719.3 145.5 %shard_map.176 = (f32[256,2048]{1,0:T(8,128)}, f32[1,2048]{1,0:T(1,128)}, f32[1,2048]{1,0:T(1,128)}, bf16[4,256,2048]{2,1,0:T(8,128)(2,1)}, bf16[4,256,512]{2,1,0:T(8,128)(2,1)}) custom-call(bf16[4,256,2816]{2,1,0:T(8,128)(2,1)} %get-tuple-element.103.refs_0_, bf16[2048,2816]{1,0:T(8,128)(2,1)} %all-gather.20.cloned.1.call-done.refs_5_.refs_1_, ...), custom_call_target="tpu_custom_call" | custom-call | flops 13958643712 | bytes 45088768 | tf_op jit(solution)/shard_map/pallas_call | solution.py:822
  864.8 6.3 convolution_convert_fusion.3
  872.0 2.1 copy.61.sin_down
  876.2 18.9 %shard_map.177 = (bf16[3,1024,512]{2,1,0:T(8,128)(2,1)}, f32[3,512]{1,0:T(4,128)}) custom-call(s32[1,1024]{1,0:T(1,128)} %bitcast.124, bf16[3,1024,512]{2,1,0:T(8,128)(2,1)} %bitcast.141, bf16[3,1024,512]{2,1,0:T(8,128)(2,1)} %bitcast.142, bf16[3,1024,512]{2,1,0:T(8,128)(2,1)} %bitcast.143, bf16[1024,512]{1,0:T(8,128)(2,1)} %get-tuple-element.90.attended, ...), custom_call_target="tpu_custom_call" | custom-call | flops 10737418240 | bytes 8388608 | tf_op jit(solution)/shard_map/pallas_call | solution.py:1085
  895.1 3.2 copy.45
  898.4 11.0 convolution_convert_fusion.1
  909.5 126.3 %shard_map.178 = (f32[256,2048]{1,0:T(8,128)}, f32[1,2048]{1,0:T(1,128)}, f32[1,2048]{1,0:T(1,128)}, bf16[4,256,2048]{2,1,0:T(8,128)(2,1)}, bf16[4,256,2816]{2,1,0:T(8,128)(2,1)}) custom-call(bf16[3,4,256,512]{3,2,1,0:T(8,128)(2,1)} %bitcast.103, bf16[2048,1536]{1,0:T(8,128)(2,1)} %all-gather.16.cloned.1.call-done.refs_5_.refs_1_, ...), custom_call_target="tpu_custom_call" | custom-call | flops 12348030976 | bytes 43515904 | tf_op jit(solution)/shard_map/pallas_call | solution.py:891
  1035.8 10.5 bitcast_convert_fusion.2
  1046.2 18.2 %bitcast_convert_fusion = bf16[2048,2816]{1,0:T(8,128)(2,1)} fusion(bf16[4,256,2048]{2,1,0:T(8,128)(2,1)} %get-tuple-element.116, bf16[4,256,2816]{2,1,0:T(8,128)(2,1)} %get-tuple-element.119.refs_0_), kind=kOutput, calls=%fused_computation | convolution fusion | flops 11816927232 | bytes 21495808 | tf_op jit(solution)/shard_map/dot_general | solution.py:29
  1065.1 133.4 %shard_map.179 = (f32[256,2048]{1,0:T(8,128)}, f32[1,2048]{1,0:T(1,128)}, f32[1,2048]{1,0:T(1,128)}, bf16[4,256,2048]{2,1,0:T(8,128)(2,1)}, bf16[4,256,512]{2,1,0:T(8,128)(2,1)}) custom-call(bf16[4,256,2816]{2,1,0:T(8,128)(2,1)} %get-tuple-element.119.refs_0_, bf16[2048,2816]{1,0:T(8,128)(2,1)} %all-gather.12.cloned.1.call-done.refs_5_.refs_1_, ...), custom_call_target="tpu_custom_call" | custom-call | flops 13958643712 | bytes 45088768 | tf_op jit(solution)/shard_map/pallas_call | solution.py:822
  1198.5 6.1 convolution_convert_fusion.2
  1204.7 18.8 %shard_map.180 = (bf16[3,1024,512]{2,1,0:T(8,128)(2,1)}, f32[3,512]{1,0:T(4,128)}) custom-call(s32[1,1024]{1,0:T(1,128)} %bitcast.125, bf16[3,1024,512]{2,1,0:T(8,128)(2,1)} %bitcast.135, bf16[3,1024,512]{2,1,0:T(8,128)(2,1)} %bitcast.136, bf16[3,1024,512]{2,1,0:T(8,128)(2,1)} %bitcast.137, bf16[1024,512]{1,0:T(8,128)(2,1)} %get-tuple-element.84.attended, ...), custom_call_target="tpu_custom_call" | custom-call | flops 10737418240 | bytes 8388608 | tf_op jit(solution)/shard_map/pallas_call | solution.py:1085
  1223.5 3.3 copy.48
  1226.8 11.1 convolution_convert_fusion
  1238.9 77.6 %shard_map.181 = (f32[256,2048]{1,0:T(8,128)}, f32[1,2048]{1,0:T(1,128)}, f32[1,2048]{1,0:T(1,128)}) custom-call(bf16[3,4,256,512]{3,2,1,0:T(8,128)(2,1)} %bitcast.101, bf16[2048,1536]{1,0:T(8,128)(2,1)} %all-gather.10.cloned.1.call-done.refs_1_, f32[256,2048]{1,0:T(8,128)} %get-tuple-element.133.refs_2_, f32[256,2048]{1,0:T(8,128)} %convert_element_type.44.refs_2_.refs_3_, ...), custom_call_target="tpu_custom_call" | custom-call | flops 6442450944 | bytes 16777216 | tf_op jit(solution)/shard_map/pallas_call | solution.py:939
  1317.4 1.3 collective-permute-done
  1318.8 5.5 collective-permute-done.1
  1324.9 3.2 stack_reshape.18
  1329.4 2.4 collective-permute-start.3
  1331.9 6.2 maximum_convert_fusion
  1338.1 1.4 collective-permute-start.4
  1339.5 3.1 maximum_convert_fusion.2
  1346.3 2.0 maximum_convert_fusion.3
  1348.3 2.3 copy.49
  1350.5 1.6 maximum_convert_fusion.1
  1352.1 2.4 copy.51
  1354.5 2.5 copy.68
  (159 shorter events, 27.6 us)
Async XLA Ops:
  7.2 4.0 copy-start.12
  7.2 52.4 %all-gather.10.cloned.1.call-start = ((), (), s32[]{:S(2)}) async-start(), calls=%async_computation.8 | async-start | bytes 7077888 | tf_op jit(solution)/shard_map/all_gather | solution.py:1169
  11.1 161.2 %all-gather.24.cloned.1.call-start = ((), (), s32[]{:S(2)}) async-start(), calls=%async_computation.23 | async-start | bytes 2359296 | tf_op jit(solution)/shard_map/all_gather | solution.py:1169
  12.1 160.3 %all-gather.12.cloned.1.call-start = ((), (), s32[]{:S(2)}) async-start(), calls=%async_computation.9 | async-start | bytes 12976128 | tf_op jit(solution)/shard_map/all_gather | solution.py:1169
  16.8 1.5 copy-start.25
  18.1 278.5 %all-gather.14.cloned.1.call-start = ((), (), s32[]{:S(2)}) async-start(), calls=%async_computation.10 | async-start | bytes 6488064 | tf_op jit(solution)/shard_map/all_gather | solution.py:1169
  18.8 2.5 copy-start.1
  20.8 1.0 copy-start.3
  23.1 4.2 copy-start.14
  23.1 4.8 copy-start
  23.2 5.3 copy-start.5
  23.2 5.3 copy-start.15
  23.2 6.0 copy-start.16
  145.5 1.8 copy-start.7
  145.5 151.1 %all-gather.16.cloned.1.call-start = ((), (), s32[]{:S(2)}) async-start(), calls=%async_computation.11 | async-start | bytes 7077888 | tf_op jit(solution)/shard_map/all_gather | solution.py:1169
  168.1 271.9 %all-gather.18.cloned.1.call-start = ((), (), s32[]{:S(2)}) async-start(), calls=%async_computation.12 | async-start | bytes 2359296 | tf_op jit(solution)/shard_map/all_gather | solution.py:1169
  168.7 271.3 %all-gather.20.cloned.1.call-start = ((), (), s32[]{:S(2)}) async-start(), calls=%async_computation.13 | async-start | bytes 12976128 | tf_op jit(solution)/shard_map/all_gather | solution.py:1169
  169.4 392.3 %all-gather.22.cloned.1.call-start = ((), (), s32[]{:S(2)}) async-start(), calls=%async_computation.14 | async-start | bytes 6488064 | tf_op jit(solution)/shard_map/all_gather | solution.py:1169
  170.2 894.9 %reduce-scatter.9.cloned.1.call-start = ((), (), s32[]{:S(2)}) async-start(), calls=%async_computation.15 | async-start | bytes 12976128 | tf_op jit(solution)/shard_map/reduce_scatter | solution.py:1148
  716.5 1.2 copy-start.10
  716.5 488.2 %reduce-scatter.11.cloned.1.call-start = ((), (), s32[]{:S(2)}) async-start(), calls=%async_computation.16 | async-start | bytes 6488064 | tf_op jit(solution)/shard_map/reduce_scatter | solution.py:1148
  717.1 521.7 %reduce-scatter.15.cloned.1.call-start = ((), (), s32[]{:S(2)}) async-start(), calls=%async_computation.18 | async-start | bytes 2359296 | tf_op jit(solution)/shard_map/reduce_scatter | solution.py:1148
  864.8 6.4 copy-start.6
  871.0 3.0 copy-start.4
  871.1 4.1 copy-start.2
  871.1 367.7 %reduce-scatter.13.cloned.1.call-start = ((), (), s32[]{:S(2)}) async-start(), calls=%async_computation.17 | async-start | bytes 7077888 | tf_op jit(solution)/shard_map/reduce_scatter | solution.py:1148
  909.4 415.4 %reduce-scatter.21.cloned.1.call-start = ((), (), s32[]{:S(2)}) async-start(), calls=%async_computation.21 | async-start | bytes 12976128 | tf_op jit(solution)/shard_map/reduce_scatter | solution.py:1148
  1064.5 275.1 %reduce-scatter.23.cloned.1.call-start = ((), (), s32[]{:S(2)}) async-start(), calls=%async_computation.22 | async-start | bytes 6488064 | tf_op jit(solution)/shard_map/reduce_scatter | solution.py:1148
  1065.0 281.2 %reduce-scatter.19.cloned.1.call-start = ((), (), s32[]{:S(2)}) async-start(), calls=%async_computation.20 | async-start | bytes 2359296 | tf_op jit(solution)/shard_map/reduce_scatter | solution.py:1148
  1065.1 133.4 %copy-start.26 = (bf16[1024,512]{1,0:T(8,128)(2,1)S(1)}, bf16[1024,512]{1,0:T(8,128)(2,1)}, u32[]{:S(2)}) copy-start(bf16[1024,512]{1,0:T(8,128)(2,1)} %get-tuple-element.84.attended) | copy-start | bytes 3145732
  1204.6 143.6 %reduce-scatter.17.cloned.1.call-start = ((), (), s32[]{:S(2)}) async-start(), calls=%async_computation.19 | async-start | bytes 7077888 | tf_op jit(solution)/shard_map/reduce_scatter | solution.py:1148
  1237.9 0.7 copy-start.23
  1237.9 0.7 copy-start.17
  1237.9 0.7 copy-start.18
  1237.9 0.7 copy-start.19
  1237.9 0.8 copy-start.20
  1238.0 0.9 copy-start.24
  1238.9 77.6 %copy-start.21 = (f32[1,2048]{1,0:T(1,128)S(1)}, f32[1,2048]{1,0:T(1,128)}, u32[]{:S(2)}) copy-start(f32[1,2048]{1,0:T(1,128)} %get-tuple-element.136) | copy-start | bytes 24580
  1238.9 77.6 %copy-start.22 = (f32[1,2048]{1,0:T(1,128)S(1)}, f32[1,2048]{1,0:T(1,128)}, u32[]{:S(2)}) copy-start(f32[1,2048]{1,0:T(1,128)} %get-tuple-element.138) | copy-start | bytes 24580
  1238.9 85.6 %copy-start.9 = (bf16[256,2816]{1,0:T(8,128)(2,1)S(1)}, bf16[256,2816]{1,0:T(8,128)(2,1)}, u32[]{:S(2)}) copy-start(bf16[256,2816]{1,0:T(8,128)(2,1)} %reduce-scatter.9.cloned.1.call-done) | copy-start | bytes 4325380
  1317.3 1.4 collective-permute-start
  1318.7 5.6 collective-permute-start.1
  1324.4 5.0 collective-permute-start.2
  1329.4 8.7 collective-permute-start.3
  1338.1 4.6 copy-start.11
  1338.1 6.8 collective-permute-start.4
  1339.5 6.7 copy-start.13
  1354.5 2.5 copy-start.8
Sparse Core Ops, SparseCore 0:
  11.3 48.2 all-gather.9
  61.4 28.1 all-gather.23
  92.1 67.7 all-gather.11
  161.6 44.3 all-gather.13
  207.8 45.4 all-gather.15
  255.0 28.2 all-gather.17
  285.8 67.8 all-gather.19
  355.6 44.2 all-gather.21
  716.6 82.6 reduce-scatter.8
  803.2 59.0 reduce-scatter.10
  871.2 37.1 reduce-scatter.14
  911.6 61.8 reduce-scatter.12
  1064.6 84.1 reduce-scatter.20
  1152.5 59.0 reduce-scatter.22
  1214.7 41.2 reduce-scatter.18
  1259.6 61.7 reduce-scatter.16

commit v3 on v2

--- a/solution.py
+++ b/solution.py
@@ -16,6 +16,7 @@
 F32 = jnp.float32
 BF16 = jnp.bfloat16
 VMEM_LIMIT = 62 * 2**20
+LAG = 6
 
 norm_eps = 1e-05
 theta_log = math.log(10000.0)
@@ -29,8 +30,10 @@
     return lax.dot_general(left, right, dims, preferred_element_type=F32)
 
 
-def line_barrier(place, count):
+def line_barrier(place, count, others=()):
     barrier = pltpu.get_barrier_semaphore()
+    for other in others:
+        pl.semaphore_signal(barrier, inc=1, device_id={"dp": other}, device_id_type=MESH)
 
     @pl.when(place > 0)
     def _():
@@ -44,11 +47,11 @@
 
     @pl.when(middle)
     def _():
-        pl.semaphore_wait(barrier, 2)
+        pl.semaphore_wait(barrier, 2 + len(others))
 
     @pl.when(jnp.logical_not(middle))
     def _():
-        pl.semaphore_wait(barrier, 1)
+        pl.semaphore_wait(barrier, 1 + len(others))
 
 
 def each_tile(width, tile, run):
@@ -128,7 +131,6 @@
         lax.fori_loop(0, self.rows // chunk, one, 0)
 
     def pass_on(self, piece, owner, right):
-        side = piece % 2
         first = pl.multiple_of(piece * self.rows, self.rows)
         onward = jnp.where(right, self.place > 0, self.place < self.count - 1)
 
@@ -139,7 +141,7 @@
             def rows(start, size):
                 at = pl.ds(pl.multiple_of(first + start, size), size)
                 self.sending[owner, at, :] = (
-                    self.shares[side, owner, pl.ds(start, size), :]
+                    self.shares[owner, at, :]
                     + self.arrived[owner, at, :].astype(F32)
                 ).astype(BF16)
 
@@ -149,14 +151,13 @@
         def _():
             def rows(start, size):
                 at = pl.ds(pl.multiple_of(first + start, size), size)
-                self.sending[owner, at, :] = self.shares[side, owner, pl.ds(start, size), :].astype(BF16)
+                self.sending[owner, at, :] = self.shares[owner, at, :].astype(BF16)
 
             self.chunks(rows)
 
         self.sum_hop(piece, owner).start()
 
     def collect(self, piece):
-        side = piece % 2
         first = pl.multiple_of(piece * self.rows, self.rows)
 
         def add(slot):
@@ -164,10 +165,9 @@
 
             def rows(start, size):
                 at = pl.ds(pl.multiple_of(first + start, size), size)
-                mine = pl.ds(start, size)
-                self.shares[side, self.place, mine, :] = self.shares[
-                    side, self.place, mine, :
-                ] + self.arrived[slot, at, :].astype(F32)
+                self.shares[self.place, at, :] = self.shares[self.place, at, :] + self.arrived[
+                    slot, at, :
+                ].astype(F32)
 
             self.chunks(rows)
 
@@ -180,86 +180,95 @@
             add(self.count)
 
     def own_rows(self, piece, run):
-        side = piece % 2
         first = pl.multiple_of(piece * self.rows, self.rows)
 
         def rows(start, size):
             at = pl.ds(pl.multiple_of(first + start, size), size)
-            run(at, self.shares[side, self.place, pl.ds(start, size), :])
+            run(at, self.shares[self.place, at, :])
 
         self.chunks(rows)
 
-    def run(self, term, finish, process):
+    def run(self, term, finish, process, each_tick=None):
         count, pieces, place = self.count, self.pieces, self.place
         scatter, gather = term is not None, process is not None
+        lead = count - 1 if scatter else 0
         if scatter:
             term(0)
 
-        def period(number, carry):
+        def tick(number, carry):
+            if each_tick is not None:
+                each_tick(number)
+
+            def valid(piece):
+                return (piece >= 0) & (piece < pieces)
+
             if scatter:
 
-                @pl.when(number < pieces)
-                def _():
-                    self.sides(count - 1, lambda owner, right: self.pass_on(number, owner, right))
-
-            @pl.when(number >= 1)
+                def sum_step(step, inner):
+                    piece = number - step
+
+                    @pl.when(valid(piece))
+                    def _():
+                        self.sides(
+                            count - 1 - step,
+                            lambda owner, right: self.pass_on(piece, owner, right),
+                        )
+
+                    return inner
+
+                lax.fori_loop(0, count - 1, sum_step, 0)
+            mine = number - lead
+
+            @pl.when(valid(mine))
             def _():
-                piece = number - 1
                 if scatter:
-                    self.collect(piece)
-                finish(piece)
+                    self.collect(mine)
+                finish(mine)
                 if gather:
 
                     @pl.when(place < count - 1)
                     def _():
-                        self.row_hop(piece, place, True).start()
+                        self.row_hop(mine, place, True).start()
 
                     @pl.when(place > 0)
                     def _():
-                        self.row_hop(piece, place, False).start()
-
+                        self.row_hop(mine, place, False).start()
+
+            if gather:
+
+                def row_step(step, inner):
+                    piece = mine - step
+
+                    def forward(block, right):
+                        self.row_hop(piece, block, True).wait_recv()
+                        onward = jnp.where(right, place > 0, place < count - 1)
+
+                        @pl.when(onward)
+                        def _():
+                            self.row_hop(piece, block, jnp.logical_not(right)).start()
+
+                    @pl.when(valid(piece))
+                    def _():
+                        self.sides(step, forward)
+
+                    return inner
+
+                lax.fori_loop(1, count, row_step, 0)
             if scatter:
 
                 @pl.when(number + 1 < pieces)
                 def _():
                     term(number + 1)
 
-            def slot(step, inner):
-                if scatter:
-
-                    @pl.when((number < pieces) & (step < count - 1))
-                    def _():
-                        self.sides(
-                            count - 1 - step,
-                            lambda owner, right: self.pass_on(number, owner, right),
-                        )
-
-                if gather:
-
-                    @pl.when(number >= 1)
-                    def _():
-                        def forward(block, right):
-                            self.row_hop(number - 1, block, True).wait_recv()
-                            onward = jnp.where(right, place > 0, place < count - 1)
-
-                            @pl.when(onward)
-                            def _():
-                                self.row_hop(number - 1, block, jnp.logical_not(right)).start()
-
-                        self.sides(step, forward)
-
-                    @pl.when((step == 1) & (number >= 2))
-                    def _():
-                        process(number - 2)
-
-                return inner
-
-            lax.fori_loop(1, count, slot, 0)
+            if gather:
+
+                @pl.when(valid(mine - (count - 1)))
+                def _():
+                    process(mine - (count - 1))
+
             return carry
 
-        lax.fori_loop(0, pieces + 1, period, 0)
-        if gather:
-            process(pieces - 1)
+        lax.fori_loop(0, pieces + lead + (count - 1 if gather else 0), tick, 0)
 
     def drain(self):
         def piece_sends(piece, carry):
@@ -298,7 +307,7 @@
 
 def scatter_scratch(count, pieces, rows, width):
     return [
-        pltpu.VMEM((2, count, rows // pieces, width), F32),
+        pltpu.VMEM((count, rows, width), F32),
         pltpu.VMEM((count, rows, width), BF16),
         pltpu.VMEM((count + 1, rows, width), BF16),
         pltpu.SemaphoreType.DMA((count, pieces)),
@@ -476,14 +485,9 @@
 
         def run(start, size):
             at = pl.ds(start, size)
-            put_rows(
-                line.shares.at[piece % 2],
-                slice(None),
-                at,
-                matmul(flat_rows(source, rows), weight[:, at]),
-            )
-
-        each_tile(line.shares.shape[3], 256, run)
+            put_rows(line.shares, rows, at, matmul(flat_rows(source, rows), weight[:, at]))
+
+        each_tile(line.shares.shape[2], 256, run)
 
     return term
 
@@ -503,9 +507,9 @@
                     weight[at, number * width : (number + 1) * width],
                     cols_cols,
                 )
-            put_rows(line.shares.at[piece % 2], slice(None), at, result)
-
-        each_tile(line.shares.shape[3], 256, run)
+            put_rows(line.shares, rows, at, result)
+
+        each_tile(line.shares.shape[2], 256, run)
 
     return term
 
@@ -575,6 +579,7 @@
         saves.start(piece)
 
     line.run(None, finish, process)
+
     line.drain()
     saves.wait()
 
@@ -603,14 +608,17 @@
     )(own, weight, bias, *tables)
 
 
-def middle_kernel(count, pieces, *refs):
-    ins, outs, scatter, gather, rest = split(refs, 6, 5, 5, 3, 8)
+def middle_kernel(count, pieces, lag, *refs):
+    ins, outs, scatter, gather, rest = split(refs, 6, 5, 5, 3, 9)
     source, w_out, before, gain, shift, w_up = ins
     after, rows_out, act_out, slope_out, silu_out = outs
-    source_held, out_held, up_held, act, slope, silu, load_sem, save_sem = rest
+    source_held, out_held, up_held, act, slope, silu, load_sem, save_sem, turn = rest
     line = Line(count, pieces, *scatter, *gather)
     loads = Loads([(source, source_held), (w_out, out_held), (w_up, up_held)], load_sem)
-    line_barrier(line.place, count)
+    member = lax.axis_index("dp")
+    core = member % 2
+    partner = member + 1 - 2 * core
+    line_barrier(line.place, count, (partner,) if lag else ())
     saves = Saves(
         [(line.held, rows_out), (act, act_out), (slope, slope_out), (silu, silu_out)], save_sem, line
     )
@@ -624,21 +632,35 @@
         compute(piece)
         saves.start(piece)
 
+    def signal(number):
+        @pl.when((core == 0) & (number == lag))
+        def _():
+            pl.semaphore_signal(turn, inc=1, device_id={"dp": partner}, device_id_type=MESH)
+
     loads.wait(0, 1)
+    if lag:
+
+        @pl.when(core == 1)
+        def _():
+            pl.semaphore_wait(turn, 1)
+
     line.run(
-        share_of(line, source_held, out_held), add_and_norm(line, before, gain, shift, after), process
+        share_of(line, source_held, out_held),
+        add_and_norm(line, before, gain, shift, after),
+        process,
+        signal if lag else None,
     )
     line.drain()
     saves.wait()
 
 
-def middle(count, source, w_out, before, gain, shift, w_up):
+def middle(count, source, w_out, before, gain, shift, w_up, lag=0):
     rows, depth = before.shape
     pieces = pieces_of(rows)
     width = w_up.shape[1] // 2
     wide = jax.ShapeDtypeStruct((count, rows, width), BF16)
     return line_call(
-        functools.partial(middle_kernel, count, pieces),
+        functools.partial(middle_kernel, count, pieces, lag),
         (
             jax.ShapeDtypeStruct((rows, depth), F32),
             jax.ShapeDtypeStruct((count, rows, depth), BF16),
@@ -659,8 +681,9 @@
             pltpu.VMEM(wide.shape, BF16),
             pltpu.SemaphoreType.DMA((3,)),
             pltpu.SemaphoreType.DMA((4, pieces)),
+            pltpu.SemaphoreType.REGULAR,
         ],
-        1,
+        7 if lag else 1,
         2 * count * rows * (w_out.size + w_up.size),
         (w_out.size + w_up.size) * 2 + before.size * 60,
     )(source, w_out, before, gain, shift, w_up)
@@ -1206,6 +1229,7 @@
             norm_gain[layer, 1:2],
             norm_bias[layer, 1:2],
             full_gu,
+            LAG if layer == 0 else 0,
         )
         kept.append((hidden, rows_a, mixed, attended, logsums, hidden_mid, rows_b, act, slope, silu))
         if layer + 1 < LAYERS:

time: 1370 us -> 1160 us (0.85)
  Pallas kernels: 1140 us -> 846 us
  waiting for transfers between devices: 38.4 us -> 81 us
  starting transfers between devices: 4.88 us -> 41.4 us
    pallas_call x2, Pallas kernels: 279 us -> 197 us  [middle_back(): line_call(functools.partial(middle_back_kernel, count, pieces), (jax.Shap...]
    pallas_call x2, Pallas kernels: 246 us -> 176 us  [middle(): line_call(functools.partial(middle_kernel, count, pieces, lag), (jax.Shap...]
    reduce_scatter x8, waiting for transfers between devices: 0.1 us -> 41.4 us  [owner_sum(): return lax.psum_scatter(part, 'dp', scatter_dimension=axis, tiled=True)]
    pallas_call x1, Pallas kernels: 126 us -> 88.8 us  [turn(): line_call(functools.partial(turn_kernel, count, pieces), (jax.ShapeDtypeS...]
    pallas_call x1, Pallas kernels: 125 us -> 88.2 us  [between(): line_call(functools.partial(between_kernel, count, pieces), (jax.ShapeDty...]
    ppermute x5, starting transfers between devices: 4.06 us -> 40.1 us  [all_sum(): lax.ppermute(values, axis, [(i, i ^ step) for i in range(size)])]
    pallas_call x1, Pallas kernels: 126 us -> 94.4 us  [between_back(): line_call(functools.partial(between_back_kernel, count, pieces), (jax.Sha...]
    pallas_call x1, Pallas kernels: 77.6 us -> 49.4 us  [last(): line_call(functools.partial(last_kernel, count, pieces), (jax.ShapeDtypeS...]
  transfers between devices with their start and end apart: 21 -> 21, of which waited for: 5 -> 7; matrix products, arithmetic and copies ran while one was open for 9% -> 11% of each run, Pallas kernels for 74% -> 66%
where the time goes in v3:
time: 1160 us; the launch traced here: 1150 us
  Pallas kernels  846 us (73%)
  matrix products  92.6 us (8%)
  waiting for transfers between devices  81 us (7%)
  local copies, waits for them, and re-layouts  56.3 us (5%)
  starting transfers between devices  41.4 us (4%)
  other arithmetic  19.2 us (2%)
  between operations  15 us (1%)
    pallas_call x2, Pallas kernels, middle_back(): line_call(functools.partial(middle_back_kernel, count, pieces), (jax.Shap...  197 us
    pallas_call x2, Pallas kernels, middle(): line_call(functools.partial(middle_kernel, count, pieces, lag), (jax.Shap...  176 us
    pallas_call x1, Pallas kernels, between_back(): line_call(functools.partial(between_back_kernel, count, pieces), (jax.Sha...  94.4 us
    dot_general x8, matrix products, matmul(): return lax.dot_general(left, right, dims, preferred_element_type=F32)  92.6 us
    pallas_call x1, Pallas kernels, turn(): line_call(functools.partial(turn_kernel, count, pieces), (jax.ShapeDtypeS...  88.8 us
    pallas_call x1, Pallas kernels, between(): line_call(functools.partial(between_kernel, count, pieces), (jax.ShapeDty...  88.2 us
    pallas_call x1, Pallas kernels, first(): line_call(functools.partial(first_kernel, count, pieces), (jax.ShapeDtype...  78.1 us
    pallas_call x1, Pallas kernels, last(): line_call(functools.partial(last_kernel, count, pieces), (jax.ShapeDtypeS...  49.4 us
  transfers between devices with their start and end apart: 21, of which 7 were waited for; matrix products, arithmetic and copies ran while one was open for 11% of the time, Pallas kernels for 66%

profile of v3, /device:TPU:0, one launch (start us, length us, event | category | flops | bytes accessed | tf_op | source)
XLA Modules:
  0.0 1151.8 jit_solution(15647460907631108858)
XLA Ops:
  7.2 2.4 fusion.3
  12.1 4.6 fusion.2
  23.3 1.4 tile.38
  24.7 2.6 copy.34.refs_5_.refs_9_
  31.3 2.5 slice_bitcast_fusion
  33.8 25.8 %all-gather.10.cloned.1.call-done.refs_1_ = bf16[2048,1536]{1,0:T(8,128)(2,1)} async-done(((bf16[256,1536]{1,0:T(8,128)(2,1)}), bf16[2048,1536]{1,0:T(8,128)(2,1)}) %all-gather.10.cloned.1.call-update) | async-done | bytes 6291472 | tf_op jit(solution)/shard_map/all_gather | solution.py:1192
  59.6 78.1 %shard_map.169 = (bf16[4,256,2048]{2,1,0:T(8,128)(2,1)}, bf16[3,4,256,512]{3,2,1,0:T(8,128)(2,1)}) custom-call(bf16[256,2048]{1,0:T(8,128)(2,1)} %add_convert_fusion.refs_0_, bf16[2048,1536]{1,0:T(8,128)(2,1)} %all-gather.10.cloned.1.call-done.refs_1_, f32[1,1536]{1,0:T(1,128)} %bitcast.120, f32[4,256,256]{2,1,0:T(8,128)} %copy.32.refs_3_.refs_7_, ...), custom_call_target="tpu_custom_call" | custom-call | flops 6442450944 | bytes 23068672 | tf_op jit(solution)/shard_map/pallas_call | solution.py:590
  141.0 18.3 %shard_map.170 = (bf16[1024,512]{1,0:T(8,128)(2,1)}, f32[4,2,1024]{2,1,0:T(2,128)}) custom-call(s32[1,1024]{1,0:T(1,128)} %bitcast.122, bf16[3,1024,512]{2,1,0:T(8,128)(2,1)} %bitcast.132, bf16[3,1024,512]{2,1,0:T(8,128)(2,1)} %bitcast.133, bf16[3,1024,512]{2,1,0:T(8,128)(2,1)} %bitcast.134), custom_call_target="tpu_custom_call" | custom-call | flops 4294967296 | bytes 4194304 | tf_op jit(solution)/shard_map/pallas_call | solution.py:1024
  162.6 1.6 convert_element_type.44.refs_2_.refs_3_
  164.8 85.8 %shard_map.171 = (f32[256,2048]{1,0:T(8,128)}, bf16[4,256,2048]{2,1,0:T(8,128)(2,1)}, bf16[4,256,1408]{2,1,0:T(8,128)(2,1)}, bf16[4,256,1408]{2,1,0:T(8,128)(2,1)}, bf16[4,256,1408]{2,1,0:T(8,128)(2,1)}) custom-call(bf16[4,256,512]{2,1,0:T(8,128)(2,1)} %bitcast.144, bf16[512,2048]{1,0:T(8,128)(2,1)} %bitcast.126, ...), custom_call_target="tpu_custom_call" | custom-call | flops 13958643712 | bytes 45088768 | tf_op jit(solution)/shard_map/pallas_call | solution.py:662
  250.6 2.8 all-gather.16.cloned.1.call-done.refs_5_.refs_1_
  253.3 88.2 %shard_map.172 = (f32[256,2048]{1,0:T(8,128)}, bf16[4,256,2048]{2,1,0:T(8,128)(2,1)}, bf16[3,4,256,512]{3,2,1,0:T(8,128)(2,1)}) custom-call(bf16[4,256,1408]{2,1,0:T(8,128)(2,1)} %get-tuple-element.85.refs_0_, bf16[1408,2048]{1,0:T(8,128)(2,1)} %all-gather.14.cloned.1.call-done.refs_1_.refs_5_, f32[256,2048]{1,0:T(8,128)} %get-tuple-element.87.refs_2_.refs_3_, ...), custom_call_target="tpu_custom_call" | custom-call | flops 12348030976 | bytes 43515904 | tf_op jit(solution)/shard_map/pallas_call | solution.py:723
  341.6 18.3 %shard_map.173 = (bf16[1024,512]{1,0:T(8,128)(2,1)}, f32[4,2,1024]{2,1,0:T(2,128)}) custom-call(s32[1,1024]{1,0:T(1,128)} %bitcast.123, bf16[3,1024,512]{2,1,0:T(8,128)(2,1)} %bitcast.138, bf16[3,1024,512]{2,1,0:T(8,128)(2,1)} %bitcast.139, bf16[3,1024,512]{2,1,0:T(8,128)(2,1)} %bitcast.140), custom_call_target="tpu_custom_call" | custom-call | flops 4294967296 | bytes 4194304 | tf_op jit(solution)/shard_map/pallas_call | solution.py:1024
  359.9 90.3 %shard_map.174 = (f32[256,2048]{1,0:T(8,128)}, bf16[4,256,2048]{2,1,0:T(8,128)(2,1)}, bf16[4,256,1408]{2,1,0:T(8,128)(2,1)}, bf16[4,256,1408]{2,1,0:T(8,128)(2,1)}, bf16[4,256,1408]{2,1,0:T(8,128)(2,1)}) custom-call(bf16[4,256,512]{2,1,0:T(8,128)(2,1)} %bitcast.145, bf16[512,2048]{1,0:T(8,128)(2,1)} %all-gather.18.cloned.1.call-done.refs_1_.refs_5_, ...), custom_call_target="tpu_custom_call" | custom-call | flops 13958643712 | bytes 45088768 | tf_op jit(solution)/shard_map/pallas_call | solution.py:662
  450.2 88.8 %shard_map.175 = (bf16[256,2048]{1,0:T(8,128)(2,1)}, bf16[4,256,2048]{2,1,0:T(8,128)(2,1)}, bf16[4,256,2816]{2,1,0:T(8,128)(2,1)}) custom-call(bf16[4,256,1408]{2,1,0:T(8,128)(2,1)} %get-tuple-element.94.refs_0_, bf16[1408,2048]{1,0:T(8,128)(2,1)} %all-gather.22.cloned.1.call-done.refs_1_, f32[256,2048]{1,0:T(8,128)} %get-tuple-element.96.refs_2_.refs_3_, ...), custom_call_target="tpu_custom_call" | custom-call | flops 11811160064 | bytes 37224448 | tf_op jit(solution)/shard_map/pallas_call | solution.py:786
  539.0 10.4 bitcast_convert_fusion.3
  549.5 18.2 %bitcast_convert_fusion.1 = bf16[2048,2816]{1,0:T(8,128)(2,1)} fusion(bf16[4,256,2048]{2,1,0:T(8,128)(2,1)} %get-tuple-element.102, bf16[4,256,2816]{2,1,0:T(8,128)(2,1)} %get-tuple-element.103.refs_0_), kind=kOutput, calls=%fused_computation.1 | convolution fusion | flops 11816927232 | bytes 21495808 | tf_op jit(solution)/shard_map/dot_general | solution.py:30
  569.0 1.6 convert_element_type.49.refs_2_
  570.5 96.2 %shard_map.176 = (f32[256,2048]{1,0:T(8,128)}, f32[1,2048]{1,0:T(1,128)}, f32[1,2048]{1,0:T(1,128)}, bf16[4,256,2048]{2,1,0:T(8,128)(2,1)}, bf16[4,256,512]{2,1,0:T(8,128)(2,1)}) custom-call(bf16[4,256,2816]{2,1,0:T(8,128)(2,1)} %get-tuple-element.103.refs_0_, bf16[2048,2816]{1,0:T(8,128)(2,1)} %all-gather.20.cloned.1.call-done.refs_5_.refs_1_, ...), custom_call_target="tpu_custom_call" | custom-call | flops 13958643712 | bytes 45088768 | tf_op jit(solution)/shard_map/pallas_call | solution.py:845
  666.7 6.3 convolution_convert_fusion.3
  673.9 2.1 copy.61.sin_down
  678.1 18.7 %shard_map.177 = (bf16[3,1024,512]{2,1,0:T(8,128)(2,1)}, f32[3,512]{1,0:T(4,128)}) custom-call(s32[1,1024]{1,0:T(1,128)} %bitcast.124, bf16[3,1024,512]{2,1,0:T(8,128)(2,1)} %bitcast.141, bf16[3,1024,512]{2,1,0:T(8,128)(2,1)} %bitcast.142, bf16[3,1024,512]{2,1,0:T(8,128)(2,1)} %bitcast.143, bf16[1024,512]{1,0:T(8,128)(2,1)} %get-tuple-element.90.attended, ...), custom_call_target="tpu_custom_call" | custom-call | flops 10737418240 | bytes 8388608 | tf_op jit(solution)/shard_map/pallas_call | solution.py:1108
  696.9 3.2 copy.45
  700.1 11.0 convolution_convert_fusion.1
  711.3 94.4 %shard_map.178 = (f32[256,2048]{1,0:T(8,128)}, f32[1,2048]{1,0:T(1,128)}, f32[1,2048]{1,0:T(1,128)}, bf16[4,256,2048]{2,1,0:T(8,128)(2,1)}, bf16[4,256,2816]{2,1,0:T(8,128)(2,1)}) custom-call(bf16[3,4,256,512]{3,2,1,0:T(8,128)(2,1)} %bitcast.103, bf16[2048,1536]{1,0:T(8,128)(2,1)} %all-gather.16.cloned.1.call-done.refs_5_.refs_1_, ...), custom_call_target="tpu_custom_call" | custom-call | flops 12348030976 | bytes 43515904 | tf_op jit(solution)/shard_map/pallas_call | solution.py:914
  805.8 10.5 bitcast_convert_fusion.2
  816.3 19.2 %bitcast_convert_fusion = bf16[2048,2816]{1,0:T(8,128)(2,1)} fusion(bf16[4,256,2048]{2,1,0:T(8,128)(2,1)} %get-tuple-element.116, bf16[4,256,2816]{2,1,0:T(8,128)(2,1)} %get-tuple-element.119.refs_0_), kind=kOutput, calls=%fused_computation | convolution fusion | flops 11816927232 | bytes 21495808 | tf_op jit(solution)/shard_map/dot_general | solution.py:30
  836.2 101.0 %shard_map.179 = (f32[256,2048]{1,0:T(8,128)}, f32[1,2048]{1,0:T(1,128)}, f32[1,2048]{1,0:T(1,128)}, bf16[4,256,2048]{2,1,0:T(8,128)(2,1)}, bf16[4,256,512]{2,1,0:T(8,128)(2,1)}) custom-call(bf16[4,256,2816]{2,1,0:T(8,128)(2,1)} %get-tuple-element.119.refs_0_, bf16[2048,2816]{1,0:T(8,128)(2,1)} %all-gather.12.cloned.1.call-done.refs_5_.refs_1_, ...), custom_call_target="tpu_custom_call" | custom-call | flops 13958643712 | bytes 45088768 | tf_op jit(solution)/shard_map/pallas_call | solution.py:845
  937.2 5.8 convolution_convert_fusion.2
  943.1 18.7 %shard_map.180 = (bf16[3,1024,512]{2,1,0:T(8,128)(2,1)}, f32[3,512]{1,0:T(4,128)}) custom-call(s32[1,1024]{1,0:T(1,128)} %bitcast.125, bf16[3,1024,512]{2,1,0:T(8,128)(2,1)} %bitcast.135, bf16[3,1024,512]{2,1,0:T(8,128)(2,1)} %bitcast.136, bf16[3,1024,512]{2,1,0:T(8,128)(2,1)} %bitcast.137, bf16[1024,512]{1,0:T(8,128)(2,1)} %get-tuple-element.84.attended, ...), custom_call_target="tpu_custom_call" | custom-call | flops 10737418240 | bytes 8388608 | tf_op jit(solution)/shard_map/pallas_call | solution.py:1108
  961.9 3.2 copy.48
  965.0 11.1 convolution_convert_fusion
  977.1 49.4 %shard_map.181 = (f32[256,2048]{1,0:T(8,128)}, f32[1,2048]{1,0:T(1,128)}, f32[1,2048]{1,0:T(1,128)}) custom-call(bf16[3,4,256,512]{3,2,1,0:T(8,128)(2,1)} %bitcast.101, bf16[2048,1536]{1,0:T(8,128)(2,1)} %all-gather.10.cloned.1.call-done.refs_1_, f32[256,2048]{1,0:T(8,128)} %get-tuple-element.133.refs_2_, f32[256,2048]{1,0:T(8,128)} %convert_element_type.44.refs_2_.refs_3_, ...), custom_call_target="tpu_custom_call" | custom-call | flops 6442450944 | bytes 16777216 | tf_op jit(solution)/shard_map/pallas_call | solution.py:962
  1027.3 33.1 %collective-permute-start = (f32[2,7,2048]{2,1,0:T(8,128)S(1)}, f32[2,7,2048]{2,1,0:T(8,128)S(1)}, u32[]{:S(2)}, u32[]{:S(2)}) collective-permute-start(f32[2,7,2048]{2,1,0:T(8,128)S(1)} %pad_maximum_fusion), channel_id=1, source_target_pairs={{0,4},{4,0},{8,12},{12,8},{16,20},{20,16},{24,28},{28,24},{1,5},{5... | collective-permute-start | bytes 344072 | tf_op jit(solution)/shard_map/ppermute | solution.py:1165
  1061.5 1.7 collective-permute-start.1
  1063.2 5.4 collective-permute-done.1
  1068.6 1.5 collective-permute-start.2
  1070.6 3.2 stack_reshape.18
  1074.0 2.2 collective-permute-start.3
  1076.2 6.6 maximum_convert_fusion
  1082.8 1.5 collective-permute-start.4
  1084.3 3.3 maximum_convert_fusion.2
  1091.6 2.0 maximum_convert_fusion.3
  1093.5 41.3 %reduce-scatter.17.cloned.1.call-done = bf16[256,1536]{1,0:T(8,128)(2,1)} async-done(((bf16[2048,1536]{1,0:T(8,128)(2,1)}), bf16[256,1536]{1,0:T(8,128)(2,1)}) %reduce-scatter.17.cloned.1.call-update) | async-done | bytes 786448 | tf_op jit(solution)/shard_map/reduce_scatter | solution.py:1171
  1134.8 2.3 copy.49
  1137.1 1.6 maximum_convert_fusion.1
  1138.7 2.4 copy.51
  1141.0 2.5 copy.68
  (159 shorter events, 33.6 us)
Async XLA Ops:
  7.2 4.0 copy-start.12
  7.2 52.4 %all-gather.10.cloned.1.call-start = ((), (), s32[]{:S(2)}) async-start(), calls=%async_computation.8 | async-start | bytes 7077888 | tf_op jit(solution)/shard_map/all_gather | solution.py:1192
  11.1 153.6 %all-gather.24.cloned.1.call-start = ((), (), s32[]{:S(2)}) async-start(), calls=%async_computation.23 | async-start | bytes 2359296 | tf_op jit(solution)/shard_map/all_gather | solution.py:1192
  12.1 152.7 %all-gather.12.cloned.1.call-start = ((), (), s32[]{:S(2)}) async-start(), calls=%async_computation.9 | async-start | bytes 12976128 | tf_op jit(solution)/shard_map/all_gather | solution.py:1192
  16.8 1.5 copy-start.25
  18.1 232.5 %all-gather.14.cloned.1.call-start = ((), (), s32[]{:S(2)}) async-start(), calls=%async_computation.10 | async-start | bytes 6488064 | tf_op jit(solution)/shard_map/all_gather | solution.py:1192
  18.8 2.5 copy-start.1
  20.8 1.0 copy-start.3
  23.1 4.2 copy-start.14
  23.1 4.8 copy-start
  23.2 5.3 copy-start.5
  23.2 5.3 copy-start.15
  23.2 6.0 copy-start.16
  137.7 2.0 copy-start.7
  137.7 115.6 %all-gather.16.cloned.1.call-start = ((), (), s32[]{:S(2)}) async-start(), calls=%async_computation.11 | async-start | bytes 7077888 | tf_op jit(solution)/shard_map/all_gather | solution.py:1192
  160.5 199.4 %all-gather.18.cloned.1.call-start = ((), (), s32[]{:S(2)}) async-start(), calls=%async_computation.12 | async-start | bytes 2359296 | tf_op jit(solution)/shard_map/all_gather | solution.py:1192
  161.1 198.9 %all-gather.20.cloned.1.call-start = ((), (), s32[]{:S(2)}) async-start(), calls=%async_computation.13 | async-start | bytes 12976128 | tf_op jit(solution)/shard_map/all_gather | solution.py:1192
  161.8 288.4 %all-gather.22.cloned.1.call-start = ((), (), s32[]{:S(2)}) async-start(), calls=%async_computation.14 | async-start | bytes 6488064 | tf_op jit(solution)/shard_map/all_gather | solution.py:1192
  162.6 673.6 %reduce-scatter.9.cloned.1.call-start = ((), (), s32[]{:S(2)}) async-start(), calls=%async_computation.15 | async-start | bytes 12976128 | tf_op jit(solution)/shard_map/reduce_scatter | solution.py:1171
  567.7 1.2 copy-start.10
  567.7 375.4 %reduce-scatter.11.cloned.1.call-start = ((), (), s32[]{:S(2)}) async-start(), calls=%async_computation.16 | async-start | bytes 6488064 | tf_op jit(solution)/shard_map/reduce_scatter | solution.py:1171
  568.3 408.7 %reduce-scatter.15.cloned.1.call-start = ((), (), s32[]{:S(2)}) async-start(), calls=%async_computation.18 | async-start | bytes 2359296 | tf_op jit(solution)/shard_map/reduce_scatter | solution.py:1171
  666.7 6.4 copy-start.6
  673.0 3.0 copy-start.4
  673.0 4.1 copy-start.2
  673.0 304.0 %reduce-scatter.13.cloned.1.call-start = ((), (), s32[]{:S(2)}) async-start(), calls=%async_computation.17 | async-start | bytes 7077888 | tf_op jit(solution)/shard_map/reduce_scatter | solution.py:1171
  711.1 359.4 %reduce-scatter.21.cloned.1.call-start = ((), (), s32[]{:S(2)}) async-start(), calls=%async_computation.21 | async-start | bytes 12976128 | tf_op jit(solution)/shard_map/reduce_scatter | solution.py:1171
  835.5 248.8 %reduce-scatter.23.cloned.1.call-start = ((), (), s32[]{:S(2)}) async-start(), calls=%async_computation.22 | async-start | bytes 6488064 | tf_op jit(solution)/shard_map/reduce_scatter | solution.py:1171
  836.1 255.5 %reduce-scatter.19.cloned.1.call-start = ((), (), s32[]{:S(2)}) async-start(), calls=%async_computation.20 | async-start | bytes 2359296 | tf_op jit(solution)/shard_map/reduce_scatter | solution.py:1171
  836.2 101.0 %copy-start.26 = (bf16[1024,512]{1,0:T(8,128)(2,1)S(1)}, bf16[1024,512]{1,0:T(8,128)(2,1)}, u32[]{:S(2)}) copy-start(bf16[1024,512]{1,0:T(8,128)(2,1)} %get-tuple-element.84.attended) | copy-start | bytes 3145732
  943.0 191.8 %reduce-scatter.17.cloned.1.call-start = ((), (), s32[]{:S(2)}) async-start(), calls=%async_computation.19 | async-start | bytes 7077888 | tf_op jit(solution)/shard_map/reduce_scatter | solution.py:1171
  976.1 0.7 copy-start.23
  976.1 0.7 copy-start.17
  976.1 0.7 copy-start.18
  976.1 0.8 copy-start.19
  976.1 0.8 copy-start.20
  976.1 0.9 copy-start.24
  977.1 49.4 %copy-start.21 = (f32[1,2048]{1,0:T(1,128)S(1)}, f32[1,2048]{1,0:T(1,128)}, u32[]{:S(2)}) copy-start(f32[1,2048]{1,0:T(1,128)} %get-tuple-element.136) | copy-start | bytes 24580
  977.1 49.4 %copy-start.22 = (f32[1,2048]{1,0:T(1,128)S(1)}, f32[1,2048]{1,0:T(1,128)}, u32[]{:S(2)}) copy-start(f32[1,2048]{1,0:T(1,128)} %get-tuple-element.138) | copy-start | bytes 24580
  977.1 93.1 %copy-start.9 = (bf16[256,2816]{1,0:T(8,128)(2,1)S(1)}, bf16[256,2816]{1,0:T(8,128)(2,1)}, u32[]{:S(2)}) copy-start(bf16[256,2816]{1,0:T(8,128)(2,1)} %reduce-scatter.9.cloned.1.call-done) | copy-start | bytes 4325380
  1027.3 34.1 %collective-permute-start = (f32[2,7,2048]{2,1,0:T(8,128)S(1)}, f32[2,7,2048]{2,1,0:T(8,128)S(1)}, u32[]{:S(2)}, u32[]{:S(2)}) collective-permute-start(f32[2,7,2048]{2,1,0:T(8,128)S(1)} %pad_maximum_fusion), channel_id=1, source_target_pairs={{0,4},{4,0},{8,12},{12,8},{16,20},{20,16},{24,28},{28,24},{1,5},{5... | collective-permute-start | bytes 344072 | tf_op jit(solution)/shard_map/ppermute | solution.py:1165
  1061.5 7.1 collective-permute-start.1
  1068.6 5.3 collective-permute-start.2
  1074.0 8.8 collective-permute-start.3
  1082.8 4.9 copy-start.11
  1082.8 7.4 collective-permute-start.4
  1084.3 7.2 copy-start.13
  1141.0 2.5 copy-start.8
Sparse Core Ops, SparseCore 0:
  11.3 48.2 all-gather.9
  61.4 28.1 all-gather.23
  92.1 67.7 all-gather.11
  161.7 44.3 all-gather.13
  207.8 45.5 all-gather.15
  255.1 28.2 all-gather.17
  285.8 67.8 all-gather.19
  355.6 44.4 all-gather.21
  567.8 127.1 reduce-scatter.8
  698.9 59.0 reduce-scatter.10
  762.2 41.2 reduce-scatter.14
  806.7 61.7 reduce-scatter.12
  872.4 87.3 reduce-scatter.20
  963.4 59.0 reduce-scatter.22
  1025.7 42.5 reduce-scatter.18
  1071.9 62.8 reduce-scatter.16

commit v4 on v3

--- a/solution.py
+++ b/solution.py
@@ -28,6 +28,158 @@
 
 def matmul(left, right, dims=rows_cols):
     return lax.dot_general(left, right, dims, preferred_element_type=F32)
+
+
+def member_at(member, step):
+    bit = 1
+    while bit <= step:
+        if step & bit:
+            member = member + bit * (1 - 2 * ((member // bit) % 2))
+        bit *= 2
+    return member
+
+
+class Whole:
+    def __init__(self, held, size, send_sem, recv_sem):
+        self.held, self.size, self.send_sem, self.recv_sem = held, size, send_sem, recv_sem
+        self.member = lax.axis_index("dp")
+        self.share = held.shape[0] // size
+        self.evens = range(0, size, 2)
+
+    def peers(self):
+        return tuple(member_at(self.member, step) for step in self.evens if step) + (
+            member_at(self.member, 1),
+        )
+
+    def rows(self, step):
+        start = member_at(self.member, step) * self.share
+        return pl.ds(pl.multiple_of(start, self.share), self.share)
+
+    def hop(self, source_step, target_step, number):
+        return pltpu.make_async_remote_copy(
+            src_ref=self.held.at[self.rows(source_step)],
+            dst_ref=self.held.at[self.rows(source_step)],
+            send_sem=self.send_sem.at[number],
+            recv_sem=self.recv_sem.at[number],
+            device_id={"dp": member_at(self.member, target_step)},
+            device_id_type=MESH,
+        )
+
+    def to_chips(self, step):
+        return self.hop(0, step, step)
+
+    def to_core(self, step):
+        return self.hop(step, 1, step + 1)
+
+    def start(self):
+        for step in self.evens:
+            if step:
+                self.to_chips(step).start()
+        self.to_core(0).start()
+
+    def pass_on(self):
+        for step in self.evens:
+            if step:
+                self.to_chips(step).wait_recv()
+                self.to_core(step).start()
+
+    def wait(self):
+        for step in self.evens:
+            self.to_core(step).wait_recv()
+
+    def drain(self):
+        for step in self.evens:
+            if step:
+                self.to_chips(step).wait_send()
+            self.to_core(step).wait_send()
+
+
+class Owned:
+    def __init__(self, part, size, mine, swapped, landed, load_sem, sems):
+        self.part, self.mine, self.swapped, self.landed = part, mine, swapped, landed
+        self.load_sem, (self.swap_send, self.swap_recv, self.send_sem, self.recv_sem) = load_sem, sems
+        self.member = lax.axis_index("dp")
+        self.share = part.shape[0] // size
+        self.chips = range(size // 2)
+
+    def peers(self):
+        return tuple(member_at(self.member, 2 * chip) for chip in self.chips if chip) + (
+            member_at(self.member, 1),
+        )
+
+    def rows(self, step):
+        return pl.ds(pl.multiple_of(member_at(self.member, step) * self.share, self.share), self.share)
+
+    def load(self, chip):
+        return pltpu.make_async_copy(
+            self.part.at[self.rows(2 * chip)], self.mine.at[chip], self.load_sem.at[chip]
+        )
+
+    def swap(self, chip):
+        return pltpu.make_async_remote_copy(
+            src_ref=self.part.at[self.rows(2 * chip + 1)],
+            dst_ref=self.swapped.at[chip],
+            send_sem=self.swap_send.at[chip],
+            recv_sem=self.swap_recv.at[chip],
+            device_id={"dp": member_at(self.member, 1)},
+            device_id_type=MESH,
+        )
+
+    def hop(self, chip):
+        return pltpu.make_async_remote_copy(
+            src_ref=self.mine.at[chip],
+            dst_ref=self.landed.at[chip - 1],
+            send_sem=self.send_sem.at[chip],
+            recv_sem=self.recv_sem.at[chip],
+            device_id={"dp": member_at(self.member, 2 * chip)},
+            device_id_type=MESH,
+        )
+
+    def each_rows(self, run):
+        def one(number, carry):
+            run(pl.ds(pl.multiple_of(number * 16, 16), 16))
+            return carry
+
+        lax.fori_loop(0, self.share // 16, one, 0)
+
+    def start(self):
+        for chip in self.chips:
+            self.swap(chip).start()
+            self.load(chip).start()
+
+    def across_chips(self, total):
+        for chip in (*self.chips[1:], 0):
+            self.load(chip).wait()
+            self.swap(chip).wait_recv()
+
+            def rows(at):
+                both = self.mine[chip, at, :].astype(F32) + self.swapped[chip, at, :].astype(F32)
+                if chip:
+                    self.mine[chip, at, :] = both.astype(BF16)
+                else:
+                    total[at, :] = both
+
+            self.each_rows(rows)
+            if chip:
+                self.hop(chip).start()
+
+    def finish(self, total):
+        for chip in self.chips[1:]:
+            self.hop(chip).wait_recv()
+
+        def rows(at):
+            values = total[at, :]
+            for chip in self.chips[1:]:
+                values = values + self.landed[chip - 1, at, :].astype(F32)
+            total[at, :] = values
+
+        self.each_rows(rows)
+
+    def drain(self):
+        for chip in self.chips:
+            self.swap(chip).wait_send()
+            if chip:
+                self.hop(chip).wait_send()
 
 
 def line_barrier(place, count, others=()):
@@ -188,7 +340,7 @@
 
         self.chunks(rows)
 
-    def run(self, term, finish, process, each_tick=None):
+    def run(self, term, finish, process, each_tick=None, delay=0):
         count, pieces, place = self.count, self.pieces, self.place
         scatter, gather = term is not None, process is not None
         lead = count - 1 if scatter else 0
@@ -262,13 +414,13 @@
 
             if gather:
 
-                @pl.when(valid(mine - (count - 1)))
+                @pl.when(valid(mine - (count - 1) - delay))
                 def _():
-                    process(mine - (count - 1))
+                    process(mine - (count - 1) - delay)
 
             return carry
 
-        lax.fori_loop(0, pieces + lead + (count - 1 if gather else 0), tick, 0)
+        lax.fori_loop(0, pieces + lead + (count - 1 + delay if gather else 0), tick, 0)
 
     def drain(self):
         def piece_sends(piece, carry):
@@ -395,6 +547,9 @@
     cos, sin_up, sin_down = tables
     width = mixed.shape[3]
 
+    def factor(table, rows, size):
+        return jnp.concatenate([flat_rows(table, rows)] * (size // PAIR), axis=1)
+
     def process(piece):
         rows = line.at(piece)
 
@@ -404,9 +559,9 @@
                 result = matmul(flat_rows(line.held, rows), weight[:, source]) + bias[:, source]
                 if kind < 2:
                     result = (
-                        result * flat_rows(cos, rows, slice(0, size))
-                        + pltpu.roll(result, size - ROT // 2, 1) * flat_rows(sin_up, rows, slice(0, size))
-                        + pltpu.roll(result, ROT // 2, 1) * flat_rows(sin_down, rows, slice(0, size))
+                        result * factor(cos, rows, size)
+                        + pltpu.roll(result, size - ROT // 2, 1) * factor(sin_up, rows, size)
+                        + pltpu.roll(result, ROT // 2, 1) * factor(sin_down, rows, size)
                     )
                 if kind == 0:
                     result = result * (1.0 / math.sqrt(HD))
@@ -517,7 +672,7 @@
 def add_and_norm(line, before, gain, shift, after):
     def finish(piece):
         def rows(at, total):
-            hidden = before[at, :] + total
+            hidden = before[at, :].astype(F32) + total
             after[at, :] = hidden
             scaled, _ = norm_rows(hidden)
             line.held[line.place, at, :] = (scaled * gain[...] + shift[...]).astype(BF16)
@@ -533,11 +688,11 @@
 
     def finish(piece):
         def rows(at, grad_normed):
-            scaled, inverse = norm_rows(hidden[at, :])
+            scaled, inverse = norm_rows(hidden[at, :].astype(F32))
             weighted = grad_normed * gain[...]
             first = jnp.mean(weighted, axis=-1, keepdims=True)
             second = jnp.mean(weighted * scaled, axis=-1, keepdims=True)
-            result = grad[at, :] + inverse * (weighted - first - scaled * second)
+            result = grad[at, :].astype(F32) + inverse * (weighted - first - scaled * second)
             out[at, :] = result
             if line.held is not None:
                 line.held[line.place, at, :] = result.astype(BF16)
@@ -557,55 +712,78 @@
     return parts
 
 
-def first_kernel(count, pieces, *refs):
-    (own, weight, bias, *tables), (rows_out, mixed_out), gather, rest = split(refs, 6, 2, 3, 4)
-    weight_held, mixed, load_sem, save_sem = rest
+def first_kernel(count, pieces, size, *refs):
+    (own, gain, shift, share, bias, *tables), outs, gather, rest = split(refs, 8, 3, 3, 6)
+    rows_out, mixed_out, weight_out = outs
+    weight_held, mixed, load_sem, save_sem, weight_send, weight_recv = rest
     line = Line(count, pieces, None, None, None, None, None, *gather)
-    loads = Loads([(weight, weight_held)], load_sem)
-    line_barrier(line.place, count)
+    weight = Whole(weight_held, size, weight_send, weight_recv)
+    load = pltpu.make_async_copy(share, weight_held.at[weight.rows(0)], load_sem.at[0])
+    keep = pltpu.make_async_copy(weight_held, weight_out, load_sem.at[1])
+    load.start()
+    line_barrier(line.place, count, weight.peers())
     saves = Saves([(line.held, rows_out), (mixed, mixed_out)], save_sem, line)
     compute = query_key_value(line, weight_held, bias, tables, mixed)
+    load.wait()
+    weight.start()
 
     def finish(piece):
-        rows = line.at(piece)
-        line.held[line.place, rows, :] = own[rows, :]
+        first_row = pl.multiple_of(piece * line.rows, line.rows)
+
+        def rows(start, size):
+            at = pl.ds(pl.multiple_of(first_row + start, size), size)
+            scaled, _ = norm_rows(own[at, :].astype(F32))
+            line.held[line.place, at, :] = (scaled * gain[...] + shift[...]).astype(BF16)
+
+        line.chunks(rows)
+
+    def each_tick(number):
+        @pl.when(number == count - 1)
+        def _():
+            weight.pass_on()
 
     def process(piece):
         @pl.when(piece == 0)
         def _():
-            loads.wait(0)
+            weight.wait()
+            keep.start()
 
         compute(piece)
         saves.start(piece)
 
-    line.run(None, finish, process)
-
+    line.run(None, finish, process, each_tick, 2)
     line.drain()
+    weight.drain()
+    keep.wait()
     saves.wait()
 
 
-def first(count, own, weight, bias, tables, width):
+def first(count, own, gain, shift, share, bias, tables, width):
     rows, depth = own.shape
     pieces = pieces_of(rows)
+    size = lax.axis_size("dp")
     return line_call(
-        functools.partial(first_kernel, count, pieces),
+        functools.partial(first_kernel, count, pieces, size),
         (
             jax.ShapeDtypeStruct((count, rows, depth), BF16),
             jax.ShapeDtypeStruct((3, count, rows, width), BF16),
+            jax.ShapeDtypeStruct((depth, 3 * width), BF16),
         ),
-        (hbm, hbm),
-        [vmem, hbm, vmem, vmem, vmem, vmem],
+        (hbm, hbm, hbm),
+        [vmem, vmem, vmem, hbm, vmem, vmem, vmem, vmem],
         gather_scratch(count, pieces, rows, depth)
         + [
-            pltpu.VMEM(weight.shape, BF16),
+            pltpu.VMEM((depth, 3 * width), BF16),
             pltpu.VMEM((3, count, rows, width), BF16),
-            pltpu.SemaphoreType.DMA((1,)),
+            pltpu.SemaphoreType.DMA((2,)),
             pltpu.SemaphoreType.DMA((2, pieces)),
+            pltpu.SemaphoreType.DMA((size,)),
+            pltpu.SemaphoreType.DMA((size,)),
         ],
         0,
-        2 * count * rows * weight.size,
-        weight.size * 2 + own.size * 2 * count * 4,
-    )(own, weight, bias, *tables)
+        6 * count * rows * depth * width,
+        depth * width * 6 + own.size * 2 * count * 4,
+    )(own, gain, shift, share, bias, *tables)
 
 
 def middle_kernel(count, pieces, lag, *refs):
@@ -863,7 +1041,7 @@
             pltpu.SemaphoreType.DMA((3,)),
             pltpu.SemaphoreType.DMA((2, pieces)),
         ],
-        4,
+        4 if grad.dtype == F32 else 8,
         2 * count * rows * (w_up.size + w_out.size),
         (w_up.size + w_out.size) * 2 + grad.size * 60,
     )(source, w_up, grad, hidden, gain, w_out)
@@ -940,44 +1118,64 @@
     )(source, weight, grad, hidden, gain, w_down, slope, silu)
 
 
-def last_kernel(count, pieces, *refs):
-    ins, outs, scatter, rest = split(refs, 5, 3, 5, 3)
-    source, weight, grad, hidden, gain = ins
-    source_held, weight_held, load_sem = rest
+def last_kernel(count, pieces, size, *refs):
+    ins, outs, scatter, rest = split(refs, 6, 4, 5, 11)
+    source, weight, grad, hidden, gain, part = ins
+    *outs, owned_out = outs
+    source_held, weight_held, load_sem, mine, swapped, landed, part_sem, *sems = rest
     line = Line(count, pieces, *scatter, None, None, None)
+    owned = Owned(part, size, mine, swapped, landed, part_sem, sems)
     loads = Loads([(source, source_held), (weight, weight_held)], load_sem)
-    line_barrier(line.place, count)
+    line_barrier(line.place, count, owned.peers())
+    owned.start()
+
+    def each_tick(number):
+        @pl.when(number == 1)
+        def _():
+            owned.across_chips(owned_out)
+
     loads.wait(0, 1)
     line.run(
         share_transposed(line, [source_held.at[kind] for kind in range(3)], weight_held),
         norm_backward(line, grad, hidden, gain, *outs),
         None,
+        each_tick,
     )
     line.drain()
-
-
-def last(count, source, weight, grad, hidden, gain):
+    owned.finish(owned_out)
+    owned.drain()
+
+
+def last(count, source, weight, grad, hidden, gain, part):
     rows, depth = grad.shape
     pieces = pieces_of(rows)
+    size = lax.axis_size("dp")
+    share, width = part.shape[0] // size, part.shape[1]
     return line_call(
-        functools.partial(last_kernel, count, pieces),
+        functools.partial(last_kernel, count, pieces, size),
         (
             jax.ShapeDtypeStruct((rows, depth), F32),
             jax.ShapeDtypeStruct((1, depth), F32),
             jax.ShapeDtypeStruct((1, depth), F32),
+            jax.ShapeDtypeStruct((share, width), F32),
         ),
-        (vmem, vmem, vmem),
-        [hbm, hbm, vmem, vmem, vmem],
+        (vmem, vmem, vmem, vmem),
+        [hbm, hbm, vmem, vmem, vmem, hbm],
         scatter_scratch(count, pieces, rows, depth)
         + [
             pltpu.VMEM(source.shape, BF16),
             pltpu.VMEM(weight.shape, BF16),
             pltpu.SemaphoreType.DMA((2,)),
-        ],
+            pltpu.VMEM((size // 2, share, width), BF16),
+            pltpu.VMEM((size // 2, share, width), BF16),
+            pltpu.VMEM((size // 2 - 1, share, width), BF16),
+            pltpu.SemaphoreType.DMA((size // 2,)),
+        ]
+        + [pltpu.SemaphoreType.DMA((size // 2,))] * 4,
         6,
         2 * count * rows * weight.size,
         weight.size * 2 + grad.size * 20,
-    )(source, weight, grad, hidden, gain)
+    )(source, weight, grad, hidden, gain, part)
 
 
 def usable(first, start, keys, queries):
@@ -1138,19 +1336,16 @@
     )(positions, mixed, mixed, mixed, attended, grad_attended, logsums, *tables)
 
 
-def rotary_tables(positions, width):
+def rotary_tables(positions):
     half_rot = ROT // 2
-    frequency = jnp.exp(-(jnp.arange(half_rot, dtype=F32) * 2.0 / ROT) * theta_log)
+    lane = jnp.arange(PAIR, dtype=jnp.int32) % HD
+    frequency = jnp.exp(-((lane % half_rot).astype(F32) * 2.0 / ROT) * theta_log)
     angles = positions.astype(F32)[:, None] * frequency[None, :]
     cos, sin = jnp.cos(angles), jnp.sin(angles)
-    length = positions.shape[0]
-    rest = jnp.ones((length, HD - ROT), F32)
-    none, gap = jnp.zeros((length, half_rot), F32), jnp.zeros((length, HD - ROT), F32)
-    copies = width // HD
     return (
-        jnp.tile(jnp.concatenate([cos, cos, rest], axis=1), (1, copies)),
-        jnp.tile(jnp.concatenate([-sin, none, gap], axis=1), (1, copies)),
-        jnp.tile(jnp.concatenate([none, sin, gap], axis=1), (1, copies)),
+        jnp.where(lane < ROT, cos, 1.0),
+        jnp.where(lane < half_rot, -sin, 0.0),
+        jnp.where((lane >= half_rot) & (lane < ROT), sin, 0.0),
     )
 
 
@@ -1184,8 +1379,7 @@
     ff_local = w_gate_up.shape[3]
     rows, depth = tokens.shape
     length = positions.shape[0]
-    tables = rotary_tables(positions, min(256, width))
-    pair_tables = tuple(table[:, :PAIR] for table in tables)
+    tables = rotary_tables(positions)
     positions_row = positions.reshape(1, length)
 
     def whole(weight, axis):
@@ -1201,16 +1395,16 @@
         for layer in range(LAYERS)
     ]
     axes = (0, 1, 0, 1)
-    gathered = [[whole(flat[0][kind], axes[kind]) for kind in range(3)] + [None]]
-    hidden = tokens.astype(F32)
-    scaled, _ = norm_rows(hidden)
-    normed = (scaled * norm_gain[0, 0] + norm_bias[0, 0]).astype(BF16)
+    gathered = [[None, whole(flat[0][1], axes[1]), whole(flat[0][2], axes[2]), None]]
+    hidden = tokens
     block_tables = tuple(table.reshape(count, rows, -1) for table in tables)
     biases = [
         lax.dynamic_slice_in_dim(b_qkv[layer], tensor_rank * width, width, 1).reshape(1, 3 * width)
         for layer in range(LAYERS)
     ]
-    rows_a, mixed = first(count, normed, gathered[0][0], biases[0], block_tables, width)
+    rows_a, mixed, gathered[0][0] = first(
+        count, tokens, norm_gain[0, 0:1], norm_bias[0, 0:1], flat[0][0], biases[0], block_tables, width
+    )
     mixed, flat[0][3] = after(mixed, flat[0][3])
     gathered[0][3] = whole(flat[0][3], axes[3])
     kept = []
@@ -1248,7 +1442,7 @@
             activations, grad_rows_b, wide = turn(
                 count, act, full_down, hidden_mid, cotangent, slope, silu
             )
-    grad = cotangent.astype(F32)
+    grad = cotangent
     scattered = [None] * LAYERS
     small = [None] * LAYERS
     for layer in reversed(range(LAYERS)):
@@ -1274,12 +1468,13 @@
         if later:
             grad_attended, later[3] = after(grad_attended, later[3])
         grad_mixed, bias_sum = attend_backward(
-            mixed, positions_row, attended, grad_attended.reshape(length, width), logsums, pair_tables
+            mixed, positions_row, attended, grad_attended.reshape(length, width), logsums, tables
         )
         flat_mixed = grad_mixed.transpose(1, 0, 2).reshape(length, 3 * width)
         qkv_part = matmul(rows_a.reshape(length, depth), flat_mixed, rows_rows).astype(BF16)
         grad_mixed, qkv_part = after(grad_mixed, qkv_part)
-        qkv_grad = owner_sum(qkv_part, 0)
+        if layer:
+            qkv_grad = owner_sum(qkv_part, 0)
         if later:
             grad_mixed, later[0], later[1] = after(grad_mixed, later[0], later[1])
         source = grad_mixed.reshape(3, count, rows, width)
@@ -1297,7 +1492,9 @@
                 below[9],
             )
         else:
-            grad, gain_a, shift_a = last(count, source, full_qkv, grad, hidden, norm_gain[layer, 0:1])
+            grad, gain_a, shift_a, qkv_grad = last(
+                count, source, full_qkv, grad, hidden, norm_gain[layer, 0:1], qkv_part
+            )
         bias_full = lax.dynamic_update_slice(
             jnp.zeros((3, b_qkv.shape[2]), F32), bias_sum, (jnp.int32(0), tensor_rank * width)
         )

time: 1160 us -> 1140 us (0.983)
  Pallas kernels: 846 us -> 937 us
  waiting for transfers between devices: 81 us -> 7.75 us
  starting transfers between devices: 41.4 us -> 11.3 us
  local copies, waits for them, and re-layouts: 56.3 us -> 42.5 us
    pallas_call x2, Pallas kernels: 128 us -> 217 us  [the longest x1 109 us: last(): line_call(functools.partial(last_kernel, count, pieces, size), (jax.Shape...]
    reduce_scatter x8 -> x7, waiting for transfers between devices: 41.4 us -> 0.05 us  [owner_sum(): return lax.psum_scatter(part, 'dp', scatter_dimension=axis, tiled=True)]
    ppermute x5, starting transfers between devices: 40.1 us -> 10.7 us  [all_sum(): lax.ppermute(values, axis, [(i, i ^ step) for i in range(size)])]
    all_gather x8 -> x7, waiting for transfers between devices: 28.6 us -> 0.08 us  [whole(): return lax.all_gather(weight, 'dp', axis=axis, tiled=True)]
  transfers between devices with their start and end apart: 21 -> 19, of which waited for: 7 -> 3; matrix products, arithmetic and copies ran while one was open for 11% -> 11% of each run, Pallas kernels for 66% -> 75%
where the time goes in v4:
time: 1140 us; the launch traced here: 1130 us
  Pallas kernels  937 us (82%)
  matrix products  92.4 us (8%)
  local copies, waits for them, and re-layouts  42.5 us (4%)
  other arithmetic  21.9 us (2%)
  between operations  14.9 us (1%)
    pallas_call x2, Pallas kernels, middle_back(): line_call(functools.partial(middle_back_kernel, count, pieces), (jax.Shap...  197 us
    pallas_call x2, Pallas kernels, middle(): line_call(functools.partial(middle_kernel, count, pieces, lag), (jax.Shap...  173 us
    pallas_call x1, Pallas kernels, last(): line_call(functools.partial(last_kernel, count, pieces, size), (jax.Shape...  109 us
    pallas_call x1, Pallas kernels, first(): line_call(functools.partial(first_kernel, count, pieces, size), (jax.Shap...  107 us
    pallas_call x1, Pallas kernels, between_back(): line_call(functools.partial(between_back_kernel, count, pieces), (jax.Sha...  98.8 us
    dot_general x8, matrix products, matmul(): return lax.dot_general(left, right, dims, preferred_element_type=F32)  92.4 us
    pallas_call x1, Pallas kernels, turn(): line_call(functools.partial(turn_kernel, count, pieces), (jax.ShapeDtypeS...  89.1 us
    pallas_call x1, Pallas kernels, between(): line_call(functools.partial(between_kernel, count, pieces), (jax.ShapeDty...  87.5 us
  transfers between devices with their start and end apart: 19, of which 3 were waited for; matrix products, arithmetic and copies ran while one was open for 11% of the time, Pallas kernels for 75%

profile of v4, /device:TPU:0, one launch (start us, length us, event | category | flops | bytes accessed | tf_op | source)
XLA Modules:
  0.0 1127.2 jit_solution(5412289695633269455)
XLA Ops:
  7.2 1.9 fusion.17
  9.1 3.7 fusion.15
  12.9 1.3 copy.51
  14.2 2.7 fusion.16
  16.9 1.4 copy.48
  20.2 3.2 fusion
  24.1 2.5 slice_bitcast_fusion
  26.6 107.5 %shard_map.169 = (bf16[4,256,2048]{2,1,0:T(8,128)(2,1)}, bf16[3,4,256,512]{3,2,1,0:T(8,128)(2,1)}, bf16[2048,1536]{1,0:T(8,128)(2,1)}) custom-call(bf16[256,2048]{1,0:T(8,128)(2,1)} %refs_3_.3, f32[1,2048]{1,0:T(1,128)} %get-tuple-element.204.refs_1_.refs_4_, f32[1,2048]{1,0:T(1,128)} %get-tuple-element.189.refs_2_, bf16[256,1536]{1,0:T(8,128)(2,1)} %copy.31.refs_3_, ...), custom_call_target="tpu_custom_call" | custom-call | flops 6442450944 | bytes 23068672 | tf_op jit(solution)/shard_map/pallas_call | solution.py:765
  134.1 2.3 copy.49
  137.7 18.5 %shard_map.170 = (bf16[1024,512]{1,0:T(8,128)(2,1)}, f32[4,2,1024]{2,1,0:T(2,128)}) custom-call(s32[1,1024]{1,0:T(1,128)} %bitcast.108, bf16[3,1024,512]{2,1,0:T(8,128)(2,1)} %bitcast.118, bf16[3,1024,512]{2,1,0:T(8,128)(2,1)} %bitcast.119, bf16[3,1024,512]{2,1,0:T(8,128)(2,1)} %bitcast.120), custom_call_target="tpu_custom_call" | custom-call | flops 4294967296 | bytes 4194304 | tf_op jit(solution)/shard_map/pallas_call | solution.py:1222
  160.0 85.3 %shard_map.171 = (f32[256,2048]{1,0:T(8,128)}, bf16[4,256,2048]{2,1,0:T(8,128)(2,1)}, bf16[4,256,1408]{2,1,0:T(8,128)(2,1)}, bf16[4,256,1408]{2,1,0:T(8,128)(2,1)}, bf16[4,256,1408]{2,1,0:T(8,128)(2,1)}) custom-call(bf16[4,256,512]{2,1,0:T(8,128)(2,1)} %bitcast.130, bf16[512,2048]{1,0:T(8,128)(2,1)} %bitcast.112, bf16[256,2048]{1,0:T(8,128)(2,1)} %refs_3_.3, ...), custom_call_target="tpu_custom_call" | custom-call | flops 13958643712 | bytes 45088768 | tf_op jit(solution)/shard_map/pallas_call | solution.py:840
  245.4 87.5 %shard_map.172 = (f32[256,2048]{1,0:T(8,128)}, bf16[4,256,2048]{2,1,0:T(8,128)(2,1)}, bf16[3,4,256,512]{3,2,1,0:T(8,128)(2,1)}) custom-call(bf16[4,256,1408]{2,1,0:T(8,128)(2,1)} %get-tuple-element.87.refs_0_, bf16[1408,2048]{1,0:T(8,128)(2,1)} %all-gather.11.cloned.1.call-done.refs_1_.refs_5_, f32[256,2048]{1,0:T(8,128)} %get-tuple-element.89.refs_2_.refs_3_, ...), custom_call_target="tpu_custom_call" | custom-call | flops 12348030976 | bytes 43515904 | tf_op jit(solution)/shard_map/pallas_call | solution.py:901
  332.8 18.5 %shard_map.173 = (bf16[1024,512]{1,0:T(8,128)(2,1)}, f32[4,2,1024]{2,1,0:T(2,128)}) custom-call(s32[1,1024]{1,0:T(1,128)} %bitcast.109, bf16[3,1024,512]{2,1,0:T(8,128)(2,1)} %bitcast.124, bf16[3,1024,512]{2,1,0:T(8,128)(2,1)} %bitcast.125, bf16[3,1024,512]{2,1,0:T(8,128)(2,1)} %bitcast.126), custom_call_target="tpu_custom_call" | custom-call | flops 4294967296 | bytes 4194304 | tf_op jit(solution)/shard_map/pallas_call | solution.py:1222
  351.3 87.3 %shard_map.174 = (f32[256,2048]{1,0:T(8,128)}, bf16[4,256,2048]{2,1,0:T(8,128)(2,1)}, bf16[4,256,1408]{2,1,0:T(8,128)(2,1)}, bf16[4,256,1408]{2,1,0:T(8,128)(2,1)}, bf16[4,256,1408]{2,1,0:T(8,128)(2,1)}) custom-call(bf16[4,256,512]{2,1,0:T(8,128)(2,1)} %bitcast.131, bf16[512,2048]{1,0:T(8,128)(2,1)} %all-gather.15.cloned.1.call-done.refs_1_.refs_5_, ...), custom_call_target="tpu_custom_call" | custom-call | flops 13958643712 | bytes 45088768 | tf_op jit(solution)/shard_map/pallas_call | solution.py:840
  438.7 89.1 %shard_map.175 = (bf16[256,2048]{1,0:T(8,128)(2,1)}, bf16[4,256,2048]{2,1,0:T(8,128)(2,1)}, bf16[4,256,2816]{2,1,0:T(8,128)(2,1)}) custom-call(bf16[4,256,1408]{2,1,0:T(8,128)(2,1)} %get-tuple-element.96.refs_0_, bf16[1408,2048]{1,0:T(8,128)(2,1)} %all-gather.19.cloned.1.call-done.refs_1_, f32[256,2048]{1,0:T(8,128)} %get-tuple-element.98.refs_2_.refs_3_, ...), custom_call_target="tpu_custom_call" | custom-call | flops 11811160064 | bytes 37224448 | tf_op jit(solution)/shard_map/pallas_call | solution.py:964
  527.8 10.5 bitcast_convert_fusion.3
  538.3 18.2 %bitcast_convert_fusion.1 = bf16[2048,2816]{1,0:T(8,128)(2,1)} fusion(bf16[4,256,2048]{2,1,0:T(8,128)(2,1)} %get-tuple-element.104, bf16[4,256,2816]{2,1,0:T(8,128)(2,1)} %get-tuple-element.105.refs_0_), kind=kOutput, calls=%fused_computation.1 | convolution fusion | flops 11816927232 | bytes 21495808 | tf_op jit(solution)/shard_map/dot_general | solution.py:30
  557.3 96.5 %shard_map.176 = (f32[256,2048]{1,0:T(8,128)}, f32[1,2048]{1,0:T(1,128)}, f32[1,2048]{1,0:T(1,128)}, bf16[4,256,2048]{2,1,0:T(8,128)(2,1)}, bf16[4,256,512]{2,1,0:T(8,128)(2,1)}) custom-call(bf16[4,256,2816]{2,1,0:T(8,128)(2,1)} %get-tuple-element.105.refs_0_, bf16[2048,2816]{1,0:T(8,128)(2,1)} %all-gather.17.cloned.1.call-done.refs_5_.refs_1_, ...), custom_call_target="tpu_custom_call" | custom-call | flops 13958643712 | bytes 45088768 | tf_op jit(solution)/shard_map/pallas_call | solution.py:1023
  653.8 5.9 convolution_convert_fusion.3
  659.8 3.2 fusion.2
  663.0 19.1 %shard_map.177 = (bf16[3,1024,512]{2,1,0:T(8,128)(2,1)}, f32[3,512]{1,0:T(4,128)}) custom-call(s32[1,1024]{1,0:T(1,128)} %bitcast.110, bf16[3,1024,512]{2,1,0:T(8,128)(2,1)} %bitcast.127, bf16[3,1024,512]{2,1,0:T(8,128)(2,1)} %bitcast.128, bf16[3,1024,512]{2,1,0:T(8,128)(2,1)} %bitcast.129, bf16[1024,512]{1,0:T(8,128)(2,1)} %get-tuple-element.92.attended, ...), custom_call_target="tpu_custom_call" | custom-call | flops 10737418240 | bytes 8388608 | tf_op jit(solution)/shard_map/pallas_call | solution.py:1306
  682.1 3.2 copy.36
  685.3 11.1 convolution_convert_fusion.1
  696.5 98.8 %shard_map.178 = (f32[256,2048]{1,0:T(8,128)}, f32[1,2048]{1,0:T(1,128)}, f32[1,2048]{1,0:T(1,128)}, bf16[4,256,2048]{2,1,0:T(8,128)(2,1)}, bf16[4,256,2816]{2,1,0:T(8,128)(2,1)}) custom-call(bf16[3,4,256,512]{3,2,1,0:T(8,128)(2,1)} %bitcast.91, bf16[2048,1536]{1,0:T(8,128)(2,1)} %all-gather.13.cloned.1.call-done.refs_5_.refs_1_, ...), custom_call_target="tpu_custom_call" | custom-call | flops 12348030976 | bytes 43515904 | tf_op jit(solution)/shard_map/pallas_call | solution.py:1092
  795.2 10.5 bitcast_convert_fusion.2
  805.7 19.2 %bitcast_convert_fusion = bf16[2048,2816]{1,0:T(8,128)(2,1)} fusion(bf16[4,256,2048]{2,1,0:T(8,128)(2,1)} %get-tuple-element.118, bf16[4,256,2816]{2,1,0:T(8,128)(2,1)} %get-tuple-element.121.refs_0_), kind=kOutput, calls=%fused_computation | convolution fusion | flops 11816927232 | bytes 21495808 | tf_op jit(solution)/shard_map/dot_general | solution.py:30
  826.0 100.5 %shard_map.179 = (f32[256,2048]{1,0:T(8,128)}, f32[1,2048]{1,0:T(1,128)}, f32[1,2048]{1,0:T(1,128)}, bf16[4,256,2048]{2,1,0:T(8,128)(2,1)}, bf16[4,256,512]{2,1,0:T(8,128)(2,1)}) custom-call(bf16[4,256,2816]{2,1,0:T(8,128)(2,1)} %get-tuple-element.121.refs_0_, bf16[2048,2816]{1,0:T(8,128)(2,1)} %all-gather.9.cloned.1.call-done.refs_5_.refs_1_, ...), custom_call_target="tpu_custom_call" | custom-call | flops 13958643712 | bytes 45088768 | tf_op jit(solution)/shard_map/pallas_call | solution.py:1023
  926.6 5.9 convolution_convert_fusion.2
  932.5 18.7 %shard_map.180 = (bf16[3,1024,512]{2,1,0:T(8,128)(2,1)}, f32[3,512]{1,0:T(4,128)}) custom-call(s32[1,1024]{1,0:T(1,128)} %bitcast.111, bf16[3,1024,512]{2,1,0:T(8,128)(2,1)} %bitcast.121, bf16[3,1024,512]{2,1,0:T(8,128)(2,1)} %bitcast.122, bf16[3,1024,512]{2,1,0:T(8,128)(2,1)} %bitcast.123, bf16[1024,512]{1,0:T(8,128)(2,1)} %get-tuple-element.86.attended, ...), custom_call_target="tpu_custom_call" | custom-call | flops 10737418240 | bytes 8388608 | tf_op jit(solution)/shard_map/pallas_call | solution.py:1306
  951.2 3.2 copy.39
  954.4 11.1 convolution_convert_fusion.refs_5_
  965.6 109.3 %shard_map.181 = (f32[256,2048]{1,0:T(8,128)}, f32[1,2048]{1,0:T(1,128)}, f32[1,2048]{1,0:T(1,128)}, f32[256,1536]{1,0:T(8,128)}) custom-call(bf16[3,4,256,512]{3,2,1,0:T(8,128)(2,1)} %bitcast.89, bf16[2048,1536]{1,0:T(8,128)(2,1)} %get-tuple-element.135.refs_1_, f32[256,2048]{1,0:T(8,128)} %get-tuple-element.136.refs_2_, bf16[256,2048]{1,0:T(8,128)(2,1)} %refs_3_.3, ...), custom_call_target="tpu_custom_call" | custom-call | flops 6442450944 | bytes 16777216 | tf_op jit(solution)/shard_map/pallas_call | solution.py:1154
  1075.7 1.7 collective-permute-start
  1078.5 1.4 collective-permute-start.1
  1080.3 3.2 stack_reshape.20
  1085.3 2.2 collective-permute-start.2
  1087.6 6.2 maximum_convert_fusion
  1093.8 3.8 collective-permute-start.3
  1097.6 3.2 maximum_convert_fusion.1
  1100.8 1.4 copy.41
  1102.2 1.6 copy.40
  1103.9 1.6 collective-permute-start.4
  1105.5 2.1 pad_maximum_fusion
  1107.6 2.4 copy.42
  1109.9 2.5 collective-permute-done.4
  1114.7 2.0 maximum_convert_fusion.2
  1116.7 2.3 copy.56
  1119.0 1.3 copy.57
  (114 shorter events, 15.9 us)
Async XLA Ops:
  7.2 152.8 %all-gather.21.cloned.1.call-start = ((), (), s32[]{:S(2)}) async-start(), calls=%async_computation.20 | async-start | bytes 2359296 | tf_op jit(solution)/shard_map/all_gather | solution.py:1386
  9.1 150.9 %all-gather.9.cloned.1.call-start = ((), (), s32[]{:S(2)}) async-start(), calls=%async_computation.7 | async-start | bytes 12976128 | tf_op jit(solution)/shard_map/all_gather | solution.py:1386
  14.2 231.2 %all-gather.11.cloned.1.call-start = ((), (), s32[]{:S(2)}) async-start(), calls=%async_computation.8 | async-start | bytes 6488064 | tf_op jit(solution)/shard_map/all_gather | solution.py:1386
  14.2 5.3 copy-start.17
  14.2 5.3 copy-start.6
  16.9 6.5 copy-start.7
  16.9 6.5 copy-start.8
  134.1 111.3 %all-gather.13.cloned.1.call-start = ((), (), s32[]{:S(2)}) async-start(), calls=%async_computation.9 | async-start | bytes 7077888 | tf_op jit(solution)/shard_map/all_gather | solution.py:1386
  137.7 18.5 %copy-start = (bf16[1,256,3,512]{1,3,2,0:T(8,128)(2,1)S(1)}, bf16[1,256,3,512]{1,3,2,0:T(8,128)(2,1)}, u32[]{:S(2)}) copy-start(bf16[1,256,3,512]{1,3,2,0:T(8,128)(2,1)} %copy.49) | copy-start | bytes 2359300
  157.4 193.9 %all-gather.15.cloned.1.call-start = ((), (), s32[]{:S(2)}) async-start(), calls=%async_computation.10 | async-start | bytes 2359296 | tf_op jit(solution)/shard_map/all_gather | solution.py:1386
  158.0 193.3 %all-gather.17.cloned.1.call-start = ((), (), s32[]{:S(2)}) async-start(), calls=%async_computation.11 | async-start | bytes 12976128 | tf_op jit(solution)/shard_map/all_gather | solution.py:1386
  158.6 280.1 %all-gather.19.cloned.1.call-start = ((), (), s32[]{:S(2)}) async-start(), calls=%async_computation.12 | async-start | bytes 6488064 | tf_op jit(solution)/shard_map/all_gather | solution.py:1386
  159.3 666.7 %reduce-scatter.8.cloned.1.call-start = ((), (), s32[]{:S(2)}) async-start(), calls=%async_computation.13 | async-start | bytes 12976128 | tf_op jit(solution)/shard_map/reduce_scatter | solution.py:1366
  556.5 376.0 %reduce-scatter.10.cloned.1.call-start = ((), (), s32[]{:S(2)}) async-start(), calls=%async_computation.14 | async-start | bytes 6488064 | tf_op jit(solution)/shard_map/reduce_scatter | solution.py:1366
  557.2 96.5 %copy-start.19 = (bf16[1024,512]{1,0:T(8,128)(2,1)S(1)}, bf16[1024,512]{1,0:T(8,128)(2,1)}, u32[]{:S(2)}) copy-start(bf16[1024,512]{1,0:T(8,128)(2,1)} %get-tuple-element.92.attended) | copy-start | bytes 3145732
  557.2 408.3 %reduce-scatter.14.cloned.1.call-start = ((), (), s32[]{:S(2)}) async-start(), calls=%async_computation.16 | async-start | bytes 2359296 | tf_op jit(solution)/shard_map/reduce_scatter | solution.py:1366
  659.8 305.7 %reduce-scatter.12.cloned.1.call-start = ((), (), s32[]{:S(2)}) async-start(), calls=%async_computation.15 | async-start | bytes 7077888 | tf_op jit(solution)/shard_map/reduce_scatter | solution.py:1366
  696.4 383.9 %reduce-scatter.18.cloned.1.call-start = ((), (), s32[]{:S(2)}) async-start(), calls=%async_computation.18 | async-start | bytes 12976128 | tf_op jit(solution)/shard_map/reduce_scatter | solution.py:1366
  825.0 0.9 copy-start.15
  825.0 0.9 copy-start.9
  825.0 0.9 copy-start.10
  825.0 0.9 copy-start.13
  825.0 0.9 copy-start.14
  825.0 272.6 %reduce-scatter.20.cloned.1.call-start = ((), (), s32[]{:S(2)}) async-start(), calls=%async_computation.19 | async-start | bytes 6488064 | tf_op jit(solution)/shard_map/reduce_scatter | solution.py:1366
  825.8 288.9 %reduce-scatter.16.cloned.1.call-start = ((), (), s32[]{:S(2)}) async-start(), calls=%async_computation.17 | async-start | bytes 2359296 | tf_op jit(solution)/shard_map/reduce_scatter | solution.py:1366
  826.0 100.5 %copy-start.18 = (bf16[1024,512]{1,0:T(8,128)(2,1)S(1)}, bf16[1024,512]{1,0:T(8,128)(2,1)}, u32[]{:S(2)}) copy-start(bf16[1024,512]{1,0:T(8,128)(2,1)} %get-tuple-element.86.attended) | copy-start | bytes 3145732
  965.5 109.4 %copy-start.16 = (f32[3,512]{1,0:T(4,128)S(1)}, f32[3,512]{1,0:T(4,128)}, u32[]{:S(2)}) copy-start(f32[3,512]{1,0:T(4,128)} %get-tuple-element.143) | copy-start | bytes 18436
  965.5 109.4 %copy-start.11 = (f32[1,2048]{1,0:T(1,128)S(1)}, f32[1,2048]{1,0:T(1,128)}, u32[]{:S(2)}) copy-start(f32[1,2048]{1,0:T(1,128)} %get-tuple-element.140) | copy-start | bytes 24580
  965.5 109.4 %copy-start.12 = (f32[1,2048]{1,0:T(1,128)S(1)}, f32[1,2048]{1,0:T(1,128)}, u32[]{:S(2)}) copy-start(f32[1,2048]{1,0:T(1,128)} %get-tuple-element.142) | copy-start | bytes 24580
  965.6 114.3 %copy-start.3 = (bf16[256,2816]{1,0:T(8,128)(2,1)S(1)}, bf16[256,2816]{1,0:T(8,128)(2,1)}, u32[]{:S(2)}) copy-start(bf16[256,2816]{1,0:T(8,128)(2,1)} %reduce-scatter.8.cloned.1.call-done) | copy-start | bytes 4325380
  1075.7 2.7 collective-permute-start
  1078.5 5.9 collective-permute-start.1
  1085.3 8.5 collective-permute-start.2
  1093.8 7.0 copy-start.4
  1093.8 10.0 collective-permute-start.3
  1097.6 4.6 copy-start.2
  1103.9 8.5 collective-permute-start.4
  1107.6 7.1 copy-start.5
  1109.9 9.0 copy-start.1
Sparse Core Ops, SparseCore 0:
  9.9 36.2 all-gather.20
  48.6 80.2 all-gather.8
  134.2 42.4 all-gather.10
  179.0 45.5 all-gather.12
  226.3 28.1 all-gather.14
  256.9 67.7 all-gather.16
  327.1 44.4 all-gather.18
  556.6 127.3 reduce-scatter.7
  688.0 59.0 reduce-scatter.9
  751.2 41.2 reduce-scatter.13
  795.8 61.7 reduce-scatter.11
  861.3 86.7 reduce-scatter.17
  952.0 59.0 reduce-scatter.19
  1014.2 50.1 reduce-scatter.15

commit v5 on v4

--- a/solution.py
+++ b/solution.py
@@ -92,94 +92,6 @@
             if step:
                 self.to_chips(step).wait_send()
             self.to_core(step).wait_send()
-
-
-class Owned:
-    def __init__(self, part, size, mine, swapped, landed, load_sem, sems):
-        self.part, self.mine, self.swapped, self.landed = part, mine, swapped, landed
-        self.load_sem, (self.swap_send, self.swap_recv, self.send_sem, self.recv_sem) = load_sem, sems
-        self.member = lax.axis_index("dp")
-        self.share = part.shape[0] // size
-        self.chips = range(size // 2)
-
-    def peers(self):
-        return tuple(member_at(self.member, 2 * chip) for chip in self.chips if chip) + (
-            member_at(self.member, 1),
-        )
-
-    def rows(self, step):
-        return pl.ds(pl.multiple_of(member_at(self.member, step) * self.share, self.share), self.share)
-
-    def load(self, chip):
-        return pltpu.make_async_copy(
-            self.part.at[self.rows(2 * chip)], self.mine.at[chip], self.load_sem.at[chip]
-        )
-
-    def swap(self, chip):
-        return pltpu.make_async_remote_copy(
-            src_ref=self.part.at[self.rows(2 * chip + 1)],
-            dst_ref=self.swapped.at[chip],
-            send_sem=self.swap_send.at[chip],
-            recv_sem=self.swap_recv.at[chip],
-            device_id={"dp": member_at(self.member, 1)},
-            device_id_type=MESH,
-        )
-
-    def hop(self, chip):
-        return pltpu.make_async_remote_copy(
-            src_ref=self.mine.at[chip],
-            dst_ref=self.landed.at[chip - 1],
-            send_sem=self.send_sem.at[chip],
-            recv_sem=self.recv_sem.at[chip],
-            device_id={"dp": member_at(self.member, 2 * chip)},
-            device_id_type=MESH,
-        )
-
-    def each_rows(self, run):
-        def one(number, carry):
-            run(pl.ds(pl.multiple_of(number * 16, 16), 16))
-            return carry
-
-        lax.fori_loop(0, self.share // 16, one, 0)
-
-    def start(self):
-        for chip in self.chips:
-            self.swap(chip).start()
-            self.load(chip).start()
-
-    def across_chips(self, total):
-        for chip in (*self.chips[1:], 0):
-            self.load(chip).wait()
-            self.swap(chip).wait_recv()
-
-            def rows(at):
-                both = self.mine[chip, at, :].astype(F32) + self.swapped[chip, at, :].astype(F32)
-                if chip:
-                    self.mine[chip, at, :] = both.astype(BF16)
-                else:
-                    total[at, :] = both
-
-            self.each_rows(rows)
-            if chip:
-                self.hop(chip).start()
-
-    def finish(self, total):
-        for chip in self.chips[1:]:
-            self.hop(chip).wait_recv()
-
-        def rows(at):
-            values = total[at, :]
-            for chip in self.chips[1:]:
-                values = values + self.landed[chip - 1, at, :].astype(F32)
-            total[at, :] = values
-
-        self.each_rows(rows)
-
-    def drain(self):
-        for chip in self.chips:
-            self.swap(chip).wait_send()
-            if chip:
-                self.hop(chip).wait_send()
 
 
 def line_barrier(place, count, others=()):
@@ -491,6 +403,26 @@
     def wait(self, *numbers):
         for number in numbers:
             self.copies[number].wait()
+
+
+class Tiles:
+    def __init__(self, source, target, axis, sems):
+        self.source, self.target, self.axis, self.sems = source, target, axis, sems
+        self.size = min(256, target.shape[axis])
+        for number in range(target.shape[axis] // self.size):
+            self.copy(number).start()
+
+    def copy(self, number):
+        at = pl.ds(pl.multiple_of(number * self.size, self.size), self.size)
+        where = (at,) if self.axis == 0 else (slice(None), at)
+        return pltpu.make_async_copy(
+            self.source.at[where], self.target.at[where], self.sems.at[number]
+        )
+
+    def need(self, piece, start):
+        @pl.when(piece == 0)
+        def _():
+            self.copy(start // self.size).wait()
 
 
 class Saves:
@@ -634,11 +566,12 @@
     return process
 
 
-def share_of(line, source, weight):
+def share_of(line, source, weight, tiles):
     def term(piece):
         rows = line.at(piece)
 
         def run(start, size):
+            tiles.need(piece, start)
             at = pl.ds(start, size)
             put_rows(line.shares, rows, at, matmul(flat_rows(source, rows), weight[:, at]))
 
@@ -647,13 +580,14 @@
     return term
 
 
-def share_transposed(line, sources, weight):
+def share_transposed(line, sources, weight, tiles):
     width = sources[0].shape[2]
 
     def term(piece):
         rows = line.at(piece)
 
         def run(start, size):
+            tiles.need(piece, start)
             at = pl.ds(start, size)
             result = matmul(flat_rows(sources[0], rows), weight[at, :width], cols_cols)
             for number in range(1, len(sources)):
@@ -787,15 +721,16 @@
 
 
 def middle_kernel(count, pieces, lag, *refs):
-    ins, outs, scatter, gather, rest = split(refs, 6, 5, 5, 3, 9)
+    ins, outs, scatter, gather, rest = split(refs, 6, 5, 5, 3, 10)
     source, w_out, before, gain, shift, w_up = ins
     after, rows_out, act_out, slope_out, silu_out = outs
-    source_held, out_held, up_held, act, slope, silu, load_sem, save_sem, turn = rest
+    source_held, out_held, up_held, act, slope, silu, load_sem, tile_sem, save_sem, turn = rest
     line = Line(count, pieces, *scatter, *gather)
-    loads = Loads([(source, source_held), (w_out, out_held), (w_up, up_held)], load_sem)
+    loads = Loads([(source, source_held), (w_up, up_held)], load_sem)
     member = lax.axis_index("dp")
     core = member % 2
     partner = member + 1 - 2 * core
+    tiles = Tiles(w_out, out_held, 1, tile_sem)
     line_barrier(line.place, count, (partner,) if lag else ())
     saves = Saves(
         [(line.held, rows_out), (act, act_out), (slope, slope_out), (silu, silu_out)], save_sem, line
@@ -805,7 +740,7 @@
     def process(piece):
         @pl.when(piece == 0)
         def _():
-            loads.wait(2)
+            loads.wait(1)
 
         compute(piece)
         saves.start(piece)
@@ -815,7 +750,7 @@
         def _():
             pl.semaphore_signal(turn, inc=1, device_id={"dp": partner}, device_id_type=MESH)
 
-    loads.wait(0, 1)
+    loads.wait(0)
     if lag:
 
         @pl.when(core == 1)
@@ -823,7 +758,7 @@
             pl.semaphore_wait(turn, 1)
 
     line.run(
-        share_of(line, source_held, out_held),
+        share_of(line, source_held, out_held, tiles),
         add_and_norm(line, before, gain, shift, after),
         process,
         signal if lag else None,
@@ -857,7 +792,8 @@
             pltpu.VMEM(wide.shape, BF16),
             pltpu.VMEM(wide.shape, BF16),
             pltpu.VMEM(wide.shape, BF16),
-            pltpu.SemaphoreType.DMA((3,)),
+            pltpu.SemaphoreType.DMA((2,)),
+            pltpu.SemaphoreType.DMA((max(1, depth // 256),)),
             pltpu.SemaphoreType.DMA((4, pieces)),
             pltpu.SemaphoreType.REGULAR,
         ],
@@ -868,12 +804,13 @@
 
 
 def between_kernel(count, pieces, *refs):
-    ins, outs, scatter, gather, rest = split(refs, 10, 3, 5, 3, 6)
+    ins, outs, scatter, gather, rest = split(refs, 10, 3, 5, 3, 7)
     source, w_down, before, gain, shift, weight, bias, *tables = ins
     after, rows_out, mixed_out = outs
-    source_held, down_held, weight_held, mixed, load_sem, save_sem = rest
+    source_held, down_held, weight_held, mixed, load_sem, tile_sem, save_sem = rest
     line = Line(count, pieces, *scatter, *gather)
-    loads = Loads([(source, source_held), (w_down, down_held), (weight, weight_held)], load_sem)
+    loads = Loads([(source, source_held), (weight, weight_held)], load_sem)
+    tiles = Tiles(w_down, down_held, 1, tile_sem)
     line_barrier(line.place, count)
     saves = Saves([(line.held, rows_out), (mixed, mixed_out)], save_sem, line)
     compute = query_key_value(line, weight_held, bias, tables, mixed)
@@ -881,14 +818,14 @@
     def process(piece):
         @pl.when(piece == 0)
         def _():
-            loads.wait(2)
+            loads.wait(1)
 
         compute(piece)
         saves.start(piece)
 
-    loads.wait(0, 1)
+    loads.wait(0)
     line.run(
-        share_of(line, source_held, down_held), add_and_norm(line, before, gain, shift, after), process
+        share_of(line, source_held, down_held, tiles), add_and_norm(line, before, gain, shift, after), process
     )
     line.drain()
     saves.wait()
@@ -914,7 +851,8 @@
             pltpu.VMEM(w_down.shape, BF16),
             pltpu.VMEM(weight.shape, BF16),
             pltpu.VMEM(mixed, BF16),
-            pltpu.SemaphoreType.DMA((3,)),
+            pltpu.SemaphoreType.DMA((2,)),
+            pltpu.SemaphoreType.DMA((max(1, depth // 256),)),
             pltpu.SemaphoreType.DMA((2, pieces)),
         ],
         2,
@@ -924,14 +862,15 @@
 
 
 def turn_kernel(count, pieces, *refs):
-    ins, outs, scatter, gather, rest = split(refs, 6, 3, 5, 3, 7)
+    ins, outs, scatter, gather, rest = split(refs, 6, 3, 5, 3, 8)
     source, w_down, before, own, slope_in, silu_in = ins
     after, rows_out, wide_out = outs
-    source_held, down_held, slope, silu, wide, load_sem, save_sem = rest
+    source_held, down_held, slope, silu, wide, load_sem, tile_sem, save_sem = rest
     line = Line(count, pieces, *scatter, *gather)
     loads = Loads(
-        [(source, source_held), (w_down, down_held), (slope_in, slope), (silu_in, silu)], load_sem
-    )
+        [(source, source_held), (slope_in, slope), (silu_in, silu)], load_sem
+    )
+    tiles = Tiles(w_down, down_held, 1, tile_sem)
     line_barrier(line.place, count)
     saves = Saves([(line.held, rows_out), (wide, wide_out)], save_sem, line)
     compute = grad_gate_and_up(line, down_held, slope, silu, wide)
@@ -946,13 +885,13 @@
     def process(piece):
         @pl.when(piece == 0)
         def _():
-            loads.wait(2, 3)
+            loads.wait(1, 2)
 
         compute(piece)
         saves.start(piece)
 
-    loads.wait(0, 1)
-    line.run(share_of(line, source_held, down_held), finish, process)
+    loads.wait(0)
+    line.run(share_of(line, source_held, down_held, tiles), finish, process)
     line.drain()
     saves.wait()
 
@@ -978,7 +917,8 @@
             pltpu.VMEM(slope.shape, BF16),
             pltpu.VMEM(silu.shape, BF16),
             pltpu.VMEM((count, rows, 2 * width), BF16),
-            pltpu.SemaphoreType.DMA((4,)),
+            pltpu.SemaphoreType.DMA((3,)),
+            pltpu.SemaphoreType.DMA((max(1, depth // 256),)),
             pltpu.SemaphoreType.DMA((2, pieces)),
         ],
         3,
@@ -988,12 +928,13 @@
 
 
 def middle_back_kernel(count, pieces, *refs):
-    ins, outs, scatter, gather, rest = split(refs, 6, 5, 5, 3, 6)
+    ins, outs, scatter, gather, rest = split(refs, 6, 5, 5, 3, 7)
     source, w_up, grad, hidden, gain, w_out = ins
     out, gain_sum, shift_sum, rows_out, result_out = outs
-    source_held, up_held, out_held, result, load_sem, save_sem = rest
+    source_held, up_held, out_held, result, load_sem, tile_sem, save_sem = rest
     line = Line(count, pieces, *scatter, *gather)
-    loads = Loads([(source, source_held), (w_up, up_held), (w_out, out_held)], load_sem)
+    loads = Loads([(source, source_held), (w_out, out_held)], load_sem)
+    tiles = Tiles(w_up, up_held, 0, tile_sem)
     line_barrier(line.place, count)
     saves = Saves([(line.held, rows_out), (result, result_out)], save_sem, line)
     compute = through_transposed(line, out_held, result)
@@ -1001,14 +942,14 @@
     def process(piece):
         @pl.when(piece == 0)
         def _():
-            loads.wait(2)
+            loads.wait(1)
 
         compute(piece)
         saves.start(piece)
 
-    loads.wait(0, 1)
+    loads.wait(0)
     line.run(
-        share_transposed(line, [source_held], up_held),
+        share_transposed(line, [source_held], up_held, tiles),
         norm_backward(line, grad, hidden, gain, out, gain_sum, shift_sum),
         process,
     )
@@ -1038,7 +979,8 @@
             pltpu.VMEM(w_up.shape, BF16),
             pltpu.VMEM(w_out.shape, BF16),
             pltpu.VMEM((count, rows, width), BF16),
-            pltpu.SemaphoreType.DMA((3,)),
+            pltpu.SemaphoreType.DMA((2,)),
+            pltpu.SemaphoreType.DMA((max(1, depth // 256),)),
             pltpu.SemaphoreType.DMA((2, pieces)),
         ],
         4 if grad.dtype == F32 else 8,
@@ -1048,21 +990,21 @@
 
 
 def between_back_kernel(count, pieces, *refs):
-    ins, outs, scatter, gather, rest = split(refs, 8, 5, 5, 3, 8)
+    ins, outs, scatter, gather, rest = split(refs, 8, 5, 5, 3, 9)
     source, weight, grad, hidden, gain, w_down, slope_in, silu_in = ins
     out, gain_sum, shift_sum, rows_out, wide_out = outs
-    source_held, weight_held, down_held, slope, silu, wide, load_sem, save_sem = rest
+    source_held, weight_held, down_held, slope, silu, wide, load_sem, tile_sem, save_sem = rest
     line = Line(count, pieces, *scatter, *gather)
     loads = Loads(
         [
             (source, source_held),
-            (weight, weight_held),
             (w_down, down_held),
             (slope_in, slope),
             (silu_in, silu),
         ],
         load_sem,
     )
+    tiles = Tiles(weight, weight_held, 0, tile_sem)
     line_barrier(line.place, count)
     saves = Saves([(line.held, rows_out), (wide, wide_out)], save_sem, line)
     compute = grad_gate_and_up(line, down_held, slope, silu, wide)
@@ -1070,14 +1012,14 @@
     def process(piece):
         @pl.when(piece == 0)
         def _():
-            loads.wait(2, 3, 4)
+            loads.wait(1, 2, 3)
 
         compute(piece)
         saves.start(piece)
 
-    loads.wait(0, 1)
+    loads.wait(0)
     line.run(
-        share_transposed(line, [source_held.at[kind] for kind in range(3)], weight_held),
+        share_transposed(line, [source_held.at[kind] for kind in range(3)], weight_held, tiles),
         norm_backward(line, grad, hidden, gain, out, gain_sum, shift_sum),
         process,
     )
@@ -1109,7 +1051,8 @@
             pltpu.VMEM(slope.shape, BF16),
             pltpu.VMEM(silu.shape, BF16),
             pltpu.VMEM((count, rows, 2 * width), BF16),
-            pltpu.SemaphoreType.DMA((5,)),
+            pltpu.SemaphoreType.DMA((4,)),
+            pltpu.SemaphoreType.DMA((max(1, depth // 256),)),
             pltpu.SemaphoreType.DMA((2, pieces)),
         ],
         5,
@@ -1118,64 +1061,46 @@
     )(source, weight, grad, hidden, gain, w_down, slope, silu)
 
 
-def last_kernel(count, pieces, size, *refs):
-    ins, outs, scatter, rest = split(refs, 6, 4, 5, 11)
-    source, weight, grad, hidden, gain, part = ins
-    *outs, owned_out = outs
-    source_held, weight_held, load_sem, mine, swapped, landed, part_sem, *sems = rest
+def last_kernel(count, pieces, *refs):
+    ins, outs, scatter, rest = split(refs, 5, 3, 5, 4)
+    source, weight, grad, hidden, gain = ins
+    source_held, weight_held, load_sem, tile_sem = rest
     line = Line(count, pieces, *scatter, None, None, None)
-    owned = Owned(part, size, mine, swapped, landed, part_sem, sems)
-    loads = Loads([(source, source_held), (weight, weight_held)], load_sem)
-    line_barrier(line.place, count, owned.peers())
-    owned.start()
-
-    def each_tick(number):
-        @pl.when(number == 1)
-        def _():
-            owned.across_chips(owned_out)
-
-    loads.wait(0, 1)
+    loads = Loads([(source, source_held), ], load_sem)
+    tiles = Tiles(weight, weight_held, 0, tile_sem)
+    line_barrier(line.place, count)
+    loads.wait(0)
     line.run(
-        share_transposed(line, [source_held.at[kind] for kind in range(3)], weight_held),
+        share_transposed(line, [source_held.at[kind] for kind in range(3)], weight_held, tiles),
         norm_backward(line, grad, hidden, gain, *outs),
         None,
-        each_tick,
     )
     line.drain()
-    owned.finish(owned_out)
-    owned.drain()
-
-
-def last(count, source, weight, grad, hidden, gain, part):
+
+
+def last(count, source, weight, grad, hidden, gain):
     rows, depth = grad.shape
     pieces = pieces_of(rows)
-    size = lax.axis_size("dp")
-    share, width = part.shape[0] // size, part.shape[1]
     return line_call(
-        functools.partial(last_kernel, count, pieces, size),
+        functools.partial(last_kernel, count, pieces),
         (
             jax.ShapeDtypeStruct((rows, depth), F32),
             jax.ShapeDtypeStruct((1, depth), F32),
             jax.ShapeDtypeStruct((1, depth), F32),
-            jax.ShapeDtypeStruct((share, width), F32),
         ),
-        (vmem, vmem, vmem, vmem),
-        [hbm, hbm, vmem, vmem, vmem, hbm],
+        (vmem, vmem, vmem),
+        [hbm, hbm, vmem, vmem, vmem],
         scatter_scratch(count, pieces, rows, depth)
         + [
             pltpu.VMEM(source.shape, BF16),
             pltpu.VMEM(weight.shape, BF16),
-            pltpu.SemaphoreType.DMA((2,)),
-            pltpu.VMEM((size // 2, share, width), BF16),
-            pltpu.VMEM((size // 2, share, width), BF16),
-            pltpu.VMEM((size // 2 - 1, share, width), BF16),
-            pltpu.SemaphoreType.DMA((size // 2,)),
-        ]
-        + [pltpu.SemaphoreType.DMA((size // 2,))] * 4,
+            pltpu.SemaphoreType.DMA((1,)),
+            pltpu.SemaphoreType.DMA((max(1, depth // 256),)),
+        ],
         6,
         2 * count * rows * weight.size,
         weight.size * 2 + grad.size * 20,
-    )(source, weight, grad, hidden, gain, part)
+    )(source, weight, grad, hidden, gain)
 
 
 def usable(first, start, keys, queries):
@@ -1336,6 +1261,95 @@
     )(positions, mixed, mixed, mixed, attended, grad_attended, logsums, *tables)
 
 
+def weight_grad_kernel(groups, tile, *refs):
+    ins, (out,), rest = split(refs, 2 * groups, 1, 2 * groups + 6)
+    held, (across, stages, tail, load_sem, out_sem, tail_sem) = split(rest, 2 * groups, 6)
+    loads = Loads(list(zip(ins, held)), load_sem)
+    depth, length = across.shape
+    chunk = min(1024, depth)
+
+    def save(slot, column):
+        return pltpu.make_async_copy(
+            stages.at[slot], out.at[:, pl.ds(pl.multiple_of(column, 128), tile)], out_sem.at[slot]
+        )
+
+    column, done = 0, 0
+    for group in range(groups):
+        left, right = held[2 * group], held[2 * group + 1]
+        loads.wait(2 * group)
+
+        def turn_over(number, carry, left=left):
+            at = pl.ds(pl.multiple_of(number * 256, 256), 256)
+            across[at, :] = jnp.transpose(left[:, at])
+            return carry
+
+        lax.fori_loop(0, depth // 256, turn_over, 0)
+        loads.wait(2 * group + 1)
+        kinds, _, width = right.shape
+        full, short = width // tile, width % tile
+        for kind in range(kinds):
+
+            def fill(target, start, size, kind=kind, right=right):
+                def rows(number, carry):
+                    at = pl.ds(pl.multiple_of(number * chunk, chunk), chunk)
+                    target[at, :] = matmul(across[at, :], right[kind, :, pl.ds(start, size)]).astype(BF16)
+                    return carry
+
+                lax.fori_loop(0, depth // chunk, rows, 0)
+
+            def one(number, carry, fill=fill, column=column, done=done):
+                slot = (done + number) % 2
+
+                @pl.when(done + number >= 2)
+                def _():
+                    save(slot, 0).wait()
+
+                start = pl.multiple_of(number * tile, tile)
+                fill(stages.at[slot], start, tile)
+                save(slot, column + start).start()
+                return carry
+
+            lax.fori_loop(0, full, one, 0)
+            done += full
+            if short:
+                fill(tail, full * tile, short)
+                copy = pltpu.make_async_copy(
+                    tail, out.at[:, column + full * tile : column + width], tail_sem
+                )
+                copy.start()
+                copy.wait()
+            column += width
+    for slot in range(min(2, done)):
+        save(slot, 0).wait()
+
+
+def weight_grad(*pairs):
+    length, depth = pairs[0][0].shape
+    total = sum(right.shape[0] * right.shape[2] for _, right in pairs)
+    tile = min(256, *(right.shape[2] for _, right in pairs))
+    short = max(right.shape[2] % tile for _, right in pairs)
+    arrays = [array for pair in pairs for array in pair]
+    return pl.pallas_call(
+        functools.partial(weight_grad_kernel, len(pairs), tile),
+        out_shape=jax.ShapeDtypeStruct((depth, total), BF16),
+        in_specs=[hbm] * len(arrays),
+        out_specs=hbm,
+        scratch_shapes=[pltpu.VMEM(array.shape, BF16) for array in arrays]
+        + [
+            pltpu.VMEM((depth, length), BF16),
+            pltpu.VMEM((2, depth, tile), BF16),
+            pltpu.VMEM((depth, short or 128), BF16),
+            pltpu.SemaphoreType.DMA((len(arrays),)),
+            pltpu.SemaphoreType.DMA((2,)),
+            pltpu.SemaphoreType.DMA,
+        ],
+        compiler_params=pltpu.CompilerParams(vmem_limit_bytes=VMEM_LIMIT),
+        cost_estimate=pl.CostEstimate(
+            flops=2 * length * depth * total, bytes_accessed=4 * depth * total, transcendentals=0
+        ),
+    )(*arrays)
+
+
 def rotary_tables(positions):
     half_rot = ROT // 2
     lane = jnp.arange(PAIR, dtype=jnp.int32) % HD
@@ -1349,7 +1363,8 @@
     )
 
 
-def all_sum(values, axes):
+def all_sum(values, axes, beside):
+    beside, made = list(beside), []
     for axis in axes:
         size = lax.axis_size(axis)
         if size & (size - 1):
@@ -1357,9 +1372,13 @@
             continue
         step = 1
         while step < size:
-            values = values + lax.ppermute(values, axis, [(i, i ^ step) for i in range(size)])
+            moved = lax.ppermute(values, axis, [(i, i ^ step) for i in range(size)])
+            if beside:
+                moved, array = lax.optimization_barrier((moved, beside.pop(0)))
+                made.append(array)
+            values = values + moved
             step *= 2
-    return values
+    return values, made + beside
 
 
 def owner_sum(part, axis):
@@ -1449,34 +1468,28 @@
         hidden, rows_a, mixed, attended, logsums, hidden_mid, rows_b, act, slope, silu = kept[layer]
         full_qkv, full_out, full_gu, full_down = gathered[layer]
         later = scattered[layer + 1] if layer + 1 < LAYERS else None
-        gu_part = matmul(
-            rows_b.reshape(length, depth), wide.reshape(length, 2 * ff_local), rows_rows
-        ).astype(BF16)
-        down_part = matmul(
-            act.reshape(length, ff_local), grad_rows_b.reshape(length, depth), rows_rows
-        ).astype(BF16)
-        wide, down_part, gu_part = after(wide, down_part, gu_part)
-        gu_grad, down_grad = owner_sum(gu_part, 0), owner_sum(down_part, 1)
+        feed_part = weight_grad(
+            (rows_b.reshape(length, depth), wide.reshape(1, length, 2 * ff_local)),
+            (grad_rows_b.reshape(length, depth), act.reshape(1, length, ff_local)),
+        )
+        wide, feed_part = after(wide, feed_part)
+        feed_grad = owner_sum(feed_part, 0)
         if later:
-            wide, later[2] = after(wide, later[2])
+            wide, later[1] = after(wide, later[1])
         grad, gain_b, shift_b, grad_rows_a, grad_attended = middle_back(
             count, wide, full_gu, grad, hidden_mid, norm_gain[layer, 1:2], full_out
         )
-        out_part = matmul(attended, grad_rows_a.reshape(length, depth), rows_rows).astype(BF16)
-        grad_attended, out_part = after(grad_attended, out_part)
-        out_grad = owner_sum(out_part, 1)
         if later:
-            grad_attended, later[3] = after(grad_attended, later[3])
+            grad_attended, later[0] = after(grad_attended, later[0])
         grad_mixed, bias_sum = attend_backward(
             mixed, positions_row, attended, grad_attended.reshape(length, width), logsums, tables
         )
-        flat_mixed = grad_mixed.transpose(1, 0, 2).reshape(length, 3 * width)
-        qkv_part = matmul(rows_a.reshape(length, depth), flat_mixed, rows_rows).astype(BF16)
-        grad_mixed, qkv_part = after(grad_mixed, qkv_part)
-        if layer:
-            qkv_grad = owner_sum(qkv_part, 0)
-        if later:
-            grad_mixed, later[0], later[1] = after(grad_mixed, later[0], later[1])
+        attend_part = weight_grad(
+            (rows_a.reshape(length, depth), grad_mixed),
+            (grad_rows_a.reshape(length, depth), attended.reshape(1, length, width)),
+        )
+        grad_mixed, attend_part = after(grad_mixed, attend_part)
+        attend_grad = owner_sum(attend_part, 0)
         source = grad_mixed.reshape(3, count, rows, width)
         if layer:
             below = kept[layer - 1]
@@ -1492,20 +1505,21 @@
                 below[9],
             )
         else:
-            grad, gain_a, shift_a, qkv_grad = last(
-                count, source, full_qkv, grad, hidden, norm_gain[layer, 0:1], qkv_part
-            )
+            grad, gain_a, shift_a = last(count, source, full_qkv, grad, hidden, norm_gain[layer, 0:1])
         bias_full = lax.dynamic_update_slice(
             jnp.zeros((3, b_qkv.shape[2]), F32), bias_sum, (jnp.int32(0), tensor_rank * width)
         )
         small[layer] = jnp.concatenate([gain_a, gain_b, shift_a, shift_b, bias_full], axis=0)
-        scattered[layer] = [qkv_grad, out_grad, gu_grad, down_grad]
-    sums = all_sum(jnp.stack(small), ("dp", "tensor"))
-    shapes = ((-1, 3, width), (width, -1), (-1, 2, ff_local), (ff_local, -1))
-    stacks = [
-        jnp.stack([scattered[layer][kind].astype(F32).reshape(shape) for layer in range(LAYERS)])
-        for kind, shape in enumerate(shapes)
-    ]
+        scattered[layer] = [attend_grad, feed_grad]
+    cuts = (
+        lambda each: each[0][:, : 3 * width].reshape(-1, 3, width),
+        lambda each: each[0][:, 3 * width :].T,
+        lambda each: each[1][:, : 2 * ff_local].reshape(-1, 2, ff_local),
+        lambda each: each[1][:, 2 * ff_local :].T,
+    )
+    stacks = [jnp.stack([cut(each).astype(F32) for each in scattered]) for cut in cuts]
+    sums, made = all_sum(jnp.stack(small), ("dp", "tensor"), stacks[2:] + stacks[:2])
+    stacks = made[2:] + made[:2]
     return (
         activations,
         grad,

time: 1140 us -> 1110 us (0.974)
  matrix products: 92.4 us -> 0 us
  starting transfers between devices: 11.3 us -> 44.5 us
  Pallas kernels: 937 us -> 967 us
    dot_general x8 -> x0, matrix products: 92.4 us -> none  [matmul(): return lax.dot_general(left, right, dims, preferred_element_type=F32)]
    pallas_call x1 -> x5, Pallas kernels: 109 us -> 146 us  [the longest x4 97.4 us: weight_grad(): pl.pallas_call(functools.partial(weight_grad_kernel, len(pairs), tile), o...]
    ppermute x5, starting transfers between devices: 10.7 us -> 44 us  [all_sum(): moved = lax.ppermute(values, axis, [(i, i ^ step) for i in range(size)])]
  transfers between devices with their start and end apart: 19 -> 16, of which waited for: 3 -> 2; matrix products, arithmetic and copies ran while one was open for 11% -> 5% of each run, Pallas kernels for 75% -> 77%
where the time goes in v5:
time: 1110 us; the launch traced here: 1100 us
  Pallas kernels  967 us (87%)
  local copies, waits for them, and re-layouts  51 us (5%)
  starting transfers between devices  44.5 us (4%)
  other arithmetic  18 us (2%)
  between operations  14.8 us (1%)
    pallas_call x2, Pallas kernels, middle_back(): line_call(functools.partial(middle_back_kernel, count, pieces), (jax.Shap...  193 us
    pallas_call x2, Pallas kernels, middle(): line_call(functools.partial(middle_kernel, count, pieces, lag), (jax.Shap...  176 us
    pallas_call x1, Pallas kernels, first(): line_call(functools.partial(first_kernel, count, pieces, size), (jax.Shap...  107 us
    pallas_call x4, Pallas kernels, weight_grad(): pl.pallas_call(functools.partial(weight_grad_kernel, len(pairs), tile), o...  97.4 us
    pallas_call x1, Pallas kernels, between_back(): line_call(functools.partial(between_back_kernel, count, pieces), (jax.Sha...  95.6 us
    pallas_call x1, Pallas kernels, turn(): line_call(functools.partial(turn_kernel, count, pieces), (jax.ShapeDtypeS...  87.6 us
    pallas_call x1, Pallas kernels, between(): line_call(functools.partial(between_kernel, count, pieces), (jax.ShapeDty...  87.1 us
    pallas_call x1, Pallas kernels, last(): line_call(functools.partial(last_kernel, count, pieces), (jax.ShapeDtypeS...  49.1 us
  transfers between devices with their start and end apart: 16, of which 2 were waited for; matrix products, arithmetic and copies ran while one was open for 5% of the time, Pallas kernels for 77%

profile of v5, /device:TPU:0, one launch (start us, length us, event | category | flops | bytes accessed | tf_op | source)
XLA Modules:
  0.0 1101.8 jit_solution(8857703857417351433)
XLA Ops:
  7.2 1.9 fusion.17
  9.2 3.7 fusion.15
  12.9 1.3 copy.41
  14.2 2.7 fusion.16
  17.0 1.4 copy.38
  18.4 1.2 copy.29.refs_3_
  20.2 3.2 fusion
  24.1 2.5 slice_bitcast_fusion.2
  26.6 107.5 %shard_map.169 = (bf16[4,256,2048]{2,1,0:T(8,128)(2,1)}, bf16[3,4,256,512]{3,2,1,0:T(8,128)(2,1)}, bf16[2048,1536]{1,0:T(8,128)(2,1)}) custom-call(bf16[256,2048]{1,0:T(8,128)(2,1)} %refs_3_.3, f32[1,2048]{1,0:T(1,128)} %get-tuple-element.200.refs_1_.refs_4_, f32[1,2048]{1,0:T(1,128)} %get-tuple-element.185.refs_2_, bf16[256,1536]{1,0:T(8,128)(2,1)} %copy.29.refs_3_, ...), custom_call_target="tpu_custom_call" | custom-call | flops 6442450944 | bytes 23068672 | tf_op jit(solution)/shard_map/pallas_call | solution.py:699
  134.2 2.3 copy.39
  136.5 1.3 copy.40
  137.7 18.5 %shard_map.170 = (bf16[1024,512]{1,0:T(8,128)(2,1)}, f32[4,2,1024]{2,1,0:T(2,128)}) custom-call(s32[1,1024]{1,0:T(1,128)} %bitcast.92, bf16[3,1024,512]{2,1,0:T(8,128)(2,1)} %bitcast.108, bf16[3,1024,512]{2,1,0:T(8,128)(2,1)} %bitcast.109, bf16[3,1024,512]{2,1,0:T(8,128)(2,1)} %bitcast.110), custom_call_target="tpu_custom_call" | custom-call | flops 4294967296 | bytes 4194304 | tf_op jit(solution)/shard_map/pallas_call | solution.py:1147
  160.0 86.9 %shard_map.171 = (f32[256,2048]{1,0:T(8,128)}, bf16[4,256,2048]{2,1,0:T(8,128)(2,1)}, bf16[4,256,1408]{2,1,0:T(8,128)(2,1)}, bf16[4,256,1408]{2,1,0:T(8,128)(2,1)}, bf16[4,256,1408]{2,1,0:T(8,128)(2,1)}) custom-call(bf16[4,256,512]{2,1,0:T(8,128)(2,1)} %bitcast.124, bf16[512,2048]{1,0:T(8,128)(2,1)} %bitcast.96, bf16[256,2048]{1,0:T(8,128)(2,1)} %refs_3_.3, ...), custom_call_target="tpu_custom_call" | custom-call | flops 13958643712 | bytes 45088768 | tf_op jit(solution)/shard_map/pallas_call | solution.py:775
  246.9 87.1 %shard_map.172 = (f32[256,2048]{1,0:T(8,128)}, bf16[4,256,2048]{2,1,0:T(8,128)(2,1)}, bf16[3,4,256,512]{3,2,1,0:T(8,128)(2,1)}) custom-call(bf16[4,256,1408]{2,1,0:T(8,128)(2,1)} %get-tuple-element.85.refs_0_, bf16[1408,2048]{1,0:T(8,128)(2,1)} %all-gather.11.cloned.1.call-done.refs_1_.refs_5_, f32[256,2048]{1,0:T(8,128)} %get-tuple-element.87.refs_2_.refs_3_, ...), custom_call_target="tpu_custom_call" | custom-call | flops 12348030976 | bytes 43515904 | tf_op jit(solution)/shard_map/pallas_call | solution.py:838
  334.0 18.5 %shard_map.173 = (bf16[1024,512]{1,0:T(8,128)(2,1)}, f32[4,2,1024]{2,1,0:T(2,128)}) custom-call(s32[1,1024]{1,0:T(1,128)} %bitcast.93, bf16[3,1024,512]{2,1,0:T(8,128)(2,1)} %bitcast.114, bf16[3,1024,512]{2,1,0:T(8,128)(2,1)} %bitcast.115, bf16[3,1024,512]{2,1,0:T(8,128)(2,1)} %bitcast.116), custom_call_target="tpu_custom_call" | custom-call | flops 4294967296 | bytes 4194304 | tf_op jit(solution)/shard_map/pallas_call | solution.py:1147
  352.6 88.9 %shard_map.174 = (f32[256,2048]{1,0:T(8,128)}, bf16[4,256,2048]{2,1,0:T(8,128)(2,1)}, bf16[4,256,1408]{2,1,0:T(8,128)(2,1)}, bf16[4,256,1408]{2,1,0:T(8,128)(2,1)}, bf16[4,256,1408]{2,1,0:T(8,128)(2,1)}) custom-call(bf16[4,256,512]{2,1,0:T(8,128)(2,1)} %bitcast.126, bf16[512,2048]{1,0:T(8,128)(2,1)} %all-gather.15.cloned.1.call-done.refs_1_.refs_5_, ...), custom_call_target="tpu_custom_call" | custom-call | flops 13958643712 | bytes 45088768 | tf_op jit(solution)/shard_map/pallas_call | solution.py:775
  441.5 87.6 %shard_map.175 = (bf16[256,2048]{1,0:T(8,128)(2,1)}, bf16[4,256,2048]{2,1,0:T(8,128)(2,1)}, bf16[4,256,2816]{2,1,0:T(8,128)(2,1)}) custom-call(bf16[4,256,1408]{2,1,0:T(8,128)(2,1)} %get-tuple-element.94.refs_0_, bf16[1408,2048]{1,0:T(8,128)(2,1)} %all-gather.19.cloned.1.call-done.refs_1_, f32[256,2048]{1,0:T(8,128)} %get-tuple-element.96.refs_2_.refs_3_, ...), custom_call_target="tpu_custom_call" | custom-call | flops 11811160064 | bytes 37224448 | tf_op jit(solution)/shard_map/pallas_call | solution.py:903
  529.1 30.7 %shard_map.176 = bf16[2048,4224]{1,0:T(8,128)(2,1)} custom-call(bf16[1024,2048]{1,0:T(8,128)(2,1)} %bitcast.106, bf16[1,1024,2816]{2,1,0:T(8,128)(2,1)} %bitcast.99, bf16[1024,2048]{1,0:T(8,128)(2,1)} %bitcast.107, bf16[1,1024,1408]{2,1,0:T(8,128)(2,1)} %bitcast.123), custom_call_target="tpu_custom_call" | custom-call | flops 17716740096 | bytes 34603008 | tf_op jit(solution)/shard_map/pallas_call | solution.py:1332
  559.9 3.2 fusion.2
  563.1 95.1 %shard_map.177 = (f32[256,2048]{1,0:T(8,128)}, f32[1,2048]{1,0:T(1,128)}, f32[1,2048]{1,0:T(1,128)}, bf16[4,256,2048]{2,1,0:T(8,128)(2,1)}, bf16[4,256,512]{2,1,0:T(8,128)(2,1)}) custom-call(bf16[4,256,2816]{2,1,0:T(8,128)(2,1)} %get-tuple-element.103.refs_0_, bf16[2048,2816]{1,0:T(8,128)(2,1)} %all-gather.17.cloned.1.call-done.refs_5_.refs_1_, ...), custom_call_target="tpu_custom_call" | custom-call | flops 13958643712 | bytes 45088768 | tf_op jit(solution)/shard_map/pallas_call | solution.py:964
  658.2 18.7 %shard_map.178 = (bf16[3,1024,512]{2,1,0:T(8,128)(2,1)}, f32[3,512]{1,0:T(4,128)}) custom-call(s32[1,1024]{1,0:T(1,128)} %bitcast.94, bf16[3,1024,512]{2,1,0:T(8,128)(2,1)} %bitcast.117, bf16[3,1024,512]{2,1,0:T(8,128)(2,1)} %bitcast.118, bf16[3,1024,512]{2,1,0:T(8,128)(2,1)} %bitcast.119, bf16[1024,512]{1,0:T(8,128)(2,1)} %get-tuple-element.90.attended, ...), custom_call_target="tpu_custom_call" | custom-call | flops 10737418240 | bytes 8388608 | tf_op jit(solution)/shard_map/pallas_call | solution.py:1231
  676.9 18.0 %shard_map.179 = bf16[2048,2048]{1,0:T(8,128)(2,1)} custom-call(bf16[1024,2048]{1,0:T(8,128)(2,1)} %bitcast.102, bf16[3,1024,512]{2,1,0:T(8,128)(2,1)} %get-tuple-element.109.refs_1_, bf16[1024,2048]{1,0:T(8,128)(2,1)} %bitcast.104, bf16[1,1024,512]{2,1,0:T(8,128)(2,1)} %bitcast.127), custom_call_target="tpu_custom_call" | custom-call | flops 8589934592 | bytes 16777216 | tf_op jit(solution)/shard_map/pallas_call | solution.py:1332
  695.0 95.6 %shard_map.180 = (f32[256,2048]{1,0:T(8,128)}, f32[1,2048]{1,0:T(1,128)}, f32[1,2048]{1,0:T(1,128)}, bf16[4,256,2048]{2,1,0:T(8,128)(2,1)}, bf16[4,256,2816]{2,1,0:T(8,128)(2,1)}) custom-call(bf16[3,4,256,512]{3,2,1,0:T(8,128)(2,1)} %bitcast.121, bf16[2048,1536]{1,0:T(8,128)(2,1)} %all-gather.13.cloned.1.call-done.refs_5_.refs_1_, ...), custom_call_target="tpu_custom_call" | custom-call | flops 12348030976 | bytes 43515904 | tf_op jit(solution)/shard_map/pallas_call | solution.py:1034
  790.6 30.7 %shard_map.181 = bf16[2048,4224]{1,0:T(8,128)(2,1)} custom-call(bf16[1024,2048]{1,0:T(8,128)(2,1)} %bitcast.101, bf16[1,1024,2816]{2,1,0:T(8,128)(2,1)} %bitcast.98, bf16[1024,2048]{1,0:T(8,128)(2,1)} %bitcast.105, bf16[1,1024,1408]{2,1,0:T(8,128)(2,1)} %bitcast.122), custom_call_target="tpu_custom_call" | custom-call | flops 17716740096 | bytes 34603008 | tf_op jit(solution)/shard_map/pallas_call | solution.py:1332
  821.4 97.6 %shard_map.182 = (f32[256,2048]{1,0:T(8,128)}, f32[1,2048]{1,0:T(1,128)}, f32[1,2048]{1,0:T(1,128)}, bf16[4,256,2048]{2,1,0:T(8,128)(2,1)}, bf16[4,256,512]{2,1,0:T(8,128)(2,1)}) custom-call(bf16[4,256,2816]{2,1,0:T(8,128)(2,1)} %get-tuple-element.118.refs_0_, bf16[2048,2816]{1,0:T(8,128)(2,1)} %all-gather.9.cloned.1.call-done.refs_5_.refs_1_, ...), custom_call_target="tpu_custom_call" | custom-call | flops 13958643712 | bytes 45088768 | tf_op jit(solution)/shard_map/pallas_call | solution.py:964
  919.1 18.8 %shard_map.183 = (bf16[3,1024,512]{2,1,0:T(8,128)(2,1)}, f32[3,512]{1,0:T(4,128)}) custom-call(s32[1,1024]{1,0:T(1,128)} %bitcast.95, bf16[3,1024,512]{2,1,0:T(8,128)(2,1)} %bitcast.111, bf16[3,1024,512]{2,1,0:T(8,128)(2,1)} %bitcast.112, bf16[3,1024,512]{2,1,0:T(8,128)(2,1)} %bitcast.113, bf16[1024,512]{1,0:T(8,128)(2,1)} %get-tuple-element.84.attended, ...), custom_call_target="tpu_custom_call" | custom-call | flops 10737418240 | bytes 8388608 | tf_op jit(solution)/shard_map/pallas_call | solution.py:1231
  937.8 17.9 %shard_map.184 = bf16[2048,2048]{1,0:T(8,128)(2,1)} custom-call(bf16[1024,2048]{1,0:T(8,128)(2,1)} %bitcast.100, bf16[3,1024,512]{2,1,0:T(8,128)(2,1)} %get-tuple-element.127.refs_1_, bf16[1024,2048]{1,0:T(8,128)(2,1)} %bitcast.103, bf16[1,1024,512]{2,1,0:T(8,128)(2,1)} %bitcast.125), custom_call_target="tpu_custom_call" | custom-call | flops 8589934592 | bytes 16777216 | tf_op jit(solution)/shard_map/pallas_call | solution.py:1332
  956.7 49.1 %shard_map.185 = (f32[256,2048]{1,0:T(8,128)}, f32[1,2048]{1,0:T(1,128)}, f32[1,2048]{1,0:T(1,128)}) custom-call(bf16[3,4,256,512]{3,2,1,0:T(8,128)(2,1)} %bitcast.120, bf16[2048,1536]{1,0:T(8,128)(2,1)} %get-tuple-element.128.refs_1_, f32[256,2048]{1,0:T(8,128)} %get-tuple-element.129.refs_2_, bf16[256,2048]{1,0:T(8,128)(2,1)} %refs_3_.3, ...), custom_call_target="tpu_custom_call" | custom-call | flops 6442450944 | bytes 16777216 | tf_op jit(solution)/shard_map/pallas_call | solution.py:1084
  1006.8 33.5 %collective-permute-start = (f32[2,7,2048]{2,1,0:T(8,128)S(1)}, f32[2,7,2048]{2,1,0:T(8,128)S(1)}, u32[]{:S(2)}, u32[]{:S(2)}) collective-permute-start(f32[2,7,2048]{2,1,0:T(8,128)S(1)} %pad_maximum_fusion), channel_id=1, source_target_pairs={{0,4},{4,0},{8,12},{12,8},{16,20},{20,16},{24,28},{28,24},{1,5},{5... | collective-permute-start | bytes 344072 | tf_op jit(solution)/shard_map/ppermute | solution.py:1375
  1040.2 1.3 convert_element_type.75
  1041.5 2.8 slice.120
  1044.3 4.1 convert_element_type.74
  1048.5 1.3 slice_bitcast_fusion
  1050.5 6.2 maximum_convert_fusion
  1056.7 1.8 maximum_convert_fusion.2
  1058.5 3.8 collective-permute-start.1
  1063.5 2.9 collective-permute-done.1
  1066.4 3.3 collective-permute-start.2
  1069.7 1.2 slice.122
  1072.1 1.6 maximum_convert_fusion.1
  1074.6 1.7 collective-permute-start.3
  1078.3 1.4 collective-permute-done.3
  1079.6 1.8 collective-permute-start.4
  1081.4 3.4 copy.37
  1084.8 2.4 copy.34
  1087.2 2.7 copy.36
  1091.2 2.3 copy.46
  1093.5 1.3 copy.47
  (107 shorter events, 14.7 us)
Async XLA Ops:
  7.2 152.8 %all-gather.21.cloned.1.call-start = ((), (), s32[]{:S(2)}) async-start(), calls=%async_computation.14 | async-start | bytes 2359296 | tf_op jit(solution)/shard_map/all_gather | solution.py:1405
  9.1 150.9 %all-gather.9.cloned.1.call-start = ((), (), s32[]{:S(2)}) async-start(), calls=%async_computation.4 | async-start | bytes 12976128 | tf_op jit(solution)/shard_map/all_gather | solution.py:1405
  14.2 232.7 %all-gather.11.cloned.1.call-start = ((), (), s32[]{:S(2)}) async-start(), calls=%async_computation.5 | async-start | bytes 6488064 | tf_op jit(solution)/shard_map/all_gather | solution.py:1405
  14.2 5.3 copy-start.17
  14.2 5.3 copy-start.6
  17.0 6.5 copy-start.7
  17.0 6.5 copy-start.8
  134.1 112.8 %all-gather.13.cloned.1.call-start = ((), (), s32[]{:S(2)}) async-start(), calls=%async_computation.6 | async-start | bytes 7077888 | tf_op jit(solution)/shard_map/all_gather | solution.py:1405
  137.7 18.5 %copy-start.3 = (bf16[1,256,3,512]{1,3,2,0:T(8,128)(2,1)S(1)}, bf16[1,256,3,512]{1,3,2,0:T(8,128)(2,1)}, u32[]{:S(2)}) copy-start(bf16[1,256,3,512]{1,3,2,0:T(8,128)(2,1)} %copy.39) | copy-start | bytes 2359300
  157.4 195.1 %all-gather.15.cloned.1.call-start = ((), (), s32[]{:S(2)}) async-start(), calls=%async_computation.7 | async-start | bytes 2359296 | tf_op jit(solution)/shard_map/all_gather | solution.py:1405
  158.0 194.5 %all-gather.17.cloned.1.call-start = ((), (), s32[]{:S(2)}) async-start(), calls=%async_computation.8 | async-start | bytes 12976128 | tf_op jit(solution)/shard_map/all_gather | solution.py:1405
  158.6 282.9 %all-gather.19.cloned.1.call-start = ((), (), s32[]{:S(2)}) async-start(), calls=%async_computation.9 | async-start | bytes 6488064 | tf_op jit(solution)/shard_map/all_gather | solution.py:1405
  159.3 662.1 %reduce-scatter.5.cloned.1.call-start = ((), (), s32[]{:S(2)}) async-start(), calls=%async_computation.10 | async-start | bytes 19464192 | tf_op jit(solution)/shard_map/reduce_scatter | solution.py:1385
  559.8 359.2 %reduce-scatter.7.cloned.1.call-start = ((), (), s32[]{:S(2)}) async-start(), calls=%async_computation.11 | async-start | bytes 9437184 | tf_op jit(solution)/shard_map/reduce_scatter | solution.py:1385
  694.9 346.6 %reduce-scatter.9.cloned.1.call-start = ((), (), s32[]{:S(2)}) async-start(), calls=%async_computation.12 | async-start | bytes 19464192 | tf_op jit(solution)/shard_map/reduce_scatter | solution.py:1385
  821.3 248.4 %reduce-scatter.11.cloned.1.call-start = ((), (), s32[]{:S(2)}) async-start(), calls=%async_computation.13 | async-start | bytes 9437184 | tf_op jit(solution)/shard_map/reduce_scatter | solution.py:1385
  955.8 0.7 copy-start.15
  955.8 0.7 copy-start.9
  955.8 0.7 copy-start.10
  955.8 0.7 copy-start.11
  955.8 0.7 copy-start.12
  955.9 0.8 copy-start.16
  956.7 49.1 %copy-start.13 = (f32[1,2048]{1,0:T(1,128)S(1)}, f32[1,2048]{1,0:T(1,128)}, u32[]{:S(2)}) copy-start(f32[1,2048]{1,0:T(1,128)} %get-tuple-element.132) | copy-start | bytes 24580
  956.7 49.1 %copy-start.14 = (f32[1,2048]{1,0:T(1,128)S(1)}, f32[1,2048]{1,0:T(1,128)}, u32[]{:S(2)}) copy-start(f32[1,2048]{1,0:T(1,128)} %get-tuple-element.134) | copy-start | bytes 24580
  1005.8 34.5 %slice-start = ((bf16[256,4224]{1,0:T(8,128)(2,1)}), bf16[256,2816]{1,0:T(8,128)(2,1)S(1)}, s32[]{:S(2)}) async-start(bf16[256,4224]{1,0:T(8,128)(2,1)} %reduce-scatter.5.cloned.1.call-done), calls=%async_computation.15 | async-start | bytes 2883584 | tf_op jit(solution)/shard_map/slice | solution.py:1517
  1006.8 51.7 %collective-permute-start = (f32[2,7,2048]{2,1,0:T(8,128)S(1)}, f32[2,7,2048]{2,1,0:T(8,128)S(1)}, u32[]{:S(2)}, u32[]{:S(2)}) collective-permute-start(f32[2,7,2048]{2,1,0:T(8,128)S(1)} %pad_maximum_fusion), channel_id=1, source_target_pairs={{0,4},{4,0},{8,12},{12,8},{16,20},{20,16},{24,28},{28,24},{1,5},{5... | collective-permute-start | bytes 344072 | tf_op jit(solution)/shard_map/ppermute | solution.py:1375
  1041.5 6.9 copy-start
  1048.4 1.6 copy-start.1
  1048.4 2.0 copy-start.2
  1056.7 5.6 copy-start.4
  1056.7 5.6 slice-start.1
  1058.5 7.9 collective-permute-start.1
  1066.4 7.2 collective-permute-start.2
  1074.6 5.0 collective-permute-start.3
  1079.6 10.2 collective-permute-start.4
  1087.2 6.3 copy-start.5
Sparse Core Ops, SparseCore 0:
  9.9 36.2 all-gather.20
  48.6 80.3 all-gather.8
  134.3 42.4 all-gather.10
  179.1 45.5 all-gather.12
  226.3 28.3 all-gather.14
  257.0 67.8 all-gather.16
  327.4 44.4 all-gather.18
  560.0 158.3 reduce-scatter.4
  722.3 81.1 reduce-scatter.6
  821.5 154.4 reduce-scatter.8
  979.9 82.8 reduce-scatter.10

commit v6 on v5

--- a/solution.py
+++ b/solution.py
@@ -1103,10 +1103,16 @@
     )(source, weight, grad, hidden, gain)
 
 
-def usable(first, start, keys, queries):
-    key_index = lax.broadcasted_iota(jnp.int32, (keys, queries), 0)
-    query_index = start + lax.broadcasted_iota(jnp.int32, (keys, queries), 1)
-    return (key_index >= first) & (key_index <= query_index)
+def key_parts(first, start, seen):
+    size = seen - start
+    parts = []
+    if start:
+        key_index = lax.broadcasted_iota(jnp.int32, (start, size), 0)
+        parts.append((slice(0, start), key_index >= first))
+    key_index = start + lax.broadcasted_iota(jnp.int32, (size, size), 0)
+    query_index = start + lax.broadcasted_iota(jnp.int32, (size, size), 1)
+    parts.append((slice(start, seen), (key_index >= first) & (key_index <= query_index)))
+    return parts
 
 
 def head_lanes(values, head):
@@ -1122,15 +1128,22 @@
         at = slice(start, seen)
         own = queries[at, :]
         index = start + lax.broadcasted_iota(jnp.int32, (1, block), 1)
-        allowed = usable(index - positions[:, at], start, seen, block)
+        parts = key_parts(index - positions[:, at], start, seen)
         halves = []
         for head in range(2):
-            scores = matmul(keys[:seen, :], head_lanes(own, head), cols_cols)
-            scores = jnp.where(allowed, scores, masked_score)
-            highest = jnp.max(scores, axis=0, keepdims=True)
-            weights = jnp.exp(scores - highest)
-            sums = jnp.sum(weights, axis=0, keepdims=True)
-            result = matmul(values_across[:, :seen], weights.astype(BF16))
+            own_head = head_lanes(own, head)
+            scores = [
+                jnp.where(allowed, matmul(keys[part, :], own_head, cols_cols), masked_score)
+                for part, allowed in parts
+            ]
+            highest = functools.reduce(
+                jnp.maximum, [jnp.max(each, axis=0, keepdims=True) for each in scores]
+            )
+            sums, result = 0.0, 0.0
+            for (part, _), each in zip(parts, scores):
+                weights = jnp.exp(each - highest)
+                sums = sums + jnp.sum(weights, axis=0, keepdims=True)
+                result = result + matmul(values_across[:, part], weights.astype(BF16))
             halves.append(result[head * HD : (head + 1) * HD, :] / sums)
             logsums[head : head + 1, at] = highest + jnp.log(sums)
         attended[at, :] = jnp.transpose(jnp.concatenate(halves, axis=0)).astype(BF16)
@@ -1194,19 +1207,21 @@
         grad_own = grad_attended[at, :]
         inner = jnp.transpose(grad_own.astype(F32) * attended[at, :].astype(F32))
         index = start + lax.broadcasted_iota(jnp.int32, (1, block), 1)
-        allowed = usable(index - positions[:, at], start, seen, block)
+        parts = key_parts(index - positions[:, at], start, seen)
         halves = []
         for head in range(2):
             own_head = head_lanes(own, head)
             grad_head = head_lanes(grad_own, head)
-            scores = matmul(keys[:seen, :], own_head, cols_cols)
-            weights = jnp.where(allowed, jnp.exp(scores - logsums[head : head + 1, at]), 0.0)
-            grad_weights = matmul(values[:seen, :], grad_head, cols_cols)
             row_inner = jnp.sum(inner[head * HD : (head + 1) * HD, :], axis=0, keepdims=True)
-            grad_scores = (weights * (grad_weights - row_inner)).astype(BF16)
-            grad_values[:seen, :] += matmul(weights.astype(BF16), grad_head)
-            grad_keys[:seen, :] += matmul(grad_scores, own_head)
-            result = matmul(keys_across[:, :seen], grad_scores)
+            result = 0.0
+            for part, allowed in parts:
+                scores = matmul(keys[part, :], own_head, cols_cols)
+                weights = jnp.where(allowed, jnp.exp(scores - logsums[head : head + 1, at]), 0.0)
+                grad_weights = matmul(values[part, :], grad_head, cols_cols)
+                grad_scores = (weights * (grad_weights - row_inner)).astype(BF16)
+                grad_values[part, :] += matmul(weights.astype(BF16), grad_head)
+                grad_keys[part, :] += matmul(grad_scores, own_head)
+                result = result + matmul(keys_across[:, part], grad_scores)
             halves.append(result[head * HD : (head + 1) * HD, :])
         grad_own_queries = jnp.transpose(jnp.concatenate(halves, axis=0)) * (1.0 / math.sqrt(HD))
         low = unrotate(grad_own_queries, cos[at, :], sin_up[at, :], sin_down[at, :]).astype(BF16)

time: 1110 us -> 1110 us (level)
  transfers between devices with their start and end apart: 16 -> 16, of which waited for: 2 -> 3; matrix products, arithmetic and copies ran while one was open for 5% -> 5% of each run, Pallas kernels for 77% -> 77%
where the time goes in v6:
time: 1110 us
  Pallas kernels  976 us (88%)
  local copies, waits for them, and re-layouts  51.4 us (5%)
  starting transfers between devices  38.8 us (3%)
  other arithmetic  18 us (2%)
  between operations  14.8 us (1%)
    pallas_call x2, Pallas kernels, middle_back(): line_call(functools.partial(middle_back_kernel, count, pieces), (jax.Shap...  195 us
    pallas_call x2, Pallas kernels, middle(): line_call(functools.partial(middle_kernel, count, pieces, lag), (jax.Shap...  180 us
    pallas_call x1, Pallas kernels, first(): line_call(functools.partial(first_kernel, count, pieces, size), (jax.Shap...  107 us
    pallas_call x1, Pallas kernels, between_back(): line_call(functools.partial(between_back_kernel, count, pieces), (jax.Sha...  98.2 us
    pallas_call x4, Pallas kernels, weight_grad(): pl.pallas_call(functools.partial(weight_grad_kernel, len(pairs), tile), o...  97.5 us
    pallas_call x1, Pallas kernels, turn(): line_call(functools.partial(turn_kernel, count, pieces), (jax.ShapeDtypeS...  90 us
    pallas_call x1, Pallas kernels, between(): line_call(functools.partial(between_kernel, count, pieces), (jax.ShapeDty...  87.2 us
    pallas_call x1, Pallas kernels, last(): line_call(functools.partial(last_kernel, count, pieces), (jax.ShapeDtypeS...  49.2 us
  transfers between devices with their start and end apart: 16, of which 3 were waited for; matrix products, arithmetic and copies ran while one was open for 5% of the time, Pallas kernels for 77%

profile of v6, /device:TPU:0, one launch (start us, length us, event | category | flops | bytes accessed | tf_op | source)
XLA Modules:
  0.0 1107.1 jit_solution(1561903863423608251)
XLA Ops:
  7.2 1.9 fusion.17
  9.2 3.7 fusion.15
  12.9 1.3 copy.41
  14.2 2.7 fusion.16
  17.0 1.4 copy.38
  18.4 1.2 copy.29.refs_3_
  20.2 3.2 fusion
  24.1 2.5 slice_bitcast_fusion.2
  26.6 107.5 %shard_map.169 = (bf16[4,256,2048]{2,1,0:T(8,128)(2,1)}, bf16[3,4,256,512]{3,2,1,0:T(8,128)(2,1)}, bf16[2048,1536]{1,0:T(8,128)(2,1)}) custom-call(bf16[256,2048]{1,0:T(8,128)(2,1)} %refs_3_.3, f32[1,2048]{1,0:T(1,128)} %get-tuple-element.200.refs_1_.refs_4_, f32[1,2048]{1,0:T(1,128)} %get-tuple-element.185.refs_2_, bf16[256,1536]{1,0:T(8,128)(2,1)} %copy.29.refs_3_, ...), custom_call_target="tpu_custom_call" | custom-call | flops 6442450944 | bytes 23068672 | tf_op jit(solution)/shard_map/pallas_call | solution.py:699
  134.2 2.3 copy.39
  136.5 1.3 copy.40
  137.7 14.8 %shard_map.170 = (bf16[1024,512]{1,0:T(8,128)(2,1)}, f32[4,2,1024]{2,1,0:T(2,128)}) custom-call(s32[1,1024]{1,0:T(1,128)} %bitcast.92, bf16[3,1024,512]{2,1,0:T(8,128)(2,1)} %bitcast.108, bf16[3,1024,512]{2,1,0:T(8,128)(2,1)} %bitcast.109, bf16[3,1024,512]{2,1,0:T(8,128)(2,1)} %bitcast.110), custom_call_target="tpu_custom_call" | custom-call | flops 4294967296 | bytes 4194304 | tf_op jit(solution)/shard_map/pallas_call | solution.py:1160
  152.5 1.2 copy.31
  156.3 87.1 %shard_map.171 = (f32[256,2048]{1,0:T(8,128)}, bf16[4,256,2048]{2,1,0:T(8,128)(2,1)}, bf16[4,256,1408]{2,1,0:T(8,128)(2,1)}, bf16[4,256,1408]{2,1,0:T(8,128)(2,1)}, bf16[4,256,1408]{2,1,0:T(8,128)(2,1)}) custom-call(bf16[4,256,512]{2,1,0:T(8,128)(2,1)} %bitcast.124, bf16[512,2048]{1,0:T(8,128)(2,1)} %bitcast.96, bf16[256,2048]{1,0:T(8,128)(2,1)} %refs_3_.3, ...), custom_call_target="tpu_custom_call" | custom-call | flops 13958643712 | bytes 45088768 | tf_op jit(solution)/shard_map/pallas_call | solution.py:775
  243.5 87.2 %shard_map.172 = (f32[256,2048]{1,0:T(8,128)}, bf16[4,256,2048]{2,1,0:T(8,128)(2,1)}, bf16[3,4,256,512]{3,2,1,0:T(8,128)(2,1)}) custom-call(bf16[4,256,1408]{2,1,0:T(8,128)(2,1)} %get-tuple-element.85.refs_0_, bf16[1408,2048]{1,0:T(8,128)(2,1)} %all-gather.11.cloned.1.call-done.refs_1_.refs_5_, f32[256,2048]{1,0:T(8,128)} %get-tuple-element.87.refs_2_.refs_3_, ...), custom_call_target="tpu_custom_call" | custom-call | flops 12348030976 | bytes 43515904 | tf_op jit(solution)/shard_map/pallas_call | solution.py:838
  330.7 14.6 %shard_map.173 = (bf16[1024,512]{1,0:T(8,128)(2,1)}, f32[4,2,1024]{2,1,0:T(2,128)}) custom-call(s32[1,1024]{1,0:T(1,128)} %bitcast.93, bf16[3,1024,512]{2,1,0:T(8,128)(2,1)} %bitcast.114, bf16[3,1024,512]{2,1,0:T(8,128)(2,1)} %bitcast.115, bf16[3,1024,512]{2,1,0:T(8,128)(2,1)} %bitcast.116), custom_call_target="tpu_custom_call" | custom-call | flops 4294967296 | bytes 4194304 | tf_op jit(solution)/shard_map/pallas_call | solution.py:1160
  345.3 92.4 %shard_map.174 = (f32[256,2048]{1,0:T(8,128)}, bf16[4,256,2048]{2,1,0:T(8,128)(2,1)}, bf16[4,256,1408]{2,1,0:T(8,128)(2,1)}, bf16[4,256,1408]{2,1,0:T(8,128)(2,1)}, bf16[4,256,1408]{2,1,0:T(8,128)(2,1)}) custom-call(bf16[4,256,512]{2,1,0:T(8,128)(2,1)} %bitcast.126, bf16[512,2048]{1,0:T(8,128)(2,1)} %all-gather.15.cloned.1.call-done.refs_1_.refs_5_, ...), custom_call_target="tpu_custom_call" | custom-call | flops 13958643712 | bytes 45088768 | tf_op jit(solution)/shard_map/pallas_call | solution.py:775
  437.8 90.0 %shard_map.175 = (bf16[256,2048]{1,0:T(8,128)(2,1)}, bf16[4,256,2048]{2,1,0:T(8,128)(2,1)}, bf16[4,256,2816]{2,1,0:T(8,128)(2,1)}) custom-call(bf16[4,256,1408]{2,1,0:T(8,128)(2,1)} %get-tuple-element.94.refs_0_, bf16[1408,2048]{1,0:T(8,128)(2,1)} %all-gather.19.cloned.1.call-done.refs_1_, f32[256,2048]{1,0:T(8,128)} %get-tuple-element.96.refs_2_.refs_3_, ...), custom_call_target="tpu_custom_call" | custom-call | flops 11811160064 | bytes 37224448 | tf_op jit(solution)/shard_map/pallas_call | solution.py:903
  527.8 30.7 %shard_map.176 = bf16[2048,4224]{1,0:T(8,128)(2,1)} custom-call(bf16[1024,2048]{1,0:T(8,128)(2,1)} %bitcast.106, bf16[1,1024,2816]{2,1,0:T(8,128)(2,1)} %bitcast.99, bf16[1024,2048]{1,0:T(8,128)(2,1)} %bitcast.107, bf16[1,1024,1408]{2,1,0:T(8,128)(2,1)} %bitcast.123), custom_call_target="tpu_custom_call" | custom-call | flops 17716740096 | bytes 34603008 | tf_op jit(solution)/shard_map/pallas_call | solution.py:1347
  558.6 3.2 fusion.2
  561.8 94.8 %shard_map.177 = (f32[256,2048]{1,0:T(8,128)}, f32[1,2048]{1,0:T(1,128)}, f32[1,2048]{1,0:T(1,128)}, bf16[4,256,2048]{2,1,0:T(8,128)(2,1)}, bf16[4,256,512]{2,1,0:T(8,128)(2,1)}) custom-call(bf16[4,256,2816]{2,1,0:T(8,128)(2,1)} %get-tuple-element.103.refs_0_, bf16[2048,2816]{1,0:T(8,128)(2,1)} %all-gather.17.cloned.1.call-done.refs_5_.refs_1_, ...), custom_call_target="tpu_custom_call" | custom-call | flops 13958643712 | bytes 45088768 | tf_op jit(solution)/shard_map/pallas_call | solution.py:964
  656.6 21.1 %shard_map.178 = (bf16[3,1024,512]{2,1,0:T(8,128)(2,1)}, f32[3,512]{1,0:T(4,128)}) custom-call(s32[1,1024]{1,0:T(1,128)} %bitcast.94, bf16[3,1024,512]{2,1,0:T(8,128)(2,1)} %bitcast.117, bf16[3,1024,512]{2,1,0:T(8,128)(2,1)} %bitcast.118, bf16[3,1024,512]{2,1,0:T(8,128)(2,1)} %bitcast.119, bf16[1024,512]{1,0:T(8,128)(2,1)} %get-tuple-element.90.attended, ...), custom_call_target="tpu_custom_call" | custom-call | flops 10737418240 | bytes 8388608 | tf_op jit(solution)/shard_map/pallas_call | solution.py:1246
  677.7 18.0 %shard_map.179 = bf16[2048,2048]{1,0:T(8,128)(2,1)} custom-call(bf16[1024,2048]{1,0:T(8,128)(2,1)} %bitcast.102, bf16[3,1024,512]{2,1,0:T(8,128)(2,1)} %get-tuple-element.109.refs_1_, bf16[1024,2048]{1,0:T(8,128)(2,1)} %bitcast.104, bf16[1,1024,512]{2,1,0:T(8,128)(2,1)} %bitcast.127), custom_call_target="tpu_custom_call" | custom-call | flops 8589934592 | bytes 16777216 | tf_op jit(solution)/shard_map/pallas_call | solution.py:1347
  695.8 98.2 %shard_map.180 = (f32[256,2048]{1,0:T(8,128)}, f32[1,2048]{1,0:T(1,128)}, f32[1,2048]{1,0:T(1,128)}, bf16[4,256,2048]{2,1,0:T(8,128)(2,1)}, bf16[4,256,2816]{2,1,0:T(8,128)(2,1)}) custom-call(bf16[3,4,256,512]{3,2,1,0:T(8,128)(2,1)} %bitcast.121, bf16[2048,1536]{1,0:T(8,128)(2,1)} %all-gather.13.cloned.1.call-done.refs_5_.refs_1_, ...), custom_call_target="tpu_custom_call" | custom-call | flops 12348030976 | bytes 43515904 | tf_op jit(solution)/shard_map/pallas_call | solution.py:1034
  794.0 30.8 %shard_map.181 = bf16[2048,4224]{1,0:T(8,128)(2,1)} custom-call(bf16[1024,2048]{1,0:T(8,128)(2,1)} %bitcast.101, bf16[1,1024,2816]{2,1,0:T(8,128)(2,1)} %bitcast.98, bf16[1024,2048]{1,0:T(8,128)(2,1)} %bitcast.105, bf16[1,1024,1408]{2,1,0:T(8,128)(2,1)} %bitcast.122), custom_call_target="tpu_custom_call" | custom-call | flops 17716740096 | bytes 34603008 | tf_op jit(solution)/shard_map/pallas_call | solution.py:1347
  824.9 100.2 %shard_map.182 = (f32[256,2048]{1,0:T(8,128)}, f32[1,2048]{1,0:T(1,128)}, f32[1,2048]{1,0:T(1,128)}, bf16[4,256,2048]{2,1,0:T(8,128)(2,1)}, bf16[4,256,512]{2,1,0:T(8,128)(2,1)}) custom-call(bf16[4,256,2816]{2,1,0:T(8,128)(2,1)} %get-tuple-element.118.refs_0_, bf16[2048,2816]{1,0:T(8,128)(2,1)} %all-gather.9.cloned.1.call-done.refs_5_.refs_1_, ...), custom_call_target="tpu_custom_call" | custom-call | flops 13958643712 | bytes 45088768 | tf_op jit(solution)/shard_map/pallas_call | solution.py:964
  925.1 21.3 %shard_map.183 = (bf16[3,1024,512]{2,1,0:T(8,128)(2,1)}, f32[3,512]{1,0:T(4,128)}) custom-call(s32[1,1024]{1,0:T(1,128)} %bitcast.95, bf16[3,1024,512]{2,1,0:T(8,128)(2,1)} %bitcast.111, bf16[3,1024,512]{2,1,0:T(8,128)(2,1)} %bitcast.112, bf16[3,1024,512]{2,1,0:T(8,128)(2,1)} %bitcast.113, bf16[1024,512]{1,0:T(8,128)(2,1)} %get-tuple-element.84.attended, ...), custom_call_target="tpu_custom_call" | custom-call | flops 10737418240 | bytes 8388608 | tf_op jit(solution)/shard_map/pallas_call | solution.py:1246
  946.4 17.9 %shard_map.184 = bf16[2048,2048]{1,0:T(8,128)(2,1)} custom-call(bf16[1024,2048]{1,0:T(8,128)(2,1)} %bitcast.100, bf16[3,1024,512]{2,1,0:T(8,128)(2,1)} %get-tuple-element.127.refs_1_, bf16[1024,2048]{1,0:T(8,128)(2,1)} %bitcast.103, bf16[1,1024,512]{2,1,0:T(8,128)(2,1)} %bitcast.125), custom_call_target="tpu_custom_call" | custom-call | flops 8589934592 | bytes 16777216 | tf_op jit(solution)/shard_map/pallas_call | solution.py:1347
  965.2 49.2 %shard_map.185 = (f32[256,2048]{1,0:T(8,128)}, f32[1,2048]{1,0:T(1,128)}, f32[1,2048]{1,0:T(1,128)}) custom-call(bf16[3,4,256,512]{3,2,1,0:T(8,128)(2,1)} %bitcast.120, bf16[2048,1536]{1,0:T(8,128)(2,1)} %get-tuple-element.128.refs_1_, f32[256,2048]{1,0:T(8,128)} %get-tuple-element.129.refs_2_, bf16[256,2048]{1,0:T(8,128)(2,1)} %refs_3_.3, ...), custom_call_target="tpu_custom_call" | custom-call | flops 6442450944 | bytes 16777216 | tf_op jit(solution)/shard_map/pallas_call | solution.py:1084
  1015.3 33.5 %collective-permute-start = (f32[2,7,2048]{2,1,0:T(8,128)S(1)}, f32[2,7,2048]{2,1,0:T(8,128)S(1)}, u32[]{:S(2)}, u32[]{:S(2)}) collective-permute-start(f32[2,7,2048]{2,1,0:T(8,128)S(1)} %pad_maximum_fusion), channel_id=1, source_target_pairs={{0,4},{4,0},{8,12},{12,8},{16,20},{20,16},{24,28},{28,24},{1,5},{5... | collective-permute-start | bytes 344072 | tf_op jit(solution)/shard_map/ppermute | solution.py:1390
  1048.9 1.3 convert_element_type.75
  1050.1 2.7 slice.120
  1052.8 4.3 convert_element_type.74
  1057.2 1.3 slice_bitcast_fusion
  1059.2 6.2 maximum_convert_fusion
  1065.4 1.8 maximum_convert_fusion.2
  1068.8 4.2 collective-permute-done.1
  1073.8 1.2 slice.122
  1075.0 1.2 copy.32
  1076.1 1.6 maximum_convert_fusion.1
  1079.3 1.7 collective-permute-start.3
  1083.0 1.3 collective-permute-done.3
  1084.3 2.5 collective-permute-start.4
  1086.8 3.4 copy.37
  1090.1 2.4 copy.34
  1092.5 2.7 copy.36
  1096.5 2.3 copy.46
  1098.8 1.3 copy.47
  (107 shorter events, 14.1 us)
Async XLA Ops:
  7.2 149.1 %all-gather.21.cloned.1.call-start = ((), (), s32[]{:S(2)}) async-start(), calls=%async_computation.14 | async-start | bytes 2359296 | tf_op jit(solution)/shard_map/all_gather | solution.py:1420
  9.1 147.2 %all-gather.9.cloned.1.call-start = ((), (), s32[]{:S(2)}) async-start(), calls=%async_computation.4 | async-start | bytes 12976128 | tf_op jit(solution)/shard_map/all_gather | solution.py:1420
  14.2 229.3 %all-gather.11.cloned.1.call-start = ((), (), s32[]{:S(2)}) async-start(), calls=%async_computation.5 | async-start | bytes 6488064 | tf_op jit(solution)/shard_map/all_gather | solution.py:1420
  14.2 5.3 copy-start.17
  14.2 5.3 copy-start.6
  17.0 6.5 copy-start.7
  17.0 6.5 copy-start.8
  134.1 109.3 %all-gather.13.cloned.1.call-start = ((), (), s32[]{:S(2)}) async-start(), calls=%async_computation.6 | async-start | bytes 7077888 | tf_op jit(solution)/shard_map/all_gather | solution.py:1420
  137.7 14.8 %copy-start.3 = (bf16[1,256,3,512]{1,3,2,0:T(8,128)(2,1)S(1)}, bf16[1,256,3,512]{1,3,2,0:T(8,128)(2,1)}, u32[]{:S(2)}) copy-start(bf16[1,256,3,512]{1,3,2,0:T(8,128)(2,1)} %copy.39) | copy-start | bytes 2359300
  153.7 191.6 %all-gather.15.cloned.1.call-start = ((), (), s32[]{:S(2)}) async-start(), calls=%async_computation.7 | async-start | bytes 2359296 | tf_op jit(solution)/shard_map/all_gather | solution.py:1420
  154.3 191.0 %all-gather.17.cloned.1.call-start = ((), (), s32[]{:S(2)}) async-start(), calls=%async_computation.8 | async-start | bytes 12976128 | tf_op jit(solution)/shard_map/all_gather | solution.py:1420
  154.9 282.9 %all-gather.19.cloned.1.call-start = ((), (), s32[]{:S(2)}) async-start(), calls=%async_computation.9 | async-start | bytes 6488064 | tf_op jit(solution)/shard_map/all_gather | solution.py:1420
  155.6 669.3 %reduce-scatter.5.cloned.1.call-start = ((), (), s32[]{:S(2)}) async-start(), calls=%async_computation.10 | async-start | bytes 19464192 | tf_op jit(solution)/shard_map/reduce_scatter | solution.py:1400
  558.6 366.6 %reduce-scatter.7.cloned.1.call-start = ((), (), s32[]{:S(2)}) async-start(), calls=%async_computation.11 | async-start | bytes 9437184 | tf_op jit(solution)/shard_map/reduce_scatter | solution.py:1400
  695.8 354.4 %reduce-scatter.9.cloned.1.call-start = ((), (), s32[]{:S(2)}) async-start(), calls=%async_computation.12 | async-start | bytes 19464192 | tf_op jit(solution)/shard_map/reduce_scatter | solution.py:1400
  824.9 248.9 %reduce-scatter.11.cloned.1.call-start = ((), (), s32[]{:S(2)}) async-start(), calls=%async_computation.13 | async-start | bytes 9437184 | tf_op jit(solution)/shard_map/reduce_scatter | solution.py:1400
  964.3 0.7 copy-start.15
  964.3 0.7 copy-start.9
  964.3 0.7 copy-start.10
  964.3 0.7 copy-start.11
  964.4 0.7 copy-start.12
  964.4 0.8 copy-start.16
  965.2 49.2 %copy-start.13 = (f32[1,2048]{1,0:T(1,128)S(1)}, f32[1,2048]{1,0:T(1,128)}, u32[]{:S(2)}) copy-start(f32[1,2048]{1,0:T(1,128)} %get-tuple-element.132) | copy-start | bytes 24580
  965.2 49.2 %copy-start.14 = (f32[1,2048]{1,0:T(1,128)S(1)}, f32[1,2048]{1,0:T(1,128)}, u32[]{:S(2)}) copy-start(f32[1,2048]{1,0:T(1,128)} %get-tuple-element.134) | copy-start | bytes 24580
  1014.4 34.5 %slice-start = ((bf16[256,4224]{1,0:T(8,128)(2,1)}), bf16[256,2816]{1,0:T(8,128)(2,1)S(1)}, s32[]{:S(2)}) async-start(bf16[256,4224]{1,0:T(8,128)(2,1)} %reduce-scatter.5.cloned.1.call-done), calls=%async_computation.15 | async-start | bytes 2883584 | tf_op jit(solution)/shard_map/slice | solution.py:1532
  1015.3 51.8 %collective-permute-start = (f32[2,7,2048]{2,1,0:T(8,128)S(1)}, f32[2,7,2048]{2,1,0:T(8,128)S(1)}, u32[]{:S(2)}, u32[]{:S(2)}) collective-permute-start(f32[2,7,2048]{2,1,0:T(8,128)S(1)} %pad_maximum_fusion), channel_id=1, source_target_pairs={{0,4},{4,0},{8,12},{12,8},{16,20},{20,16},{24,28},{28,24},{1,5},{5... | collective-permute-start | bytes 344072 | tf_op jit(solution)/shard_map/ppermute | solution.py:1390
  1050.1 7.0 copy-start
  1057.1 1.6 copy-start.1
  1057.1 2.0 copy-start.2
  1065.4 1.9 copy-start.4
  1065.4 2.3 slice-start.1
  1067.2 5.9 collective-permute-start.1
  1073.1 5.2 collective-permute-start.2
  1079.3 5.0 collective-permute-start.3
  1084.3 10.9 collective-permute-start.4
  1092.5 6.3 copy-start.5
Sparse Core Ops, SparseCore 0:
  9.9 36.2 all-gather.20
  48.6 80.3 all-gather.8
  134.3 42.4 all-gather.10
  179.1 45.5 all-gather.12
  226.4 28.3 all-gather.14
  257.1 67.7 all-gather.16
  327.3 44.3 all-gather.18
  558.7 157.8 reduce-scatter.4
  720.4 84.9 reduce-scatter.6
  825.0 152.7 reduce-scatter.8
  981.7 86.2 reduce-scatter.10
